TPU v7x, 32 devices: a whole 2x2x4 slice. The times are simulated.
32 devices in a mesh: slab: 8 (over z, y), row: 2 (over core), col: 2 (over x).
Axes of the slice: x: 2, y: 2, z: 4, core: 2. Of those that a mesh axis runs over, the one named last changes fastest.
Arguments:
- pressure: float32 [32, 256, 256], P('slab', 'row', 'col'), may hold values from -6 to 6
- velocity: float32 [3, 32, 256, 256], P(None, 'slab', 'row', 'col'), may hold values from -6 to 6
- kappa: float32 [32, 256, 256], P('slab', 'row', 'col'), may hold values from 0.5 to 2
- drive: float32 [32, 256, 256], P('slab', 'row', 'col'), may hold values from -6 to 6
- adj_pressure_in: float32 [32, 256, 256], P('slab', 'row', 'col'), may hold values from -6 to 6
- adj_velocity_in: float32 [3, 32, 256, 256], P(None, 'slab', 'row', 'col'), may hold values from -6 to 6
- wall_mask: int32 [32, 256, 256], P('slab', 'row', 'col'), may hold values 0 or 1
- wall_cells: int32 [8, 2, 2, 512], P('slab', 'row', 'col'), may hold values from 0 to 65535
- wall_rows: int32 [8, 2, 2, 512], P('slab', 'row', 'col'), may hold values from 0 to 2047
- slot_angle: float32 [8, 2, 2, 512], P('slab', 'row', 'col'), may hold values from 0 to 64
- wall_count: int32 [8, 2, 2], P('slab', 'row', 'col'), may hold values from 1 to 512, as said below
- step: int32 [1], replicated, may hold values from 0 to 4095
Outputs:
- adj_pressure: float32 [32, 256, 256], P('slab', 'row', 'col')
- adj_velocity: float32 [3, 32, 256, 256], P(None, 'slab', 'row', 'col')
- shape_grad: float32 [2048, 64], P(('slab', 'row', 'col'))
Inputs may be any that keep to these rules, and one draw needn't show every extreme that they name: `wall_count`: some device has all 512 slots live in every draw.
All inputs are finite; a program needn't handle non-finite values. No bound on the sum of `wall_mask` on one device may be relied on, other than what follows from the above.
Results may differ from a plain program's by a relative error of at most 0.00002.
Values sent between devices are 32-bit elements; how exact they have to be, the bound alone decides.
No kernel may reach another device: no remote copies, remote signals or barrier semaphores. Data moves between devices by JAX's collectives and lax.ppermute only.
A program may use at most 64 MiB of HBM per device.

v0:
```python
import jax
import jax.numpy as jnp
from jax import lax
from jax.sharding import PartitionSpec as P

NROWS = 2048
ANG = 64


def padded_2(cells, sides, width):
    for axis, dim in sides:
        count = lax.axis_size(axis)
        ends = count - 1
        head = lax.slice_in_dim(cells, 0, width, axis=dim)
        tail = lax.slice_in_dim(cells, cells.shape[dim] - width, cells.shape[dim], axis=dim)
        cells = jnp.concatenate(
            [
                lax.ppermute(tail, axis, [(i, (i + 1) % count) for i in range(ends)]),
                cells,
                lax.ppermute(head, axis, [((i + 1) % count, i) for i in range(ends)]),
            ],
            axis=dim,
        )
    return cells


def crop_sides(field, axis, other, along):
    for dim in range(3):
        cut = along if dim == axis else other
        field = lax.slice_in_dim(field, cut, field.shape[dim] - cut, axis=dim)
    return field


def centered(padded, axis, width, extra):
    size = padded.shape[axis]
    upper = lax.slice_in_dim(padded, 2, size, axis=axis)
    lower = lax.slice_in_dim(padded, 0, size - 2, axis=axis)
    return crop_sides((upper - lower) * 0.5, axis, width, width - 1 - extra)


def spline_weights(angle):
    knots = jnp.arange(ANG, dtype=jnp.float32)
    dist = jnp.abs(angle[..., None] - knots)
    dist = jnp.minimum(dist, ANG - dist)
    outer = jnp.maximum(2.0 - dist, 0.0)
    inner = jnp.maximum(1.0 - dist, 0.0)
    return (outer * outer * outer - 4.0 * inner * inner * inner) / 6.0


def local(
    pressure,
    velocity,
    kappa,
    drive,
    adj_pressure_in,
    adj_velocity_in,
    wall_mask,
    wall_cells,
    wall_rows,
    slot_angle,
    wall_count,
    step,
):
    open_cells = 1.0 - wall_mask.astype(jnp.float32)
    phase = jnp.cos(0.5 * (step[0] % 97).astype(jnp.float32))
    scaled = kappa * adj_pressure_in
    padded = padded_2(jnp.stack([pressure, scaled]), (("slab", 1), ("row", 2), ("col", 3)), 1)
    slopes = [centered(padded[0], comp, 1, 0) for comp in range(3)]
    total = [adj_velocity_in[comp] + centered(padded[1], comp, 1, 0) for comp in range(3)]
    lam_u = [open_cells * total[comp] for comp in range(3)]
    padded_u = padded_2(jnp.stack(lam_u), (("slab", 1), ("row", 2), ("col", 3)), 1)
    divergence = (
        centered(padded_u[0], 0, 1, 0)
        + centered(padded_u[1], 1, 1, 0)
        + centered(padded_u[2], 2, 1, 0)
    )
    adj_pressure = adj_pressure_in + 0.3 * divergence
    moved = [velocity[comp] - 0.3 * slopes[comp] for comp in range(3)]
    moved[0] = moved[0] + drive * phase
    sens = -(total[0] * moved[0] + total[1] * moved[1] + total[2] * moved[2])
    cells = wall_cells.reshape(-1)
    values = sens.reshape(-1)[cells]
    live = jnp.arange(cells.shape[0], dtype=jnp.int32) < wall_count.reshape(-1)[0]
    values = jnp.where(live, values, 0.0)
    contrib = values[:, None] * spline_weights(slot_angle.reshape(-1))
    rows = wall_rows.reshape(-1)
    dense = jnp.zeros((NROWS, ANG), jnp.float32).at[rows].add(contrib)
    partial_rows = lax.psum_scatter(dense, "slab", scatter_dimension=0, tiled=True)
    shape_grad = lax.psum_scatter(partial_rows, ("row", "col"), scatter_dimension=0, tiled=True)
    return (adj_pressure, jnp.stack(lam_u), shape_grad)


def solution(mesh):
    in_specs = (
        P("slab", "row", "col"),
        P(None, "slab", "row", "col"),
        P("slab", "row", "col"),
        P("slab", "row", "col"),
        P("slab", "row", "col"),
        P(None, "slab", "row", "col"),
        P("slab", "row", "col"),
        P("slab", "row", "col", None),
        P("slab", "row", "col", None),
        P("slab", "row", "col", None),
        P("slab", "row", "col"),
        P(),
    )
    out_specs = (
        P("slab", "row", "col"),
        P(None, "slab", "row", "col"),
        P(("slab", "row", "col"), None),
    )
    return jax.shard_map(local, mesh=mesh, in_specs=in_specs, out_specs=out_specs, check_vma=False)
```

profile of v0, /device:TPU:16, one launch (start us, length us, event | category | flops | bytes accessed | tf_op | source)
XLA Modules:
  0.0 159.0 jit_solution(9374990045942425411)
XLA Ops:
  7.2 1.1 multiply_bitcast_fusion.3
  8.3 0.9 pad_maximum_fusion.6
  9.2 3.4 %collective-permute-start = (f32[2,1,128,128]{3,2,1,0:T(8,128)S(1)}, f32[2,1,128,128]{3,2,1,0:T(8,128)S(1)}, u32[]{:S(2)}, u32[]{:S(2)}) collective-permute-start(f32[2,1,128,128]{3,2,1,0:T(8,128)S(1)} %get-tuple-element.37), channel_id=1, source_target_pairs={{0,4},{4,8},{8,12},{12,16},{16,20},{20,24},{24,28},{1,5},{5,9},{9,... | collective-permute-start | bytes 393224 | tf_op jit(solution)/shard_map/ppermute | solution.py:18
  12.7 3.3 %collective-permute-start.1 = (f32[2,1,128,128]{3,2,1,0:T(8,128)S(1)}, f32[2,1,128,128]{3,2,1,0:T(8,128)S(1)}, u32[]{:S(2)}, u32[]{:S(2)}) collective-permute-start(f32[2,1,128,128]{3,2,1,0:T(8,128)S(1)} %get-tuple-element.38), channel_id=1, source_target_pairs={{4,0},{8,4},{12,8},{16,12},{20,16},{24,20},{28,24},{5,1},{9,5},{13... | collective-permute-start | bytes 393224 | tf_op jit(solution)/shard_map/ppermute | solution.py:20
  16.0 0.7 compare_select_fusion
  16.7 0.6 collective-permute-done
  17.3 2.8 %collective-permute-done.1 = f32[2,1,128,128]{3,2,1,0:T(8,128)S(1)} collective-permute-done((f32[2,1,128,128]{3,2,1,0:T(8,128)S(1)}, f32[2,1,128,128]{3,2,1,0:T(8,128)S(1)}, u32[]{:S(2)}, u32[]{:S(2)}) %collective-permute-start.1) | collective-permute-done | bytes 131104 | tf_op jit(solution)/shard_map/ppermute | solution.py:20
  20.1 1.3 collective-permute-start.2
  21.4 1.3 collective-permute-start.3
  22.7 1.7 %collective-permute-done.3 = f32[2,6,1,128]{3,2,1,0:T(1,128)S(1)} collective-permute-done((f32[2,6,1,128]{3,2,1,0:T(1,128)S(1)}, f32[2,6,1,128]{3,2,1,0:T(1,128)S(1)}, u32[]{:S(2)}, u32[]{:S(2)}) %collective-permute-start.3) | collective-permute-done | bytes 6176 | tf_op jit(solution)/shard_map/ppermute | solution.py:20
  24.5 0.3 fusion.41
  24.8 0.5 copy.46
  25.3 0.5 copy.47
  25.7 1.3 collective-permute-start.5
  27.0 4.5 %collective-permute-start.4 = (f32[2,6,130,1]{2,0,3,1:T(2,128)S(1)}, f32[2,6,130,1]{2,0,3,1:T(2,128)S(1)}, u32[]{:S(2)}, u32[]{:S(2)}) collective-permute-start(f32[2,6,130,1]{2,0,3,1:T(2,128)S(1)} %copy.46), channel_id=1, source_target_pairs={{0,1},{2,3},{4,5},{6,7},{8,9},{10,11},{12,13},{14,15},{16,17},{18,... | collective-permute-start | bytes 18728 | tf_op jit(solution)/shard_map/ppermute | solution.py:18
  33.0 0.3 copy.48
  33.4 0.3 copy.49
  33.7 0.8 pad_maximum_fusion.1
  34.6 0.1 slice_bitcast_fusion
  34.7 0.3 fusion.36
  35.1 0.3 fusion.35
  35.4 0.8 copy-done.1
  36.2 0.3 multiply_bitcast_fusion.2
  36.6 3.9 %collective-permute-start.6 = (f32[3,1,128,128]{3,2,1,0:T(8,128)S(1)}, f32[3,1,128,128]{3,2,1,0:T(8,128)S(1)}, u32[]{:S(2)}, u32[]{:S(2)}) collective-permute-start(f32[3,1,128,128]{3,2,1,0:T(8,128)S(1)} %get-tuple-element.33), channel_id=1, source_target_pairs={{0,4},{4,8},{8,12},{12,16},{16,20},{20,24},{24,28},{1,5},{5,9},{9,... | collective-permute-start | bytes 589832 | tf_op jit(solution)/shard_map/ppermute | solution.py:18
  40.6 3.0 %collective-permute-start.7 = (f32[3,1,128,128]{3,2,1,0:T(8,128)S(1)}, f32[3,1,128,128]{3,2,1,0:T(8,128)S(1)}, u32[]{:S(2)}, u32[]{:S(2)}) collective-permute-start(f32[3,1,128,128]{3,2,1,0:T(8,128)S(1)} %get-tuple-element.34), channel_id=1, source_target_pairs={{4,0},{8,4},{12,8},{16,12},{20,16},{24,20},{28,24},{5,1},{9,5},{13... | collective-permute-start | bytes 589832 | tf_op jit(solution)/shard_map/ppermute | solution.py:20
  43.6 0.5 fusion.13
  44.1 3.1 %gather_fusion = f32[512]{0:T(512)S(1)} fusion(f32[65536]{0:T(1024)S(1)} %bitcast.58, s32[1024]{0:T(1024)S(1)} %pad_clamp_fusion), kind=kCustom, calls=%fused_computation | custom fusion | bytes 6144 | tf_op jit(solution)/shard_map/gather | solution.py:82
  47.2 1.5 collective-permute-done.6
  48.7 1.5 collective-permute-done.7
  50.2 1.9 %collective-permute-start.8 = (f32[3,6,1,128]{3,2,1,0:T(1,128)S(1)}, f32[3,6,1,128]{3,2,1,0:T(1,128)S(1)}, u32[]{:S(2)}, u32[]{:S(2)}) collective-permute-start(f32[3,6,1,128]{3,2,1,0:T(1,128)S(1)} %get-tuple-element.14), channel_id=1, source_target_pairs={{0,2},{1,3},{4,6},{5,7},{8,10},{9,11},{12,14},{13,15},{16,18},{17,... | collective-permute-start | bytes 27656 | tf_op jit(solution)/shard_map/ppermute | solution.py:18
  52.1 1.3 collective-permute-start.9
  53.5 1.7 %collective-permute-done.9 = f32[3,6,1,128]{3,2,1,0:T(1,128)S(1)} collective-permute-done((f32[3,6,1,128]{3,2,1,0:T(1,128)S(1)}, f32[3,6,1,128]{3,2,1,0:T(1,128)S(1)}, u32[]{:S(2)}, u32[]{:S(2)}) %collective-permute-start.9) | collective-permute-done | bytes 9248 | tf_op jit(solution)/shard_map/ppermute | solution.py:20
  55.3 0.4 fusion.34
  55.7 0.9 copy.50
  56.6 0.9 copy.51
  57.6 1.3 collective-permute-start.11
  58.9 4.5 %collective-permute-start.10 = (f32[3,6,130,1]{2,1,3,0:T(8,128)S(1)}, f32[3,6,130,1]{2,1,3,0:T(8,128)S(1)}, u32[]{:S(2)}, u32[]{:S(2)}) collective-permute-start(f32[3,6,130,1]{2,1,3,0:T(8,128)S(1)} %copy.50), channel_id=1, source_target_pairs={{0,1},{2,3},{4,5},{6,7},{8,9},{10,11},{12,13},{14,15},{16,17},{18,... | collective-permute-start | bytes 28088 | tf_op jit(solution)/shard_map/ppermute | solution.py:18
  63.5 0.1 copy.54
  63.6 3.2 %scatter_custom_fusion = f32[2048,64]{1,0:T(8,128)} fusion(s32[512]{0:T(512)S(1)} %bitcast.65, f32[512,64]{1,0:T(8,128)S(1)} %copy.54, f32[]{:T(128)} %constant.16.clone.1), kind=kCustom, calls=%fused_computation.20 | custom fusion | flops 32768 | bytes 524292 | tf_op jit(solution)/shard_map/scatter-add | solution.py:87
  67.0 0.5 copy.52
  67.5 0.5 copy.53
  67.9 2.0 %pad_maximum_fusion = f32[3,6,130,130]{3,2,1,0:T(8,128)S(1)} fusion(f32[3,6,130,1]{3,2,1,0:T(8,128)S(1)} %copy.53, f32[3,6,1,128]{3,2,1,0:T(1,128)S(1)} %collective-permute-done.9, f32[3,1,128,128]{3,2,1,0:T(8,128)} %copy-done.4, f32[1,4,128,128]{3,2,1,0:T(8,128)S(1)} %get-tuple-element.18, f32[1,4,128,128]{3,2,1,0:T(8,128)S(1)} %get-tuple-element.17, ...), kind=kLoop, calls=%fused_computation.2 | loop fusion | flops 2433600 | bytes 2433600 | tf_op jit(solution)/shard_map/concatenate | solution.py:16
  70.1 0.1 slice_bitcast_fusion.2
  70.2 0.2 fusion.38
  70.4 0.1 fusion.37
  70.5 58.9 %reduce-scatter.3.cloned.1.call-done = f32[256,64]{1,0:T(8,128)} async-done(((f32[2048,64]{1,0:T(8,128)}), f32[256,64]{1,0:T(8,128)}) %reduce-scatter.3.cloned.1.call-update) | async-done | bytes 65552 | tf_op jit(solution)/shard_map/reduce_scatter | solution.py:88
  129.5 1.0 fusion.25
  130.4 21.7 %reduce-scatter.5.cloned.1.call-done = f32[64,64]{1,0:T(8,128)} async-done(((f32[256,64]{1,0:T(8,128)}), f32[64,64]{1,0:T(8,128)}) %reduce-scatter.5.cloned.1.call-update) | async-done | bytes 16400 | tf_op jit(solution)/shard_map/reduce_scatter | solution.py:89
  (45 shorter events, 0.8 us)
Async XLA Ops:
  7.2 12.9 %copy-start = (f32[4,128,128]{2,1,0:T(8,128)S(1)}, f32[4,128,128]{2,1,0:T(8,128)}, u32[]{:S(2)}) copy-start(f32[4,128,128]{2,1,0:T(8,128)} %param.12) | copy-start | bytes 786436
  7.2 15.5 %copy-start.11 = (s32[1,1,1,512]{3,2,1,0:T(1,128)S(1)}, s32[1,1,1,512]{3,2,1,0:T(1,128)}, u32[]{:S(2)}) copy-start(s32[1,1,1,512]{3,2,1,0:T(1,128)} %param.20) | copy-start | bytes 6148
  7.2 122.2 %reduce-scatter.3.cloned.1.call-start = ((), (), s32[]{:S(2)}) async-start(), calls=%async_computation.2 | async-start | bytes 1179648 | tf_op jit(solution)/shard_map/reduce_scatter | solution.py:88
  9.2 8.1 %collective-permute-start = (f32[2,1,128,128]{3,2,1,0:T(8,128)S(1)}, f32[2,1,128,128]{3,2,1,0:T(8,128)S(1)}, u32[]{:S(2)}, u32[]{:S(2)}) collective-permute-start(f32[2,1,128,128]{3,2,1,0:T(8,128)S(1)} %get-tuple-element.37), channel_id=1, source_target_pairs={{0,4},{4,8},{8,12},{12,16},{16,20},{20,24},{24,28},{1,5},{5,9},{9,... | collective-permute-start | bytes 393224 | tf_op jit(solution)/shard_map/ppermute | solution.py:18
  12.7 7.4 %collective-permute-start.1 = (f32[2,1,128,128]{3,2,1,0:T(8,128)S(1)}, f32[2,1,128,128]{3,2,1,0:T(8,128)S(1)}, u32[]{:S(2)}, u32[]{:S(2)}) collective-permute-start(f32[2,1,128,128]{3,2,1,0:T(8,128)S(1)} %get-tuple-element.38), channel_id=1, source_target_pairs={{4,0},{8,4},{12,8},{16,12},{20,16},{24,20},{28,24},{5,1},{9,5},{13... | collective-permute-start | bytes 393224 | tf_op jit(solution)/shard_map/ppermute | solution.py:20
  20.1 2.6 %collective-permute-start.2 = (f32[2,6,1,128]{3,2,1,0:T(1,128)S(1)}, f32[2,6,1,128]{3,2,1,0:T(1,128)S(1)}, u32[]{:S(2)}, u32[]{:S(2)}) collective-permute-start(f32[2,6,1,128]{3,2,1,0:T(1,128)S(1)} %get-tuple-element.35), channel_id=1, source_target_pairs={{0,2},{1,3},{4,6},{5,7},{8,10},{9,11},{12,14},{13,15},{16,18},{17,... | collective-permute-start | bytes 18440 | tf_op jit(solution)/shard_map/ppermute | solution.py:18
  21.4 3.1 %collective-permute-start.3 = (f32[2,6,1,128]{3,2,1,0:T(1,128)S(1)}, f32[2,6,1,128]{3,2,1,0:T(1,128)S(1)}, u32[]{:S(2)}, u32[]{:S(2)}) collective-permute-start(f32[2,6,1,128]{3,2,1,0:T(1,128)S(1)} %get-tuple-element.36), channel_id=1, source_target_pairs={{2,0},{3,1},{6,4},{7,5},{10,8},{11,9},{14,12},{15,13},{18,16},{19,... | collective-permute-start | bytes 18440 | tf_op jit(solution)/shard_map/ppermute | solution.py:20
  25.7 7.6 %collective-permute-start.5 = (f32[2,6,130,1]{2,0,3,1:T(2,128)S(1)}, f32[2,6,130,1]{2,0,3,1:T(2,128)S(1)}, u32[]{:S(2)}, u32[]{:S(2)}) collective-permute-start(f32[2,6,130,1]{2,0,3,1:T(2,128)S(1)} %copy.47), channel_id=1, source_target_pairs={{1,0},{3,2},{5,4},{7,6},{9,8},{11,10},{13,12},{15,14},{17,16},{19,... | collective-permute-start | bytes 18728 | tf_op jit(solution)/shard_map/ppermute | solution.py:20
  27.0 6.0 %collective-permute-start.4 = (f32[2,6,130,1]{2,0,3,1:T(2,128)S(1)}, f32[2,6,130,1]{2,0,3,1:T(2,128)S(1)}, u32[]{:S(2)}, u32[]{:S(2)}) collective-permute-start(f32[2,6,130,1]{2,0,3,1:T(2,128)S(1)} %copy.46), channel_id=1, source_target_pairs={{0,1},{2,3},{4,5},{6,7},{8,9},{10,11},{12,13},{14,15},{16,17},{18,... | collective-permute-start | bytes 18728 | tf_op jit(solution)/shard_map/ppermute | solution.py:18
  35.0 1.1 copy-start.1
  35.0 1.2 copy-start.8
  36.5 7.0 %copy-start.7 = (f32[3,4,128,128]{3,2,1,0:T(8,128)S(1)}, f32[3,4,128,128]{3,2,1,0:T(8,128)}, u32[]{:S(2)}) copy-start(f32[3,4,128,128]{3,2,1,0:T(8,128)} %param.13) | copy-start | bytes 2359300
  36.5 7.0 %copy-start.9 = (f32[4,128,128]{2,1,0:T(8,128)S(1)}, f32[4,128,128]{2,1,0:T(8,128)}, u32[]{:S(2)}) copy-start(f32[4,128,128]{2,1,0:T(8,128)} %param.15) | copy-start | bytes 786436
  36.6 6.9 %copy-start.5 = (f32[3,4,128,128]{3,2,1,0:T(8,128)}, f32[3,4,128,128]{3,2,1,0:T(8,128)S(1)}, u32[]{:S(2)}) copy-start(f32[3,4,128,128]{3,2,1,0:T(8,128)S(1)} %pad_maximum_fusion.4) | copy-start | bytes 2359300
  36.6 12.1 %collective-permute-start.6 = (f32[3,1,128,128]{3,2,1,0:T(8,128)S(1)}, f32[3,1,128,128]{3,2,1,0:T(8,128)S(1)}, u32[]{:S(2)}, u32[]{:S(2)}) collective-permute-start(f32[3,1,128,128]{3,2,1,0:T(8,128)S(1)} %get-tuple-element.33), channel_id=1, source_target_pairs={{0,4},{4,8},{8,12},{12,16},{16,20},{20,24},{24,28},{1,5},{5,9},{9,... | collective-permute-start | bytes 589832 | tf_op jit(solution)/shard_map/ppermute | solution.py:18
  40.6 9.6 %collective-permute-start.7 = (f32[3,1,128,128]{3,2,1,0:T(8,128)S(1)}, f32[3,1,128,128]{3,2,1,0:T(8,128)S(1)}, u32[]{:S(2)}, u32[]{:S(2)}) collective-permute-start(f32[3,1,128,128]{3,2,1,0:T(8,128)S(1)} %get-tuple-element.34), channel_id=1, source_target_pairs={{4,0},{8,4},{12,8},{16,12},{20,16},{24,20},{28,24},{5,1},{9,5},{13... | collective-permute-start | bytes 589832 | tf_op jit(solution)/shard_map/ppermute | solution.py:20
  48.7 6.5 %copy-start.2 = (f32[3,1,128,128]{3,2,1,0:T(8,128)}, f32[3,1,128,128]{3,2,1,0:T(8,128)S(1)}, u32[]{:S(2)}) copy-start(f32[3,1,128,128]{3,2,1,0:T(8,128)S(1)} %collective-permute-done.6) | copy-start | bytes 589828
  50.2 5.0 %copy-start.4 = (f32[3,1,128,128]{3,2,1,0:T(8,128)}, f32[3,1,128,128]{3,2,1,0:T(8,128)S(1)}, u32[]{:S(2)}) copy-start(f32[3,1,128,128]{3,2,1,0:T(8,128)S(1)} %collective-permute-done.7) | copy-start | bytes 589828
  50.2 3.2 %collective-permute-start.8 = (f32[3,6,1,128]{3,2,1,0:T(1,128)S(1)}, f32[3,6,1,128]{3,2,1,0:T(1,128)S(1)}, u32[]{:S(2)}, u32[]{:S(2)}) collective-permute-start(f32[3,6,1,128]{3,2,1,0:T(1,128)S(1)} %get-tuple-element.14), channel_id=1, source_target_pairs={{0,2},{1,3},{4,6},{5,7},{8,10},{9,11},{12,14},{13,15},{16,18},{17,... | collective-permute-start | bytes 27656 | tf_op jit(solution)/shard_map/ppermute | solution.py:18
  52.1 3.1 %collective-permute-start.9 = (f32[3,6,1,128]{3,2,1,0:T(1,128)S(1)}, f32[3,6,1,128]{3,2,1,0:T(1,128)S(1)}, u32[]{:S(2)}, u32[]{:S(2)}) collective-permute-start(f32[3,6,1,128]{3,2,1,0:T(1,128)S(1)} %get-tuple-element.15), channel_id=1, source_target_pairs={{2,0},{3,1},{6,4},{7,5},{10,8},{11,9},{14,12},{15,13},{18,16},{19,... | collective-permute-start | bytes 27656 | tf_op jit(solution)/shard_map/ppermute | solution.py:20
  55.7 7.7 %copy-start.10 = (f32[1,1,1,512]{3,2,1,0:T(1,128)S(1)}, f32[1,1,1,512]{3,2,1,0:T(1,128)}, u32[]{:S(2)}) copy-start(f32[1,1,1,512]{3,2,1,0:T(1,128)} %param.21) | copy-start | bytes 6148
  57.6 9.9 %collective-permute-start.11 = (f32[3,6,130,1]{2,1,3,0:T(8,128)S(1)}, f32[3,6,130,1]{2,1,3,0:T(8,128)S(1)}, u32[]{:S(2)}, u32[]{:S(2)}) collective-permute-start(f32[3,6,130,1]{2,1,3,0:T(8,128)S(1)} %copy.51), channel_id=1, source_target_pairs={{1,0},{3,2},{5,4},{7,6},{9,8},{11,10},{13,12},{15,14},{17,16},{19,... | collective-permute-start | bytes 28088 | tf_op jit(solution)/shard_map/ppermute | solution.py:20
  58.9 8.1 %collective-permute-start.10 = (f32[3,6,130,1]{2,1,3,0:T(8,128)S(1)}, f32[3,6,130,1]{2,1,3,0:T(8,128)S(1)}, u32[]{:S(2)}, u32[]{:S(2)}) collective-permute-start(f32[3,6,130,1]{2,1,3,0:T(8,128)S(1)} %copy.50), channel_id=1, source_target_pairs={{0,1},{2,3},{4,5},{6,7},{8,9},{10,11},{12,13},{14,15},{16,17},{18,... | collective-permute-start | bytes 28088 | tf_op jit(solution)/shard_map/ppermute | solution.py:18
  66.9 1.0 copy-start.3
  66.9 85.2 %reduce-scatter.5.cloned.1.call-start = ((), (), s32[]{:S(2)}) async-start(), calls=%async_computation.3 | async-start | bytes 163840 | tf_op jit(solution)/shard_map/reduce_scatter | solution.py:89
  70.4 59.1 %copy-start.6 = (f32[4,128,128]{2,1,0:T(8,128)S(1)}, f32[4,128,128]{2,1,0:T(8,128)}, u32[]{:S(2)}) copy-start(f32[4,128,128]{2,1,0:T(8,128)} %param.16) | copy-start | bytes 786436
Sparse Core Ops, SparseCore 0:
  67.0 62.3 reduce-scatter.2
  132.4 19.6 reduce-scatter.4
where the time goes:
time: 161 us; the launch traced here: 159 us
  waiting for transfers between devices  90.5 us (56%)
  starting transfers between devices  31.2 us (19%)
  between operations  15.9 us (10%)
  other arithmetic  11 us (7%)
  local copies, waits for them, and re-layouts  10.4 us (6%)
    reduce_scatter x1, waiting for transfers between devices, local(): lax.psum_scatter(dense, 'slab', scatter_dimension=0, tiled=True)  58.9 us
    reduce_scatter x1, waiting for transfers between devices, local(): lax.psum_scatter(partial_rows, ('row', 'col'), scatter_dimension=0, tiled...  21.7 us
    ppermute x6, starting transfers between devices, padded_2(): lax.ppermute(tail, axis, [(i, (i + 1) % count) for i in range(ends)])  19.6 us
    ppermute x6, starting transfers between devices, padded_2(): lax.ppermute(head, axis, [((i + 1) % count, i) for i in range(ends)])  11.4 us
    ppermute x6, waiting for transfers between devices, padded_2(): lax.ppermute(head, axis, [((i + 1) % count, i) for i in range(ends)])  7.7 us
    scatter-add x1, other arithmetic, local(): dense = jnp.zeros((NROWS, ANG), jnp.float32).at[rows].add(contrib)  3.25 us
  transfers between devices with their start and end apart: 14, of which 8 were waited for; matrix products, arithmetic and copies ran while one was open for 8% of the time, Pallas kernels for 0%

commit v1 on v0

v1 whole, which is shorter than its diff:
```python
import jax
import jax.numpy as jnp
from jax import lax
from jax.experimental import pallas as pl
from jax.experimental.pallas import tpu as pltpu
from jax.sharding import PartitionSpec as P

NROWS = 2048
ANG = 64
F32 = jnp.float32
BF16 = jnp.bfloat16
VM = pl.BlockSpec(memory_space=pltpu.VMEM)
SM = pl.BlockSpec(memory_space=pltpu.SMEM)
LIMIT = pltpu.CompilerParams(vmem_limit_bytes=24 << 20)


def call(body, outs, args, specs, scratch=(), flops=1_000_000, moved=1_000_000):
    return pl.pallas_call(
        body,
        out_shape=outs,
        in_specs=specs,
        out_specs=jax.tree.map(lambda _: VM, outs),
        scratch_shapes=list(scratch),
        compiler_params=LIMIT,
        cost_estimate=pl.CostEstimate(flops=flops, bytes_accessed=moved, transcendentals=0),
    )(*args)


def shape(dims, dtype=F32):
    return jax.ShapeDtypeStruct(tuple(dims), dtype)


def is_odd(axis):
    return lax.rem(lax.axis_index(axis), 2) == 1


def swap_pairs(count, first):
    pairs = []
    for low in range(first, count - 1, 2):
        pairs += [(low, low + 1), (low + 1, low)]
    return pairs


def swap(axis, first, message):
    return lax.ppermute(message, axis, swap_pairs(lax.axis_size(axis), first))


def slab_faces(p_ref, k_ref, a_ref, *out_refs):
    last = p_ref.shape[0] - 1
    odd = is_odd("slab")
    for first, out_ref in enumerate(out_refs):
        at = jnp.where(odd != (first == 1), 0, last)
        out_ref[0] = p_ref[at]
        out_ref[1] = k_ref[at] * a_ref[at]


def side_faces(rounds, p_ref, k_ref, a_ref, t_ref, m_ref, *out_refs):
    depth, height, width = p_ref.shape
    lanes = lax.broadcasted_iota(jnp.int32, (height, width), 1)
    for (axis, first), out_ref in zip(rounds, out_refs):
        high = is_odd(axis) == (first == 1)
        sign = jnp.where(high, -0.5, 0.5)
        if axis == "row":
            at = jnp.where(high, height - 1, 0)
            inner = jnp.where(high, height - 2, 1)
            for x in range(depth):
                face, second = pl.ds(at, 1), pl.ds(inner, 1)
                free = 1.0 - m_ref[x, face, :].astype(F32)
                out_ref[0, pl.ds(x, 1), :] = p_ref[x, face, :]
                out_ref[1, pl.ds(x, 1), :] = k_ref[x, face, :] * a_ref[x, face, :]
                behind = k_ref[x, second, :] * a_ref[x, second, :]
                out_ref[2, pl.ds(x, 1), :] = free * (t_ref[1, x, face, :] + sign * behind)
                out_ref[3, pl.ds(x, 1), :] = free
        else:
            at = jnp.where(high, width - 1, 0)
            turn = jnp.where(high, 1, width - 1)
            table = jnp.zeros((height, width), F32)
            for x in range(depth):
                free = 1.0 - m_ref[x].astype(F32)
                scaled = k_ref[x] * a_ref[x]
                behind = pltpu.roll(scaled, turn, 1)
                fields = (p_ref[x], scaled, free * (t_ref[2, x] + sign * behind), free)
                for f, field in enumerate(fields):
                    lane = f * depth + x
                    moved = pltpu.roll(field, lax.rem(lane - at + width, width), 1)
                    table = jnp.where(lanes == lane, moved, table)
            flipped = table.T
            for f in range(4):
                out_ref[f] = flipped[f * depth : (f + 1) * depth]


def low_high(axis, first, second):
    odd = is_odd(axis)
    zero = jnp.zeros_like(first)
    second = zero if second is None else second
    return jnp.where(odd, first, second), jnp.where(odd, second, first)


def side(field, axis, low, high):
    size = field.shape[axis]
    at = lax.broadcasted_iota(jnp.int32, field.shape, axis)
    upper = jnp.where(at == size - 1, high, pltpu.roll(field, size - 1, axis))
    lower = jnp.where(at == 0, low, pltpu.roll(field, 1, axis))
    return (upper - lower) * 0.5


def halves(value):
    top = value.astype(BF16)
    rest = value - top.astype(F32)
    mid = rest.astype(BF16)
    return top, mid, (rest - mid.astype(F32)).astype(BF16)


def take_halo(axis, refs):
    first = refs[0][...]
    second = refs[1][...] if len(refs) > 1 else None
    return low_high(axis, first, second)


def columns(halo, height, width):
    depth = halo.shape[1]
    table = jnp.concatenate([halo[f] for f in range(halo.shape[0])], axis=0)
    table = jnp.concatenate([table, jnp.zeros((width - table.shape[0], height), F32)], axis=0)
    return table.T


def main_body(n_slab, n_row, n_col, refs):
    p_ref, v_ref, k_ref, d_ref, a_ref, t_ref, m_ref, c_ref, r_ref, g_ref, n_ref, ph_ref = refs[:12]
    rest = refs[12:]
    slab_refs, rest = rest[:n_slab], rest[n_slab:]
    row_refs, rest = rest[:n_row], rest[n_row:]
    col_refs, rest = rest[:n_col], rest[n_col:]
    lam_ref, slot_ref = rest[:2]
    face_refs = rest[2 : 2 + n_slab]
    q_ref, sens_ref = rest[2 + n_slab :]
    depth, height, width = p_ref.shape
    phase = ph_ref[0]
    slab_low, slab_high = take_halo("slab", slab_refs)
    row_low, row_high = take_halo("row", row_refs)
    col_low, col_high = (columns(h, height, width) for h in take_halo("col", col_refs))
    for x in range(depth):
        q_ref[x] = k_ref[x] * a_ref[x]
    for x in range(depth):
        p, q = p_ref[x], q_ref[x]

        def along(field, ref, which):
            upper = ref[x + 1] if x + 1 < depth else slab_high[which]
            lower = ref[x - 1] if x > 0 else slab_low[which]
            lane = which * depth + x
            return (
                (upper - lower) * 0.5,
                side(field, 0, row_low[which, x : x + 1], row_high[which, x : x + 1]),
                side(field, 1, col_low[:, lane : lane + 1], col_high[:, lane : lane + 1]),
            )

        slopes = along(p, p_ref, 0)
        gains = along(q, q_ref, 1)
        free = 1.0 - m_ref[x].astype(F32)
        sens = jnp.zeros((height, width), F32)
        for comp in range(3):
            total = t_ref[comp, x] + gains[comp]
            lam_ref[comp, x] = free * total
            moved = v_ref[comp, x] - 0.3 * slopes[comp]
            if comp == 0:
                moved = moved + d_ref[x] * phase
            sens = sens + total * moved
        sens_ref[pl.ds(x * height, height), :] = -sens
    odd = is_odd("slab")
    for first, face_ref in enumerate(face_refs):
        face_ref[...] = lam_ref[0, jnp.where(odd != (first == 1), 0, depth - 1)]
    cells = c_ref[...]
    slots = cells.shape[1]
    lines = depth * height
    line = lax.div(cells, width)
    picks = lax.broadcasted_iota(jnp.int32, (lines, slots), 0) == line
    picks = jnp.where(picks, 1.0, 0.0).astype(BF16)
    found = jnp.zeros((width, slots), F32)
    for piece in halves(sens_ref[...]):
        found = found + lax.dot_general(
            piece, picks, (((0,), (0,)), ((), ())), preferred_element_type=F32
        )
    lane = lax.broadcasted_iota(jnp.int32, (width, slots), 0)
    values = jnp.sum(jnp.where(lane == cells - line * width, found, 0.0), axis=0, keepdims=True)
    live = lax.broadcasted_iota(jnp.int32, (1, slots), 1) < n_ref[0]
    values = jnp.where(live, values, 0.0)
    rows = r_ref[...].astype(F32)
    angles = g_ref[...]
    for j in range(slots // 128):
        part = slice(128 * j, 128 * (j + 1))
        slot_ref[0, pl.ds(j, 1), :] = values[:, part]
        slot_ref[1, pl.ds(j, 1), :] = rows[:, part]
        slot_ref[2, pl.ds(j, 1), :] = angles[:, part]


def pressure_body(n_slab, n_row, n_col, refs):
    lam_ref, k_ref, a_ref = refs[:3]
    rest = refs[3:]
    face_refs, rest = rest[:n_slab], rest[n_slab:]
    row_refs, rest = rest[:n_row], rest[n_row:]
    col_refs, (out_ref,) = rest[:n_col], rest[n_col:]
    depth, height, width = a_ref.shape
    slab_low, slab_high = take_halo("slab", face_refs)
    row_low, row_high = take_halo("row", row_refs)
    col_low, col_high = (columns(h, height, width) for h in take_halo("col", col_refs))
    for x in range(depth):
        scaled = k_ref[x] * a_ref[x]
        half = 0.5 * scaled
        one = slice(x, x + 1)
        push, open_at = slice(2 * depth + x, 2 * depth + x + 1), slice(3 * depth + x, 3 * depth + x + 1)
        upper = lam_ref[0, x + 1] if x + 1 < depth else slab_high
        lower = lam_ref[0, x - 1] if x > 0 else slab_low
        row_above = row_high[2, one] - row_high[3, one] * half[height - 1 :]
        row_below = row_low[2, one] + row_low[3, one] * half[:1]
        col_above = col_high[:, push] - col_high[:, open_at] * half[:, width - 1 :]
        col_below = col_low[:, push] + col_low[:, open_at] * half[:, :1]
        spread = (
            (upper - lower) * 0.5
            + side(lam_ref[1, x], 0, row_below, row_above)
            + side(lam_ref[2, x], 1, col_below, col_above)
        )
        out_ref[x] = a_ref[x] + 0.3 * spread


def dense_body(block, n_slots, n_prior, refs):
    slot_refs = refs[:n_slots]
    prior = refs[n_slots : n_slots + n_prior]
    out_ref, pick_ref, *piece_refs = refs[n_slots + n_prior :]
    base = (lax.axis_index("slab") * block).astype(F32)
    here = lax.broadcasted_iota(jnp.int32, (block, 128), 0).astype(F32) + base
    knots = lax.broadcasted_iota(jnp.int32, (ANG, 128), 0).astype(F32)
    at = 0
    for slot_ref in slot_refs:
        for d in range(slot_ref.shape[0] // 3):
            for j in range(slot_ref.shape[1]):
                value = slot_ref[3 * d, pl.ds(j, 1), :]
                row = slot_ref[3 * d + 1, pl.ds(j, 1), :]
                angle = slot_ref[3 * d + 2, pl.ds(j, 1), :]
                lanes = pl.ds(at, 128)
                pick_ref[:, lanes] = jnp.where(here == row, 1.0, 0.0).astype(BF16)
                dist = jnp.abs(angle - knots)
                dist = jnp.minimum(dist, ANG - dist)
                outer = jnp.maximum(2.0 - dist, 0.0)
                inner = jnp.maximum(1.0 - dist, 0.0)
                weight = (outer * outer * outer - 4.0 * inner * inner * inner) * (1.0 / 6.0)
                for piece, piece_ref in zip(halves(value * weight), piece_refs):
                    piece_ref[:, lanes] = piece
                at += 128
    total = prior[0][...] if prior else jnp.zeros(out_ref.shape, F32)
    for piece_ref in piece_refs:
        total = total + lax.dot_general(
            pick_ref[...], piece_ref[...], (((1,), (1,)), ((), ())), preferred_element_type=F32
        )
    out_ref[...] = total


def dense(block, slots, prior=()):
    count = sum(s.shape[0] // 3 * s.shape[1] * 128 for s in slots)

    def body(*refs):
        dense_body(block, len(slots), len(prior), refs)

    return call(
        body,
        shape((block, ANG)),
        (*slots, *prior),
        [VM] * (len(slots) + len(prior)),
        [pltpu.VMEM((block, count), BF16)] + [pltpu.VMEM((ANG, count), BF16)] * 3,
    )


def share_and_add(slots, axis, block):
    count = lax.axis_size(axis)
    have = slots
    step = 1
    total = None
    while step < count:
        got = lax.ppermute(have, axis, [(i, i ^ step) for i in range(count)])
        if 2 * step < count:
            have = jnp.concatenate([have, got], axis=0)
        else:
            total = dense(block, (have,))
            total = dense(block, (got,), (total,))
        step *= 2
    return dense(block, (have,)) if total is None else total


def halve(total, axis):
    count = lax.axis_size(axis)
    me = lax.axis_index(axis)
    step = count // 2
    while step > 0:
        half = total.shape[0] // 2
        bit = lax.rem(me // step, 2)
        sent = lax.dynamic_slice_in_dim(total, (1 - bit) * half, half, axis=0)
        kept = lax.dynamic_slice_in_dim(total, bit * half, half, axis=0)
        total = kept + lax.ppermute(sent, axis, [(i, i ^ step) for i in range(count)])
        step //= 2
    return total


def rounds_of(axis):
    return [(axis, first) for first in (0, 1) if swap_pairs(lax.axis_size(axis), first)]


def local(
    pressure,
    velocity,
    kappa,
    drive,
    adj_pressure_in,
    adj_velocity_in,
    wall_mask,
    wall_cells,
    wall_rows,
    slot_angle,
    wall_count,
    step,
):
    depth, height, width = pressure.shape
    slots = wall_cells.size
    phase = jnp.cos(0.5 * (step % 97).astype(F32))
    slab_rounds, row_rounds, col_rounds = (rounds_of(a) for a in ("slab", "row", "col"))
    faces = call(
        slab_faces,
        [shape((2, height, width))] * len(slab_rounds),
        (pressure, kappa, adj_pressure_in),
        [VM] * 3,
    )
    slab_got = [swap(axis, first, m) for (axis, first), m in zip(slab_rounds, faces)]
    side_rounds = row_rounds + col_rounds
    outs = [shape((4, depth, width if axis == "row" else height)) for axis, _ in side_rounds]

    def sides(*refs):
        side_faces(side_rounds, *refs)

    messages = call(
        sides,
        outs,
        (pressure, kappa, adj_pressure_in, adj_velocity_in, wall_mask),
        [VM] * 5,
    )
    side_got = [swap(axis, first, m) for (axis, first), m in zip(side_rounds, messages)]
    counts = (len(slab_rounds), len(row_rounds), len(col_rounds))

    def main(*refs):
        main_body(*counts, refs)

    flat = (1, slots)
    lam, mine, *lam_faces = call(
        main,
        [shape((3, depth, height, width)), shape((3, slots // 128, 128))]
        + [shape((height, width))] * len(slab_rounds),
        (
            pressure,
            velocity,
            kappa,
            drive,
            adj_pressure_in,
            adj_velocity_in,
            wall_mask,
            wall_cells.reshape(flat),
            wall_rows.reshape(flat),
            slot_angle.reshape(flat),
            wall_count.reshape(1),
            phase,
            *slab_got,
            *side_got,
        ),
        [VM] * 10 + [SM] * 2 + [VM] * sum(counts),
        [pltpu.VMEM((depth, height, width), F32), pltpu.VMEM((depth * height, width), F32)],
    )
    lam_got = [swap(axis, first, m) for (axis, first), m in zip(slab_rounds, lam_faces)]

    def pressure_step(*refs):
        pressure_body(*counts, refs)

    adj_pressure = call(
        pressure_step,
        shape((depth, height, width)),
        (lam, kappa, adj_pressure_in, *lam_got, *side_got),
        [VM] * (3 + sum(counts)),
    )
    total = share_and_add(mine, "slab", NROWS // lax.axis_size("slab"))
    total = halve(halve(total, "row"), "col")
    return (adj_pressure, lam, total)


def solution(mesh):
    in_specs = (
        P("slab", "row", "col"),
        P(None, "slab", "row", "col"),
        P("slab", "row", "col"),
        P("slab", "row", "col"),
        P("slab", "row", "col"),
        P(None, "slab", "row", "col"),
        P("slab", "row", "col"),
        P("slab", "row", "col", None),
        P("slab", "row", "col", None),
        P("slab", "row", "col", None),
        P("slab", "row", "col"),
        P(),
    )
    out_specs = (
        P("slab", "row", "col"),
        P(None, "slab", "row", "col"),
        P(("slab", "row", "col"), None),
    )
    return jax.shard_map(local, mesh=mesh, in_specs=in_specs, out_specs=out_specs, check_vma=False)
```

time: 161 us -> 42.7 us (0.27); the launches traced: 159 us -> 42.3 us
  waiting for transfers between devices: 90.5 us -> 11.7 us
  starting transfers between devices: 31.2 us -> 14.8 us
  between operations: 15.9 us -> 2.19 us
  other arithmetic: 11 us -> 0.64 us
  Pallas kernels: 0 us -> 7.33 us
  local copies, waits for them, and re-layouts: 10.4 us -> 5.67 us
    reduce_scatter x2 -> x0, waiting for transfers between devices: 80.6 us -> none  [the longest x1 58.9 us: local(): lax.psum_scatter(dense, 'slab', scatter_dimension=0, tiled=True)]
    ppermute x12 -> x11, starting transfers between devices: 31.1 us -> 14.8 us  [the longest x6 9.37 us: swap(): return lax.ppermute(message, axis, swap_pairs(lax.axis_size(axis), first))]
    pallas_call x0 -> x6, Pallas kernels: none -> 7.33 us  [call(): pl.pallas_call(body, out_shape=outs, in_specs=specs, out_specs=jax.tree.m...]
    unnamed x24 -> x28, local copies, waits for them, and re-layouts: 0.89 us -> 5.64 us
    slice x11 -> x0, local copies, waits for them, and re-layouts: 4.38 us -> none  [the longest x5 2.08 us: padded_2(): lax.slice_in_dim(cells, cells.shape[dim] - width, cells.shape[dim], axis=...]
    scatter-add x1 -> x0, other arithmetic: 3.25 us -> none  [local(): dense = jnp.zeros((NROWS, ANG), jnp.float32).at[rows].add(contrib)]
    gather x1 -> x0, local copies, waits for them, and re-layouts: 3.14 us -> none  [local(): values = sens.reshape(-1)[cells]]
    concatenate x4 -> x1, other arithmetic: 2.99 us -> 0.01 us  [share_and_add(): have = jnp.concatenate([have, got], axis=0)]
  transfers between devices with their start and end apart: 14 -> 11, of which waited for: 8 -> 6; matrix products, arithmetic and copies ran while one was open for 8% -> 0% of each run, Pallas kernels for 0% -> 9%
where the time goes in v1:
time: 42.7 us; the launch traced here: 42.3 us
  starting transfers between devices  14.8 us (35%)
  waiting for transfers between devices  11.7 us (27%)
  Pallas kernels  7.33 us (17%)
  local copies, waits for them, and re-layouts  5.67 us (13%)
  between operations  2.19 us (5%)
  other arithmetic  0.64 us (1%)
    ppermute x6, starting transfers between devices, swap(): return lax.ppermute(message, axis, swap_pairs(lax.axis_size(axis), first))  9.37 us
    pallas_call x6, Pallas kernels, call(): pl.pallas_call(body, out_shape=outs, in_specs=specs, out_specs=jax.tree.m...  7.33 us
    ppermute x3, waiting for transfers between devices, share_and_add(): got = lax.ppermute(have, axis, [(i, i ^ step) for i in range(count)])  7.24 us
    unnamed x28, local copies, waits for them, and re-layouts  5.64 us
    ppermute x6, waiting for transfers between devices, swap(): return lax.ppermute(message, axis, swap_pairs(lax.axis_size(axis), first))  4.45 us
    ppermute x3, starting transfers between devices, share_and_add(): got = lax.ppermute(have, axis, [(i, i ^ step) for i in range(count)])  3.83 us
    ppermute x2, starting transfers between devices, halve(): lax.ppermute(sent, axis, [(i, i ^ step) for i in range(count)])  1.63 us
  transfers between devices with their start and end apart: 11, of which 6 were waited for; matrix products, arithmetic and copies ran while one was open for 0% of the time, Pallas kernels for 9%

profile of v1, /device:TPU:16, one launch (start us, length us, event | category | flops | bytes accessed | tf_op | source)
XLA Modules:
  0.0 42.3 jit_solution(11664229819272356044)
XLA Ops:
  0.6 0.0 copy-start
  0.6 0.9 %copy-done = f32[4,128,128]{2,1,0:T(8,128)S(1)} copy-done((f32[4,128,128]{2,1,0:T(8,128)S(1)}, f32[4,128,128]{2,1,0:T(8,128)}, u32[]{:S(2)}) %copy-start) | copy-done | bytes 262168
  1.6 0.0 copy-start.2
  1.6 0.9 %copy-done.2 = f32[4,128,128]{2,1,0:T(8,128)S(1)} copy-done((f32[4,128,128]{2,1,0:T(8,128)S(1)}, f32[4,128,128]{2,1,0:T(8,128)}, u32[]{:S(2)}) %copy-start.2) | copy-done | bytes 262168
  2.5 0.0 copy-start.5
  2.5 0.9 %copy-done.5 = f32[4,128,128]{2,1,0:T(8,128)S(1)} copy-done((f32[4,128,128]{2,1,0:T(8,128)S(1)}, f32[4,128,128]{2,1,0:T(8,128)}, u32[]{:S(2)}) %copy-start.5) | copy-done | bytes 262168
  3.5 1.6 %collective-permute-start = (f32[2,128,128]{2,1,0:T(8,128)S(1)}, f32[2,128,128]{2,1,0:T(8,128)S(1)}, u32[]{:S(2)}, u32[]{:S(2)}) collective-permute-start(f32[2,128,128]{2,1,0:T(8,128)S(1)} %get-tuple-element.11), channel_id=1, source_target_pairs={{0,4},{4,0},{8,12},{12,8},{16,20},{20,16},{24,28},{28,24},{1,5},{5... | collective-permute-start | bytes 393224 | tf_op jit(solution)/shard_map/ppermute | solution.py:45
  5.1 2.3 %collective-permute-start.1 = (f32[2,128,128]{2,1,0:T(8,128)S(1)}, f32[2,128,128]{2,1,0:T(8,128)S(1)}, u32[]{:S(2)}, u32[]{:S(2)}) collective-permute-start(f32[2,128,128]{2,1,0:T(8,128)S(1)} %get-tuple-element.12), channel_id=1, source_target_pairs={{4,8},{8,4},{12,16},{16,12},{20,24},{24,20},{5,9},{9,5},{13,17},{1... | collective-permute-start | bytes 393224 | tf_op jit(solution)/shard_map/ppermute | solution.py:45
  7.4 0.0 copy-done.4
  7.4 0.0 copy-start.6
  7.4 0.9 %copy-done.6 = s32[4,128,128]{2,1,0:T(8,128)S(1)} copy-done((s32[4,128,128]{2,1,0:T(8,128)S(1)}, s32[4,128,128]{2,1,0:T(8,128)}, u32[]{:S(2)}) %copy-start.6) | copy-done | bytes 262168
  8.4 0.0 copy-start.7
  8.4 0.0 copy-start.9
  8.4 0.5 %shard_map.140 = (f32[4,4,128]{2,1,0:T(4,128)S(1)}, f32[4,4,128]{2,1,0:T(4,128)S(1)}) custom-call(f32[4,128,128]{2,1,0:T(8,128)S(1)} %copy-done.5, f32[4,128,128]{2,1,0:T(8,128)S(1)} %copy-done, f32[4,128,128]{2,1,0:T(8,128)S(1)} %copy-done.2, f32[3,4,128,128]{3,2,1,0:T(8,128)S(1)} %copy-done.4, s32[4,128,128]{2,1,0:T(8,128)S(1)} %copy-done.6), custom_call_target="tpu_custom_call" | custom-call | flops 1000000 | bytes 1000000 | tf_op jit(solution)/shard_map/pallas_call | solution.py:18
  8.9 0.1 collective-permute-start.2
  9.0 1.6 %collective-permute-start.3 = (f32[4,4,128]{2,1,0:T(4,128)S(1)}, f32[4,4,128]{2,1,0:T(4,128)S(1)}, u32[]{:S(2)}, u32[]{:S(2)}) collective-permute-start(f32[4,4,128]{2,1,0:T(4,128)S(1)} %get-tuple-element.14), channel_id=1, source_target_pairs={{0,1},{1,0},{2,3},{3,2},{4,5},{5,4},{6,7},{7,6},{8,9},{9,8},{10,11... | collective-permute-start | bytes 24584 | tf_op jit(solution)/shard_map/ppermute | solution.py:45
  11.9 0.0 collective-permute-done.2.refs_14_.refs_5_
  11.9 0.8 %collective-permute-done.3.refs_15_.refs_6_ = f32[4,4,128]{2,1,0:T(4,128)S(1)} collective-permute-done((f32[4,4,128]{2,1,0:T(4,128)S(1)}, f32[4,4,128]{2,1,0:T(4,128)S(1)}, u32[]{:S(2)}, u32[]{:S(2)}) %collective-permute-start.3) | collective-permute-done | bytes 8224 | tf_op jit(solution)/shard_map/ppermute | solution.py:45
  12.7 0.0 collective-permute-done.refs_12_
  12.7 0.2 collective-permute-done.1.refs_13_
  12.9 0.0 copy-done.7
  12.9 0.0 copy-done.9
  12.9 0.0 copy-done.12
  12.9 0.7 %copy-done.11 = s32[1,1,1,512]{3,2,1,0:T(1,128)S(1)} copy-done((s32[1,1,1,512]{3,2,1,0:T(1,128)S(1)}, s32[1,1,1,512]{3,2,1,0:T(1,128)}, u32[]{:S(2)}) %copy-start.11) | copy-done | bytes 2072
  13.5 0.0 copy-done.10
  13.5 1.9 %shard_map.141 = (f32[3,4,128,128]{3,2,1,0:T(8,128)}, f32[3,4,128]{2,1,0:T(4,128)S(1)}, f32[128,128]{1,0:T(8,128)S(1)}, f32[128,128]{1,0:T(8,128)S(1)}) custom-call(f32[4,128,128]{2,1,0:T(8,128)S(1)} %copy-done.5, f32[3,4,128,128]{3,2,1,0:T(8,128)S(1)} %copy-done.7, f32[4,128,128]{2,1,0:T(8,128)S(1)} %copy-done, f32[4,128,128]{2,1,0:T(8,128)S(1)} %copy-done.9, ...), custom_call_target="tpu_custom_call" | custom-call | flops 1000000 | bytes 1000000 | tf_op jit(solution)/shard_map/pallas_call | solution.py:18
  15.5 2.5 %collective-permute-start.6 = (f32[3,4,128]{2,1,0:T(4,128)S(1)}, f32[3,4,128]{2,1,0:T(4,128)S(1)}, u32[]{:S(2)}, u32[]{:S(2)}) collective-permute-start(f32[3,4,128]{2,1,0:T(4,128)S(1)} %get-tuple-element.18), channel_id=1, source_target_pairs={{0,4},{4,0},{8,12},{12,8},{16,20},{20,16},{24,28},{28,24},{1,5},{5... | collective-permute-start | bytes 18440 | tf_op jit(solution)/shard_map/ppermute | solution.py:277
  18.0 1.6 %collective-permute-done.6 = f32[3,4,128]{2,1,0:T(4,128)S(1)} collective-permute-done((f32[3,4,128]{2,1,0:T(4,128)S(1)}, f32[3,4,128]{2,1,0:T(4,128)S(1)}, u32[]{:S(2)}, u32[]{:S(2)}) %collective-permute-start.6) | collective-permute-done | bytes 6176 | tf_op jit(solution)/shard_map/ppermute | solution.py:277
  19.6 1.1 %collective-permute-start.7 = (f32[6,4,128]{2,1,0:T(4,128)S(1)}, f32[6,4,128]{2,1,0:T(4,128)S(1)}, u32[]{:S(2)}, u32[]{:S(2)}) collective-permute-start(f32[6,4,128]{2,1,0:T(4,128)S(1)} %pad_maximum_fusion), channel_id=1, source_target_pairs={{0,8},{4,12},{8,0},{12,4},{16,24},{20,28},{24,16},{28,20},{1,9},{5... | collective-permute-start | bytes 36872 | tf_op jit(solution)/shard_map/ppermute | solution.py:277
  20.7 2.7 %collective-permute-done.7 = f32[6,4,128]{2,1,0:T(4,128)S(1)} collective-permute-done((f32[6,4,128]{2,1,0:T(4,128)S(1)}, f32[6,4,128]{2,1,0:T(4,128)S(1)}, u32[]{:S(2)}, u32[]{:S(2)}) %collective-permute-start.7) | collective-permute-done | bytes 12320 | tf_op jit(solution)/shard_map/ppermute | solution.py:277
  23.4 0.2 collective-permute-start.8
  23.6 1.5 %shard_map.143.refs_1_ = f32[256,64]{1,0:T(8,128)S(1)} custom-call(f32[12,4,128]{2,1,0:T(4,128)S(1)} %constant_dynamic-update-slice_fusion.refs_0_), custom_call_target="tpu_custom_call" | custom-call | flops 1000000 | bytes 1000000 | tf_op jit(solution)/shard_map/pallas_call | solution.py:18
  25.2 3.0 %collective-permute-done.8.refs_0_ = f32[12,4,128]{2,1,0:T(4,128)S(1)} collective-permute-done((f32[12,4,128]{2,1,0:T(4,128)S(1)}, f32[12,4,128]{2,1,0:T(4,128)S(1)}, u32[]{:S(2)}, u32[]{:S(2)}) %collective-permute-start.8) | collective-permute-done | bytes 24608 | tf_op jit(solution)/shard_map/ppermute | solution.py:277
  28.1 1.5 %shard_map.144 = f32[256,64]{1,0:T(8,128)S(1)} custom-call(f32[12,4,128]{2,1,0:T(4,128)S(1)} %collective-permute-done.8.refs_0_, f32[256,64]{1,0:T(8,128)S(1)} %shard_map.143.refs_1_), custom_call_target="tpu_custom_call" | custom-call | flops 1000000 | bytes 1000000 | tf_op jit(solution)/shard_map/pallas_call | solution.py:18
  29.6 0.0 copy-start.1
  29.7 0.1 collective-permute-start.9
  29.8 2.0 %collective-permute-start.4 = (f32[128,128]{1,0:T(8,128)S(1)}, f32[128,128]{1,0:T(8,128)S(1)}, u32[]{:S(2)}, u32[]{:S(2)}) collective-permute-start(f32[128,128]{1,0:T(8,128)S(1)} %get-tuple-element.16), channel_id=1, source_target_pairs={{0,4},{4,0},{8,12},{12,8},{16,20},{20,16},{24,28},{28,24},{1,5},{5... | collective-permute-start | bytes 196616 | tf_op jit(solution)/shard_map/ppermute | solution.py:45
  31.7 1.9 %collective-permute-start.5 = (f32[128,128]{1,0:T(8,128)S(1)}, f32[128,128]{1,0:T(8,128)S(1)}, u32[]{:S(2)}, u32[]{:S(2)}) collective-permute-start(f32[128,128]{1,0:T(8,128)S(1)} %get-tuple-element.17), channel_id=1, source_target_pairs={{4,8},{8,4},{12,16},{16,12},{20,24},{24,20},{5,9},{9,5},{13,17},{1... | collective-permute-start | bytes 196616 | tf_op jit(solution)/shard_map/ppermute | solution.py:45
  33.7 0.0 collective-permute-done.9
  33.7 1.6 %collective-permute-start.10 = (f32[64,64]{1,0:T(8,128)S(1)}, f32[64,64]{1,0:T(8,128)S(1)}, u32[]{:S(2)}, u32[]{:S(2)}) collective-permute-start(f32[64,64]{1,0:T(8,128)S(1)} %constant_dynamic-slice_fusion), channel_id=1, source_target_pairs={{0,1},{1,0},{2,3},{3,2},{4,5},{5,4},{6,7},{7,6},{8,9},{9,8},{10,11... | collective-permute-start | bytes 49160 | tf_op jit(solution)/shard_map/ppermute | solution.py:296
  35.3 0.0 collective-permute-done.4.refs_3_
  35.3 3.5 %collective-permute-done.5.refs_4_ = f32[128,128]{1,0:T(8,128)S(1)} collective-permute-done((f32[128,128]{1,0:T(8,128)S(1)}, f32[128,128]{1,0:T(8,128)S(1)}, u32[]{:S(2)}, u32[]{:S(2)}) %collective-permute-start.5) | collective-permute-done | bytes 65568 | tf_op jit(solution)/shard_map/ppermute | solution.py:45
  38.8 0.0 copy-done.3
  38.8 0.0 copy-done.1
  38.8 1.1 %copy-done.8 = f32[3,4,128,128]{3,2,1,0:T(8,128)S(1)} copy-done((f32[3,4,128,128]{3,2,1,0:T(8,128)S(1)}, f32[3,4,128,128]{3,2,1,0:T(8,128)}, u32[]{:S(2)}) %copy-start.8) | copy-done | bytes 786456
  39.9 1.8 %shard_map.142 = f32[4,128,128]{2,1,0:T(8,128)} custom-call(f32[3,4,128,128]{3,2,1,0:T(8,128)S(1)} %copy-done.8, f32[4,128,128]{2,1,0:T(8,128)S(1)} %copy-done.1, f32[4,128,128]{2,1,0:T(8,128)S(1)} %copy-done.3, f32[128,128]{1,0:T(8,128)S(1)} %collective-permute-done.4.refs_3_, f32[128,128]{1,0:T(8,128)S(1)} %collective-permute-done.5.refs_4_, ...), custom_call_target="tpu_custom_call" | custom-call | flops 1000000 | bytes 1000000 | tf_op jit(solution)/shard_map/pallas_call | solution.py:18
  41.7 0.0 collective-permute-done.10
  41.7 0.6 %dynamic-slice_add_fusion.1 = f32[64,64]{1,0:T(8,128)} fusion(f32[64,64]{1,0:T(8,128)S(1)} %collective-permute-done.10, f32[128,64]{1,0:T(8,128)S(1)} %dynamic-slice_add_fusion, s32[]{:T(128)S(6)} %select_n.25), kind=kLoop, calls=%fused_computation.1 | loop fusion | flops 4096 | bytes 49156 | tf_op jit(solution)/shard_map/add | solution.py:296
  (14 shorter events, 0.1 us)
Async XLA Ops:
  0.6 1.0 %copy-start = (f32[4,128,128]{2,1,0:T(8,128)S(1)}, f32[4,128,128]{2,1,0:T(8,128)}, u32[]{:S(2)}) copy-start(f32[4,128,128]{2,1,0:T(8,128)} %refs_1_.5) | copy-start | bytes 786436
  1.6 0.9 %copy-start.2 = (f32[4,128,128]{2,1,0:T(8,128)S(1)}, f32[4,128,128]{2,1,0:T(8,128)}, u32[]{:S(2)}) copy-start(f32[4,128,128]{2,1,0:T(8,128)} %refs_2_.5) | copy-start | bytes 786436
  2.5 0.9 %copy-start.5 = (f32[4,128,128]{2,1,0:T(8,128)S(1)}, f32[4,128,128]{2,1,0:T(8,128)}, u32[]{:S(2)}) copy-start(f32[4,128,128]{2,1,0:T(8,128)} %refs_0_.3) | copy-start | bytes 786436
  3.5 3.9 %copy-start.4 = (f32[3,4,128,128]{3,2,1,0:T(8,128)S(1)}, f32[3,4,128,128]{3,2,1,0:T(8,128)}, u32[]{:S(2)}) copy-start(f32[3,4,128,128]{3,2,1,0:T(8,128)} %refs_5_.1) | copy-start | bytes 2359300
  3.5 9.2 %collective-permute-start = (f32[2,128,128]{2,1,0:T(8,128)S(1)}, f32[2,128,128]{2,1,0:T(8,128)S(1)}, u32[]{:S(2)}, u32[]{:S(2)}) collective-permute-start(f32[2,128,128]{2,1,0:T(8,128)S(1)} %get-tuple-element.11), channel_id=1, source_target_pairs={{0,4},{4,0},{8,12},{12,8},{16,20},{20,16},{24,28},{28,24},{1,5},{5... | collective-permute-start | bytes 393224 | tf_op jit(solution)/shard_map/ppermute | solution.py:45
  5.1 7.7 %collective-permute-start.1 = (f32[2,128,128]{2,1,0:T(8,128)S(1)}, f32[2,128,128]{2,1,0:T(8,128)S(1)}, u32[]{:S(2)}, u32[]{:S(2)}) collective-permute-start(f32[2,128,128]{2,1,0:T(8,128)S(1)} %get-tuple-element.12), channel_id=1, source_target_pairs={{4,8},{8,4},{12,16},{16,12},{20,24},{24,20},{5,9},{9,5},{13,17},{1... | collective-permute-start | bytes 393224 | tf_op jit(solution)/shard_map/ppermute | solution.py:45
  7.4 1.0 %copy-start.6 = (s32[4,128,128]{2,1,0:T(8,128)S(1)}, s32[4,128,128]{2,1,0:T(8,128)}, u32[]{:S(2)}) copy-start(s32[4,128,128]{2,1,0:T(8,128)} %refs_6_.1) | copy-start | bytes 786436
  8.4 4.5 %copy-start.7 = (f32[3,4,128,128]{3,2,1,0:T(8,128)S(1)}, f32[3,4,128,128]{3,2,1,0:T(8,128)}, u32[]{:S(2)}) copy-start(f32[3,4,128,128]{3,2,1,0:T(8,128)} %refs_1_.4) | copy-start | bytes 2359300
  8.4 4.5 %copy-start.9 = (f32[4,128,128]{2,1,0:T(8,128)S(1)}, f32[4,128,128]{2,1,0:T(8,128)}, u32[]{:S(2)}) copy-start(f32[4,128,128]{2,1,0:T(8,128)} %refs_3_.3) | copy-start | bytes 786436
  8.9 4.0 %copy-start.12 = (f32[1,1,1,512]{3,2,1,0:T(1,128)S(1)}, f32[1,1,1,512]{3,2,1,0:T(1,128)}, u32[]{:S(2)}) copy-start(f32[1,1,1,512]{3,2,1,0:T(1,128)} %param.21) | copy-start | bytes 6148
  8.9 3.0 %collective-permute-start.2 = (f32[4,4,128]{2,1,0:T(4,128)S(1)}, f32[4,4,128]{2,1,0:T(4,128)S(1)}, u32[]{:S(2)}, u32[]{:S(2)}) collective-permute-start(f32[4,4,128]{2,1,0:T(4,128)S(1)} %get-tuple-element.13), channel_id=1, source_target_pairs={{0,2},{2,0},{1,3},{3,1},{4,6},{6,4},{5,7},{7,5},{8,10},{10,8},{9,1... | collective-permute-start | bytes 24584 | tf_op jit(solution)/shard_map/ppermute | solution.py:45
  9.0 3.7 %collective-permute-start.3 = (f32[4,4,128]{2,1,0:T(4,128)S(1)}, f32[4,4,128]{2,1,0:T(4,128)S(1)}, u32[]{:S(2)}, u32[]{:S(2)}) collective-permute-start(f32[4,4,128]{2,1,0:T(4,128)S(1)} %get-tuple-element.14), channel_id=1, source_target_pairs={{0,1},{1,0},{2,3},{3,2},{4,5},{5,4},{6,7},{7,6},{8,9},{9,8},{10,11... | collective-permute-start | bytes 24584 | tf_op jit(solution)/shard_map/ppermute | solution.py:45
  12.8 0.7 %copy-start.11 = (s32[1,1,1,512]{3,2,1,0:T(1,128)S(1)}, s32[1,1,1,512]{3,2,1,0:T(1,128)}, u32[]{:S(2)}) copy-start(s32[1,1,1,512]{3,2,1,0:T(1,128)} %param.20) | copy-start | bytes 6148
  12.8 0.7 %copy-start.10 = (s32[1,1,1,512]{3,2,1,0:T(1,128)S(1)}, s32[1,1,1,512]{3,2,1,0:T(1,128)}, u32[]{:S(2)}) copy-start(s32[1,1,1,512]{3,2,1,0:T(1,128)} %param.19) | copy-start | bytes 6148
  15.5 4.1 %collective-permute-start.6 = (f32[3,4,128]{2,1,0:T(4,128)S(1)}, f32[3,4,128]{2,1,0:T(4,128)S(1)}, u32[]{:S(2)}, u32[]{:S(2)}) collective-permute-start(f32[3,4,128]{2,1,0:T(4,128)S(1)} %get-tuple-element.18), channel_id=1, source_target_pairs={{0,4},{4,0},{8,12},{12,8},{16,20},{20,16},{24,28},{28,24},{1,5},{5... | collective-permute-start | bytes 18440 | tf_op jit(solution)/shard_map/ppermute | solution.py:277
  19.6 3.8 %collective-permute-start.7 = (f32[6,4,128]{2,1,0:T(4,128)S(1)}, f32[6,4,128]{2,1,0:T(4,128)S(1)}, u32[]{:S(2)}, u32[]{:S(2)}) collective-permute-start(f32[6,4,128]{2,1,0:T(4,128)S(1)} %pad_maximum_fusion), channel_id=1, source_target_pairs={{0,8},{4,12},{8,0},{12,4},{16,24},{20,28},{24,16},{28,20},{1,9},{5... | collective-permute-start | bytes 36872 | tf_op jit(solution)/shard_map/ppermute | solution.py:277
  23.4 4.7 %collective-permute-start.8 = (f32[12,4,128]{2,1,0:T(4,128)S(1)}, f32[12,4,128]{2,1,0:T(4,128)S(1)}, u32[]{:S(2)}, u32[]{:S(2)}) collective-permute-start(f32[12,4,128]{2,1,0:T(4,128)S(1)} %constant_dynamic-update-slice_fusion.refs_0_), channel_id=1, source_target_pairs={{0,16},{4,20},{8,24},{12,28},{16,0},{20,4},{24,8},{28,12},{1,17},{... | collective-permute-start | bytes 73736 | tf_op jit(solution)/shard_map/ppermute | solution.py:277
  28.1 10.7 %copy-start.3 = (f32[4,128,128]{2,1,0:T(8,128)S(1)}, f32[4,128,128]{2,1,0:T(8,128)}, u32[]{:S(2)}) copy-start(f32[4,128,128]{2,1,0:T(8,128)} %refs_2_.5) | copy-start | bytes 786436
  29.6 9.2 %copy-start.1 = (f32[4,128,128]{2,1,0:T(8,128)S(1)}, f32[4,128,128]{2,1,0:T(8,128)}, u32[]{:S(2)}) copy-start(f32[4,128,128]{2,1,0:T(8,128)} %refs_1_.5) | copy-start | bytes 786436
  29.7 4.0 %collective-permute-start.9 = (f32[128,64]{1,0:T(8,128)S(1)}, f32[128,64]{1,0:T(8,128)S(1)}, u32[]{:S(2)}, u32[]{:S(2)}) collective-permute-start(f32[128,64]{1,0:T(8,128)S(1)} %constant_dynamic-slice_fusion.1), channel_id=1, source_target_pairs={{0,2},{2,0},{1,3},{3,1},{4,6},{6,4},{5,7},{7,5},{8,10},{10,8},{9,1... | collective-permute-start | bytes 98312 | tf_op jit(solution)/shard_map/ppermute | solution.py:296
  29.8 5.5 %collective-permute-start.4 = (f32[128,128]{1,0:T(8,128)S(1)}, f32[128,128]{1,0:T(8,128)S(1)}, u32[]{:S(2)}, u32[]{:S(2)}) collective-permute-start(f32[128,128]{1,0:T(8,128)S(1)} %get-tuple-element.16), channel_id=1, source_target_pairs={{0,4},{4,0},{8,12},{12,8},{16,20},{20,16},{24,28},{28,24},{1,5},{5... | collective-permute-start | bytes 196616 | tf_op jit(solution)/shard_map/ppermute | solution.py:45
  31.7 7.0 %collective-permute-start.5 = (f32[128,128]{1,0:T(8,128)S(1)}, f32[128,128]{1,0:T(8,128)S(1)}, u32[]{:S(2)}, u32[]{:S(2)}) collective-permute-start(f32[128,128]{1,0:T(8,128)S(1)} %get-tuple-element.17), channel_id=1, source_target_pairs={{4,8},{8,4},{12,16},{16,12},{20,24},{24,20},{5,9},{9,5},{13,17},{1... | collective-permute-start | bytes 196616 | tf_op jit(solution)/shard_map/ppermute | solution.py:45
  33.7 8.0 %collective-permute-start.10 = (f32[64,64]{1,0:T(8,128)S(1)}, f32[64,64]{1,0:T(8,128)S(1)}, u32[]{:S(2)}, u32[]{:S(2)}) collective-permute-start(f32[64,64]{1,0:T(8,128)S(1)} %constant_dynamic-slice_fusion), channel_id=1, source_target_pairs={{0,1},{1,0},{2,3},{3,2},{4,5},{5,4},{6,7},{7,6},{8,9},{9,8},{10,11... | collective-permute-start | bytes 49160 | tf_op jit(solution)/shard_map/ppermute | solution.py:296
  38.8 1.1 %copy-start.8 = (f32[3,4,128,128]{3,2,1,0:T(8,128)S(1)}, f32[3,4,128,128]{3,2,1,0:T(8,128)}, u32[]{:S(2)}) copy-start(f32[3,4,128,128]{3,2,1,0:T(8,128)} %get-tuple-element.9.refs_0_) | copy-start | bytes 2359300

commit v2 on v1

v2 whole, which is shorter than its diff:
```python
import jax
import jax.numpy as jnp
from jax import lax
from jax.experimental import pallas as pl
from jax.experimental.pallas import tpu as pltpu
from jax.sharding import PartitionSpec as P


NROWS = 2048
ANG = 64
F32 = jnp.float32
BF16 = jnp.bfloat16
VM = pl.BlockSpec(memory_space=pltpu.VMEM)
HB = pl.BlockSpec(memory_space=pltpu.HBM)
SM = pl.BlockSpec(memory_space=pltpu.SMEM)
LIMIT = pltpu.CompilerParams(vmem_limit_bytes=24 << 20)


def call(body, outs, args, specs, scratch=(), out_specs=None):
    return pl.pallas_call(
        body,
        out_shape=outs,
        in_specs=specs,
        out_specs=jax.tree.map(lambda _: VM, outs) if out_specs is None else out_specs,
        scratch_shapes=list(scratch),
        compiler_params=LIMIT,
        cost_estimate=pl.CostEstimate(flops=1_000_000, bytes_accessed=1_000_000, transcendentals=0),
    )(*args)


def fetch(pairs, sems):
    copies = [pltpu.make_async_copy(s, d, sems.at[i]) for i, (s, d) in enumerate(pairs)]
    for copy in copies:
        copy.start()
    return copies


def shape(dims, dtype=F32):
    return jax.ShapeDtypeStruct(tuple(dims), dtype)


def is_odd(axis):
    return lax.rem(lax.axis_index(axis), 2) == 1


def swap_pairs(count, first):
    pairs = []
    for low in range(first, count - 1, 2):
        pairs += [(low, low + 1), (low + 1, low)]
    return pairs


def swap(axis, first, message):
    return lax.ppermute(message, axis, swap_pairs(lax.axis_size(axis), first))


def faces_body(rounds, refs):
    p_ref, k_ref, a_ref = refs[:3]
    outs, (pv_ref, qv_ref, av_ref, kv_ref, sems) = refs[3 : 3 + len(rounds)], refs[3 + len(rounds) :]
    depth = pv_ref.shape[0]
    copies = fetch(((k_ref, kv_ref), (a_ref, av_ref), (p_ref, pv_ref)), sems)
    copies[0].wait()
    copies[1].wait()
    for x in range(depth):
        qv_ref[x] = kv_ref[x] * av_ref[x]
    copies[2].wait()
    odd = is_odd("slab")
    for (_, first), out_ref in zip(rounds, outs):
        at = jnp.where(odd != (first == 1), 0, depth - 1)
        out_ref[0] = pv_ref[at]
        out_ref[1] = qv_ref[at]


def sides_body(rounds, refs):
    pv_ref, qv_ref, t_ref, m_ref = refs[:4]
    outs, (tv_ref, free_ref, mv_ref, sems) = refs[4 : 4 + len(rounds)], refs[4 + len(rounds) :]
    depth, height, width = pv_ref.shape
    copies = fetch(((m_ref, mv_ref), (t_ref, tv_ref)), sems)
    copies[0].wait()
    for x in range(depth):
        free_ref[x] = 1.0 - mv_ref[x].astype(F32)
    copies[1].wait()
    lanes = lax.broadcasted_iota(jnp.int32, (height, width), 1)
    for (axis, first), out_ref in zip(rounds, outs):
        high = is_odd(axis) == (first == 1)
        sign = jnp.where(high, -0.5, 0.5)
        if axis == "row":
            at = jnp.where(high, height - 1, 0)
            inner = jnp.where(high, height - 2, 1)
            for x in range(depth):
                face, second = pl.ds(at, 1), pl.ds(inner, 1)
                free = free_ref[x, face, :]
                out_ref[0, pl.ds(x, 1), :] = pv_ref[x, face, :]
                out_ref[1, pl.ds(x, 1), :] = qv_ref[x, face, :]
                out_ref[2, pl.ds(x, 1), :] = free * (tv_ref[1, x, face, :] + sign * qv_ref[x, second, :])
                out_ref[3, pl.ds(x, 1), :] = free
        else:
            at = jnp.where(high, width - 1, 0)
            turn = jnp.where(high, 1, width - 1)
            table = jnp.zeros((height, width), F32)
            for x in range(depth):
                free, scaled = free_ref[x], qv_ref[x]
                behind = pltpu.roll(scaled, turn, 1)
                fields = (pv_ref[x], scaled, free * (tv_ref[2, x] + sign * behind), free)
                for f, field in enumerate(fields):
                    lane = f * depth + x
                    moved = pltpu.roll(field, lax.rem(lane - at + width, width), 1)
                    table = jnp.where(lanes == lane, moved, table)
            flipped = table.T
            for f in range(4):
                out_ref[f] = flipped[f * depth : (f + 1) * depth]


def take_halo(axis, refs):
    odd = is_odd(axis)
    first = refs[0][...]
    second = refs[1][...] if len(refs) > 1 else jnp.zeros_like(first)
    return jnp.where(odd, first, second), jnp.where(odd, second, first)


def side(field, axis, low, high):
    size = field.shape[axis]
    at = lax.broadcasted_iota(jnp.int32, field.shape, axis)
    upper = jnp.where(at == size - 1, high, pltpu.roll(field, size - 1, axis))
    lower = jnp.where(at == 0, low, pltpu.roll(field, 1, axis))
    return (upper - lower) * 0.5


def halves(value):
    top = value.astype(BF16)
    rest = value - top.astype(F32)
    mid = rest.astype(BF16)
    return top, mid, (rest - mid.astype(F32)).astype(BF16)


def inner_body(pv_ref, qv_ref, tv_ref, v_ref, d_ref, c_ref, r_ref, g_ref, ph_ref,
               total_ref, moved_ref, pick_ref, slot_in_ref, vv_ref, dv_ref, sems):
    depth, _, width = pv_ref.shape
    copies = fetch(
        (
            (c_ref, slot_in_ref.at[0]),
            (v_ref, vv_ref),
            (d_ref, dv_ref),
        ),
        sems,
    )
    for x in range(depth):
        q = qv_ref[x]
        upper = qv_ref[x + 1] if x + 1 < depth else 0.0
        lower = qv_ref[x - 1] if x > 0 else 0.0
        total_ref[0, x] = tv_ref[0, x] + (upper - lower) * 0.5
        total_ref[1, x] = tv_ref[1, x] + side(q, 0, 0.0, 0.0)
        total_ref[2, x] = tv_ref[2, x] + side(q, 1, 0.0, 0.0)
    copies[0].wait()
    cells = slot_in_ref[0]
    line = lax.div(cells, width)
    at = lax.broadcasted_iota(jnp.int32, pick_ref.shape, 0)
    pick_ref[...] = jnp.where(at == line, 1.0, 0.0).astype(BF16)
    copies[1].wait()
    copies[2].wait()
    phase = ph_ref[0]
    for x in range(depth):
        p = pv_ref[x]
        upper = pv_ref[x + 1] if x + 1 < depth else 0.0
        lower = pv_ref[x - 1] if x > 0 else 0.0
        moved_ref[0, x] = vv_ref[0, x] - 0.3 * ((upper - lower) * 0.5) + dv_ref[x] * phase
        moved_ref[1, x] = vv_ref[1, x] - 0.3 * side(p, 0, 0.0, 0.0)
        moved_ref[2, x] = vv_ref[2, x] - 0.3 * side(p, 1, 0.0, 0.0)


def edge_table(low, high, height, width):
    count = low.shape[0]
    lines = []
    for i in range(count):
        lines += [low[i : i + 1], high[i + 1 : i + 2] if i + 1 < count else None]
    lines = [l for l in lines if l is not None]
    fill = jnp.zeros((width - 2 * count, height), F32)
    return jnp.concatenate(lines + [fill, high[:1]], axis=0).T


def main_body(counts, refs):
    total_ref, moved_ref, free_ref, pick_ref, cell_ref, row_ref, angle_ref, n_ref = refs[:8]
    rest = refs[8:]
    n_slab, n_row, n_col = counts
    slab_refs, rest = rest[:n_slab], rest[n_slab:]
    row_refs, rest = rest[:n_row], rest[n_row:]
    col_refs, rest = rest[:n_col], rest[n_col:]
    lam_ref, slot_ref, *face_refs, sens_ref = rest
    _, depth, height, width = total_ref.shape
    slab_low, slab_high = take_halo("slab", slab_refs)
    row_low, row_high = take_halo("row", row_refs)
    col_low, col_high = take_halo("col", col_refs)
    low = jnp.concatenate([col_low[0] * 0.15, col_low[1] * -0.5], axis=0)
    high = jnp.concatenate([col_high[0] * -0.15, col_high[1] * 0.5], axis=0)
    edges = edge_table(low, high, height, width)
    lanes = lax.broadcasted_iota(jnp.int32, (8, width), 1)
    is_edge = (lanes == 0) | (lanes == width - 1)
    tall = lax.broadcasted_iota(jnp.int32, (8, width), 0)
    for x in range(depth):
        for y in range(0, height, 8):
            at = slice(y, y + 8)
            totals = [total_ref[c, x, at] for c in range(3)]
            moves = [moved_ref[c, x, at] for c in range(3)]
            if x == 0:
                totals[0] = totals[0] - 0.5 * slab_low[1, at]
                moves[0] = moves[0] + 0.15 * slab_low[0, at]
            if x == depth - 1:
                totals[0] = totals[0] + 0.5 * slab_high[1, at]
                moves[0] = moves[0] - 0.15 * slab_high[0, at]
            one = slice(x, x + 1)
            if y == 0:
                totals[1] = totals[1] - jnp.where(tall == 0, 0.5 * row_low[1, one], 0.0)
                moves[1] = moves[1] + jnp.where(tall == 0, 0.15 * row_low[0, one], 0.0)
            if y == height - 8:
                totals[1] = totals[1] + jnp.where(tall == 7, 0.5 * row_high[1, one], 0.0)
                moves[1] = moves[1] - jnp.where(tall == 7, 0.15 * row_high[0, one], 0.0)
            for which, terms in ((1, totals), (0, moves)):
                shift = (width - 2 * (which * depth + x)) % width
                turned = pltpu.roll(edges[at], shift, 1) if shift else edges[at]
                terms[2] = terms[2] + jnp.where(is_edge, turned, 0.0)
            free = free_ref[x, at]
            sens = totals[0] * moves[0] + totals[1] * moves[1] + totals[2] * moves[2]
            for c in range(3):
                lam_ref[c, x, at] = free * totals[c]
            sens_ref[pl.ds(x * height + y, 8), :] = -sens
    odd = is_odd("slab")
    for first, face_ref in enumerate(face_refs):
        face_ref[...] = lam_ref[0, jnp.where(odd != (first == 1), 0, depth - 1)]
    cells = cell_ref[...]
    slots = cells.shape[1]
    pieces = jnp.concatenate(halves(sens_ref[...].T), axis=0)
    found = jnp.dot(pieces, pick_ref[...], preferred_element_type=F32)
    found = found[:width] + found[width : 2 * width] + found[2 * width :]
    lane = lax.broadcasted_iota(jnp.int32, (width, slots), 0)
    values = jnp.sum(jnp.where(lane == lax.rem(cells, width), found, 0.0), axis=0, keepdims=True)
    live = lax.broadcasted_iota(jnp.int32, (1, slots), 1) < n_ref[0]
    values = jnp.where(live, values, 0.0)
    rows = row_ref[...].astype(F32)
    angles = angle_ref[...]
    for j in range(slots // 128):
        part = slice(128 * j, 128 * (j + 1))
        slot_ref[0, pl.ds(j, 1), :] = values[:, part]
        slot_ref[1, pl.ds(j, 1), :] = rows[:, part]
        slot_ref[2, pl.ds(j, 1), :] = angles[:, part]


def columns(halo, height, width):
    table = jnp.concatenate([halo[2], halo[3]], axis=0)
    table = jnp.concatenate([table, jnp.zeros((width - table.shape[0], height), F32)], axis=0)
    return table.T


def part_body(counts, refs):
    lam_ref, qv_ref, av_ref = refs[:3]
    rest = refs[3:]
    _, n_row, n_col = counts
    row_refs, rest = rest[:n_row], rest[n_row:]
    col_refs, (part_ref, out_ref, sems) = rest[:n_col], rest[n_col:]
    copies = fetch(((lam_ref, out_ref),), sems)
    depth, height, width = av_ref.shape
    row_low, row_high = take_halo("row", row_refs)
    col_low, col_high = (columns(h, height, width) for h in take_halo("col", col_refs))
    for x in range(depth):
        half = 0.5 * qv_ref[x]
        one = slice(x, x + 1)
        free = slice(depth + x, depth + x + 1)
        upper = lam_ref[0, x + 1] if x + 1 < depth else 0.0
        lower = lam_ref[0, x - 1] if x > 0 else 0.0
        row_above = row_high[2, one] - row_high[3, one] * half[height - 1 :]
        row_below = row_low[2, one] + row_low[3, one] * half[:1]
        col_above = col_high[:, one] - col_high[:, free] * half[:, width - 1 :]
        col_below = col_low[:, one] + col_low[:, free] * half[:, :1]
        spread = (
            (upper - lower) * 0.5
            + side(lam_ref[1, x], 0, row_below, row_above)
            + side(lam_ref[2, x], 1, col_below, col_above)
        )
        part_ref[x] = av_ref[x] + 0.3 * spread
    copies[0].wait()


def fix_body(refs):
    part_ref, *face_refs, out_ref = refs
    depth = part_ref.shape[0]
    low, high = take_halo("slab", face_refs)
    for x in range(depth):
        value = part_ref[x]
        if x == 0:
            value = value - 0.15 * low
        if x == depth - 1:
            value = value + 0.15 * high
        out_ref[x] = value


def dense_body(block, n_slots, n_prior, refs):
    slot_refs = refs[:n_slots]
    prior = refs[n_slots : n_slots + n_prior]
    out_ref, pick_ref, piece_ref = refs[n_slots + n_prior :]
    base = (lax.axis_index("slab") * block).astype(F32)
    here = lax.broadcasted_iota(jnp.int32, (block, 128), 0).astype(F32) + base
    knots = lax.broadcasted_iota(jnp.int32, (ANG, 128), 0).astype(F32)
    at = 0
    for slot_ref in slot_refs:
        for d in range(slot_ref.shape[0] // 3):
            for j in range(slot_ref.shape[1]):
                value = slot_ref[3 * d, pl.ds(j, 1), :] * (1.0 / 6.0)
                row = slot_ref[3 * d + 1, pl.ds(j, 1), :]
                angle = slot_ref[3 * d + 2, pl.ds(j, 1), :]
                lanes = pl.ds(at, 128)
                pick_ref[:, lanes] = jnp.where(here == row, 1.0, 0.0).astype(BF16)
                dist = jnp.abs(angle - knots)
                dist = jnp.minimum(dist, ANG - dist)
                outer = jnp.maximum(2.0 - dist, 0.0)
                inner = jnp.maximum(1.0 - dist, 0.0)
                weight = outer * outer * outer - 4.0 * (inner * inner * inner)
                piece_ref[:, lanes] = jnp.concatenate(halves(value * weight), axis=0)
                at += 128
    total = lax.dot_general(
        piece_ref[...], pick_ref[...], (((1,), (1,)), ((), ())), preferred_element_type=F32
    )
    total = (total[:ANG] + total[ANG : 2 * ANG] + total[2 * ANG :]).T
    out_ref[...] = total + prior[0][...] if prior else total


def dense(block, slots, prior=()):
    count = sum(s.shape[0] // 3 * s.shape[1] * 128 for s in slots)

    def body(*refs):
        dense_body(block, len(slots), len(prior), refs)

    return call(
        body,
        shape((block, ANG)),
        (*slots, *prior),
        [VM] * (len(slots) + len(prior)),
        [pltpu.VMEM((block, count), BF16), pltpu.VMEM((3 * ANG, count), BF16)],
    )


def share_and_add(slots, axis, block):
    count = lax.axis_size(axis)
    have = slots
    total = None
    for k in range(count.bit_length() - 1):
        got = lax.ppermute(have, axis, [(i, i ^ (1 << k)) for i in range(count)])
        if 2 << k < count:
            have = jnp.concatenate([have, got], axis=0)
        else:
            total = dense(block, (have,))
            total = dense(block, (got,), (total,))
    return dense(block, (have,)) if total is None else total


def halve(total, axis):
    count = lax.axis_size(axis)
    me = lax.axis_index(axis)
    step = count // 2
    while step > 0:
        half = total.shape[0] // 2
        bit = lax.rem(me // step, 2)
        sent = lax.dynamic_slice_in_dim(total, (1 - bit) * half, half, axis=0)
        kept = lax.dynamic_slice_in_dim(total, bit * half, half, axis=0)
        total = kept + lax.ppermute(sent, axis, [(i, i ^ step) for i in range(count)])
        step //= 2
    return total


def rounds_of(axis):
    return [(axis, first) for first in (0, 1) if swap_pairs(lax.axis_size(axis), first)]


def swap_all(rounds, messages):
    got = []
    for (axis, first), message in zip(rounds, messages):
        got.append(swap(axis, first, message))
    return got


def step_back(
    pressure,
    velocity,
    kappa,
    drive,
    adj_pressure_in,
    adj_velocity_in,
    wall_mask,
    wall_cells,
    wall_rows,
    slot_angle,
    wall_count,
    step,
):
    grid = depth, height, width = pressure.shape
    slots = wall_cells.size
    flat = (1, slots)
    sems = pltpu.SemaphoreType.DMA
    phase = jnp.cos(0.5 * (step % 97).astype(F32))
    slab_rounds, row_rounds, col_rounds = (rounds_of(a) for a in ("slab", "row", "col"))
    side_rounds = row_rounds + col_rounds
    counts = (len(slab_rounds), len(row_rounds), len(col_rounds))

    *faces, p_in, q_in, a_in = call(
        lambda *refs: faces_body(slab_rounds, refs),
        [shape((2, height, width))] * counts[0] + [shape(grid)] * 3,
        (pressure, kappa, adj_pressure_in),
        [HB] * 3,
        [pltpu.VMEM(grid, F32), sems((3,))],
    )
    slab_got = swap_all(slab_rounds, faces)
    *messages, t_in, free = call(
        lambda *refs: sides_body(side_rounds, refs),
        [shape((4, depth, width if axis == "row" else height)) for axis, _ in side_rounds]
        + [shape((3, *grid)), shape(grid)],
        (p_in, q_in, adj_velocity_in, wall_mask),
        [VM] * 2 + [HB] * 2,
        [pltpu.VMEM(grid, jnp.int32), sems((2,))],
    )
    side_got = swap_all(side_rounds, messages)
    total, moved, picks, cells = call(
        inner_body,
        [
            shape((3, *grid)),
            shape((3, *grid)),
            shape((depth * height, slots), BF16),
            shape((1, 1, slots), jnp.int32),
        ],
        (
            p_in,
            q_in,
            t_in,
            velocity,
            drive,
            wall_cells.reshape(flat),
            wall_rows.reshape(flat),
            slot_angle.reshape(flat),
            phase,
        ),
        [VM] * 3 + [HB] * 5 + [SM],
        [pltpu.VMEM((3, *grid), F32), pltpu.VMEM(grid, F32), sems((3,))],
    )
    lam, mine, *lam_faces = call(
        lambda *refs: main_body(counts, refs),
        [shape((3, *grid)), shape((3, slots // 128, 128))] + [shape((height, width))] * counts[0],
        (
            total,
            moved,
            free,
            picks,
            cells.reshape(flat),
            wall_rows.reshape(flat),
            slot_angle.reshape(flat),
            wall_count.reshape(1),
            *slab_got,
            *side_got,
        ),
        [VM] * 7 + [SM] + [VM] * sum(counts),
        [pltpu.VMEM((depth * height, width), F32)],
    )
    lam_got = swap_all(slab_rounds, lam_faces)
    part, adj_velocity = call(
        lambda *refs: part_body(counts, refs),
        [shape(grid), shape((3, *grid))],
        (lam, q_in, a_in, *side_got),
        [VM] * (3 + counts[1] + counts[2]),
        [sems((1,))],
        [VM, HB],
    )
    adj_pressure = call(
        lambda *refs: fix_body(refs),
        shape(grid),
        (part, *lam_got),
        [VM] * (1 + counts[0]),
    )
    total = share_and_add(mine, "slab", NROWS // lax.axis_size("slab"))
    total = halve(halve(total, "row"), "col")
    return (adj_pressure, adj_velocity, total)


def solution(mesh):
    in_specs = (
        P("slab", "row", "col"),
        P(None, "slab", "row", "col"),
        P("slab", "row", "col"),
        P("slab", "row", "col"),
        P("slab", "row", "col"),
        P(None, "slab", "row", "col"),
        P("slab", "row", "col"),
        P("slab", "row", "col", None),
        P("slab", "row", "col", None),
        P("slab", "row", "col", None),
        P("slab", "row", "col"),
        P(),
    )
    out_specs = (
        P("slab", "row", "col"),
        P(None, "slab", "row", "col"),
        P(("slab", "row", "col"), None),
    )
    return jax.shard_map(step_back, mesh=mesh, in_specs=in_specs, out_specs=out_specs, check_vma=False)
```

time: 42.7 us -> 39.2 us (0.918)
  Pallas kernels: 7.33 us -> 6.23 us
  local copies, waits for them, and re-layouts: 5.67 us -> 4.58 us
  waiting for transfers between devices: 11.7 us -> 10.7 us
    ppermute x6, waiting for transfers between devices: 4.45 us -> 3.05 us  [swap(): return lax.ppermute(message, axis, swap_pairs(lax.axis_size(axis), first))]
    pallas_call x6 -> x8, Pallas kernels: 7.33 us -> 6.23 us  [call(): pl.pallas_call(body, out_shape=outs, in_specs=specs, out_specs=jax.tree.m...]
    unnamed x28 -> x22, local copies, waits for them, and re-layouts: 5.64 us -> 4.54 us
    ppermute x2, starting transfers between devices: 1.63 us -> 0.97 us  [halve(): lax.ppermute(sent, axis, [(i, i ^ step) for i in range(count)])]
  transfers between devices with their start and end apart: 11 -> 11, of which waited for: 6 -> 4; matrix products, arithmetic and copies ran while one was open for 0% -> 0% of each run, Pallas kernels for 9% -> 11%
where the time goes in v2:
time: 39.2 us; the launch traced here: 38.9 us
  starting transfers between devices  14.5 us (37%)
  waiting for transfers between devices  10.7 us (27%)
  Pallas kernels  6.23 us (16%)
  local copies, waits for them, and re-layouts  4.58 us (12%)
  between operations  2.29 us (6%)
  other arithmetic  0.64 us (2%)
    ppermute x6, starting transfers between devices, swap(): return lax.ppermute(message, axis, swap_pairs(lax.axis_size(axis), first))  9.5 us
    ppermute x3, waiting for transfers between devices, share_and_add(): got = lax.ppermute(have, axis, [(i, i ^ 1 << k) for i in range(count)])  7.65 us
    pallas_call x8, Pallas kernels, call(): pl.pallas_call(body, out_shape=outs, in_specs=specs, out_specs=jax.tree.m...  6.23 us
    unnamed x22, local copies, waits for them, and re-layouts  4.54 us
    ppermute x3, starting transfers between devices, share_and_add(): got = lax.ppermute(have, axis, [(i, i ^ 1 << k) for i in range(count)])  3.99 us
    ppermute x6, waiting for transfers between devices, swap(): return lax.ppermute(message, axis, swap_pairs(lax.axis_size(axis), first))  3.05 us
    ppermute x2, starting transfers between devices, halve(): lax.ppermute(sent, axis, [(i, i ^ step) for i in range(count)])  0.97 us
  transfers between devices with their start and end apart: 11, of which 4 were waited for; matrix products, arithmetic and copies ran while one was open for 0% of the time, Pallas kernels for 11%

profile of v2, /device:TPU:16, one launch (start us, length us, event | category | flops | bytes accessed | tf_op | source)
XLA Modules:
  0.0 38.9 jit_solution(18049057521506548517)
XLA Ops:
  0.6 0.0 copy-start
  0.6 0.0 copy-start.2
  0.7 1.0 %copy-done.2 = f32[4,128,128]{2,1,0:T(8,128)S(1)} copy-done((f32[4,128,128]{2,1,0:T(8,128)S(1)}, f32[4,128,128]{2,1,0:T(8,128)}, u32[]{:S(2)}) %copy-start.2) | copy-done | bytes 262168
  1.7 0.0 copy-start.3
  1.7 0.9 %copy-done.3 = f32[4,128,128]{2,1,0:T(8,128)S(1)} copy-done((f32[4,128,128]{2,1,0:T(8,128)S(1)}, f32[4,128,128]{2,1,0:T(8,128)}, u32[]{:S(2)}) %copy-start.3) | copy-done | bytes 262168
  2.6 0.9 %copy-done.4 = f32[4,128,128]{2,1,0:T(8,128)S(1)} copy-done((f32[4,128,128]{2,1,0:T(8,128)S(1)}, f32[4,128,128]{2,1,0:T(8,128)}, u32[]{:S(2)}) %copy-start.4) | copy-done | bytes 262168
  3.6 0.1 shard_map.139
  3.7 1.6 %collective-permute-start = (f32[2,128,128]{2,1,0:T(8,128)S(1)}, f32[2,128,128]{2,1,0:T(8,128)S(1)}, u32[]{:S(2)}, u32[]{:S(2)}) collective-permute-start(f32[2,128,128]{2,1,0:T(8,128)S(1)} %get-tuple-element.30), channel_id=1, source_target_pairs={{0,4},{4,0},{8,12},{12,8},{16,20},{20,16},{24,28},{28,24},{1,5},{5... | collective-permute-start | bytes 393224 | tf_op jit(solution)/shard_map/ppermute | solution.py:54
  5.3 2.3 %collective-permute-start.1 = (f32[2,128,128]{2,1,0:T(8,128)S(1)}, f32[2,128,128]{2,1,0:T(8,128)S(1)}, u32[]{:S(2)}, u32[]{:S(2)}) collective-permute-start(f32[2,128,128]{2,1,0:T(8,128)S(1)} %get-tuple-element.31), channel_id=1, source_target_pairs={{4,8},{8,4},{12,16},{16,12},{20,24},{24,20},{5,9},{9,5},{13,17},{1... | collective-permute-start | bytes 393224 | tf_op jit(solution)/shard_map/ppermute | solution.py:54
  7.6 0.0 copy-done
  7.6 0.0 copy-start.6
  7.6 0.9 %copy-done.6 = s32[4,128,128]{2,1,0:T(8,128)S(1)} copy-done((s32[4,128,128]{2,1,0:T(8,128)S(1)}, s32[4,128,128]{2,1,0:T(8,128)}, u32[]{:S(2)}) %copy-start.6) | copy-done | bytes 262168
  8.6 0.6 %shard_map.140 = (f32[4,4,128]{2,1,0:T(4,128)S(1)}, f32[4,4,128]{2,1,0:T(4,128)S(1)}, f32[3,4,128,128]{3,2,1,0:T(8,128)S(1)}, f32[4,128,128]{2,1,0:T(8,128)S(1)}) custom-call(f32[4,128,128]{2,1,0:T(8,128)S(1)} %get-tuple-element.22.refs_0_.pv_ref, f32[4,128,128]{2,1,0:T(8,128)S(1)} %get-tuple-element.23.refs_1_.qv_ref, f32[3,4,128,128]{3,2,1,0:T(8,128)S(1)} %copy-done, ...), custom_call_target="tpu_custom_call" | custom-call | flops 1000000 | bytes 1000000 | tf_op jit(solution)/shard_map/pallas_call | solution.py:20
  9.2 0.1 collective-permute-start.2
  9.3 0.0 copy-start.9
  9.3 1.6 %collective-permute-start.3 = (f32[4,4,128]{2,1,0:T(4,128)S(1)}, f32[4,4,128]{2,1,0:T(4,128)S(1)}, u32[]{:S(2)}, u32[]{:S(2)}) collective-permute-start(f32[4,4,128]{2,1,0:T(4,128)S(1)} %get-tuple-element.33), channel_id=1, source_target_pairs={{0,1},{1,0},{2,3},{3,2},{4,5},{5,4},{6,7},{7,6},{8,9},{9,8},{10,11... | collective-permute-start | bytes 24584 | tf_op jit(solution)/shard_map/ppermute | solution.py:54
  12.2 0.0 copy-start.8
  12.3 0.0 copy-start.7
  12.3 0.0 copy-done.1
  12.3 0.0 copy-done.5
  12.3 0.0 copy-done.9
  12.3 0.6 %copy-done.8 = f32[1,1,1,512]{3,2,1,0:T(1,128)S(1)} copy-done((f32[1,1,1,512]{3,2,1,0:T(1,128)S(1)}, f32[1,1,1,512]{3,2,1,0:T(1,128)}, u32[]{:S(2)}) %copy-start.8) | copy-done | bytes 2072
  12.9 0.0 copy-done.7
  12.9 0.7 %shard_map.141 = (f32[3,4,128,128]{3,2,1,0:T(8,128)S(1)}, f32[3,4,128,128]{3,2,1,0:T(8,128)S(1)}, bf16[512,512]{1,0:T(8,128)(2,1)S(1)}, s32[1,1,512]{2,1,0:T(1,128)S(1)}) custom-call(f32[4,128,128]{2,1,0:T(8,128)S(1)} %get-tuple-element.22.refs_0_.pv_ref, f32[4,128,128]{2,1,0:T(8,128)S(1)} %get-tuple-element.23.refs_1_.qv_ref, ...), custom_call_target="tpu_custom_call" | custom-call | flops 1000000 | bytes 1000000 | tf_op jit(solution)/shard_map/pallas_call | solution.py:20
  13.6 0.0 collective-permute-done.2.refs_10_.refs_3_
  13.6 0.0 collective-permute-done.3.refs_11_.refs_4_
  13.6 0.0 collective-permute-done.refs_8_
  13.7 0.0 collective-permute-done.1.refs_9_
  13.7 0.8 %shard_map.142 = (f32[3,4,128,128]{3,2,1,0:T(8,128)S(1)}, f32[3,4,128]{2,1,0:T(4,128)S(1)}, f32[128,128]{1,0:T(8,128)S(1)}, f32[128,128]{1,0:T(8,128)S(1)}) custom-call(f32[3,4,128,128]{3,2,1,0:T(8,128)S(1)} %get-tuple-element.25.refs_0_, f32[3,4,128,128]{3,2,1,0:T(8,128)S(1)} %get-tuple-element.26.refs_1_, f32[4,128,128]{2,1,0:T(8,128)S(1)} %get-tuple-element.27.refs_2_, ...), custom_call_target="tpu_custom_call" | custom-call | flops 1000000 | bytes 1000000 | tf_op jit(solution)/shard_map/pallas_call | solution.py:20
  14.4 2.7 %collective-permute-start.6 = (f32[3,4,128]{2,1,0:T(4,128)S(1)}, f32[3,4,128]{2,1,0:T(4,128)S(1)}, u32[]{:S(2)}, u32[]{:S(2)}) collective-permute-start(f32[3,4,128]{2,1,0:T(4,128)S(1)} %get-tuple-element.40), channel_id=1, source_target_pairs={{0,4},{4,0},{8,12},{12,8},{16,20},{20,16},{24,28},{28,24},{1,5},{5... | collective-permute-start | bytes 18440 | tf_op jit(solution)/shard_map/ppermute | solution.py:345
  17.1 1.6 %collective-permute-done.6 = f32[3,4,128]{2,1,0:T(4,128)S(1)} collective-permute-done((f32[3,4,128]{2,1,0:T(4,128)S(1)}, f32[3,4,128]{2,1,0:T(4,128)S(1)}, u32[]{:S(2)}, u32[]{:S(2)}) %collective-permute-start.6) | collective-permute-done | bytes 6176 | tf_op jit(solution)/shard_map/ppermute | solution.py:345
  18.8 0.9 %collective-permute-start.7 = (f32[6,4,128]{2,1,0:T(4,128)S(1)}, f32[6,4,128]{2,1,0:T(4,128)S(1)}, u32[]{:S(2)}, u32[]{:S(2)}) collective-permute-start(f32[6,4,128]{2,1,0:T(4,128)S(1)} %pad_maximum_fusion), channel_id=1, source_target_pairs={{0,8},{4,12},{8,0},{12,4},{16,24},{20,28},{24,16},{28,20},{1,9},{5... | collective-permute-start | bytes 36872 | tf_op jit(solution)/shard_map/ppermute | solution.py:345
  19.7 2.7 %collective-permute-done.7 = f32[6,4,128]{2,1,0:T(4,128)S(1)} collective-permute-done((f32[6,4,128]{2,1,0:T(4,128)S(1)}, f32[6,4,128]{2,1,0:T(4,128)S(1)}, u32[]{:S(2)}, u32[]{:S(2)}) %collective-permute-start.7) | collective-permute-done | bytes 12320 | tf_op jit(solution)/shard_map/ppermute | solution.py:345
  22.5 0.3 collective-permute-start.8
  22.8 1.1 %shard_map.145.refs_1_ = f32[256,64]{1,0:T(8,128)S(1)} custom-call(f32[12,4,128]{2,1,0:T(4,128)S(1)} %constant_dynamic-update-slice_fusion.refs_0_), custom_call_target="tpu_custom_call" | custom-call | flops 1000000 | bytes 1000000 | tf_op jit(solution)/shard_map/pallas_call | solution.py:20
  23.9 3.3 %collective-permute-done.8.refs_0_ = f32[12,4,128]{2,1,0:T(4,128)S(1)} collective-permute-done((f32[12,4,128]{2,1,0:T(4,128)S(1)}, f32[12,4,128]{2,1,0:T(4,128)S(1)}, u32[]{:S(2)}, u32[]{:S(2)}) %collective-permute-start.8) | collective-permute-done | bytes 24608 | tf_op jit(solution)/shard_map/ppermute | solution.py:345
  27.2 1.1 %shard_map.146 = f32[256,64]{1,0:T(8,128)S(1)} custom-call(f32[12,4,128]{2,1,0:T(4,128)S(1)} %collective-permute-done.8.refs_0_, f32[256,64]{1,0:T(8,128)S(1)} %shard_map.145.refs_1_), custom_call_target="tpu_custom_call" | custom-call | flops 1000000 | bytes 1000000 | tf_op jit(solution)/shard_map/pallas_call | solution.py:20
  28.3 0.1 collective-permute-start.9
  28.4 2.1 %collective-permute-start.4 = (f32[128,128]{1,0:T(8,128)S(1)}, f32[128,128]{1,0:T(8,128)S(1)}, u32[]{:S(2)}, u32[]{:S(2)}) collective-permute-start(f32[128,128]{1,0:T(8,128)S(1)} %get-tuple-element.37), channel_id=1, source_target_pairs={{0,4},{4,0},{8,12},{12,8},{16,20},{20,16},{24,28},{28,24},{1,5},{5... | collective-permute-start | bytes 196616 | tf_op jit(solution)/shard_map/ppermute | solution.py:54
  30.5 1.9 %collective-permute-start.5 = (f32[128,128]{1,0:T(8,128)S(1)}, f32[128,128]{1,0:T(8,128)S(1)}, u32[]{:S(2)}, u32[]{:S(2)}) collective-permute-start(f32[128,128]{1,0:T(8,128)S(1)} %get-tuple-element.38), channel_id=1, source_target_pairs={{4,8},{8,4},{12,16},{16,12},{20,24},{24,20},{5,9},{9,5},{13,17},{1... | collective-permute-start | bytes 196616 | tf_op jit(solution)/shard_map/ppermute | solution.py:54
  32.4 0.0 collective-permute-done.9
  32.5 0.9 %collective-permute-start.10 = (f32[64,64]{1,0:T(8,128)S(1)}, f32[64,64]{1,0:T(8,128)S(1)}, u32[]{:S(2)}, u32[]{:S(2)}) collective-permute-start(f32[64,64]{1,0:T(8,128)S(1)} %constant_dynamic-slice_fusion), channel_id=1, source_target_pairs={{0,1},{1,0},{2,3},{3,2},{4,5},{5,4},{6,7},{7,6},{8,9},{9,8},{10,11... | collective-permute-start | bytes 49160 | tf_op jit(solution)/shard_map/ppermute | solution.py:363
  33.4 1.1 %shard_map.143 = (f32[4,128,128]{2,1,0:T(8,128)S(1)}, f32[3,4,128,128]{3,2,1,0:T(8,128)}) custom-call(f32[3,4,128,128]{3,2,1,0:T(8,128)S(1)} %get-tuple-element.34.refs_0_, f32[4,128,128]{2,1,0:T(8,128)S(1)} %get-tuple-element.23.refs_1_.qv_ref, f32[4,128,128]{2,1,0:T(8,128)S(1)} %get-tuple-element.35.refs_2_, ...), custom_call_target="tpu_custom_call" | custom-call | flops 1000000 | bytes 1000000 | tf_op jit(solution)/shard_map/pallas_call | solution.py:20
  34.5 0.0 collective-permute-done.4.refs_1_
  34.5 3.0 %collective-permute-done.5.refs_2_ = f32[128,128]{1,0:T(8,128)S(1)} collective-permute-done((f32[128,128]{1,0:T(8,128)S(1)}, f32[128,128]{1,0:T(8,128)S(1)}, u32[]{:S(2)}, u32[]{:S(2)}) %collective-permute-start.5) | collective-permute-done | bytes 65568 | tf_op jit(solution)/shard_map/ppermute | solution.py:54
  37.5 0.7 %shard_map.144 = f32[4,128,128]{2,1,0:T(8,128)} custom-call(f32[4,128,128]{2,1,0:T(8,128)S(1)} %get-tuple-element.36.refs_0_, f32[128,128]{1,0:T(8,128)S(1)} %collective-permute-done.4.refs_1_, f32[128,128]{1,0:T(8,128)S(1)} %collective-permute-done.5.refs_2_), custom_call_target="tpu_custom_call" | custom-call | flops 1000000 | bytes 1000000 | tf_op jit(solution)/shard_map/pallas_call | solution.py:20
  38.3 0.0 collective-permute-done.10
  38.3 0.6 %dynamic-slice_add_fusion.1 = f32[64,64]{1,0:T(8,128)} fusion(f32[64,64]{1,0:T(8,128)S(1)} %collective-permute-done.10, f32[128,64]{1,0:T(8,128)S(1)} %dynamic-slice_add_fusion, s32[]{:T(128)S(6)} %select_n.25), kind=kLoop, calls=%fused_computation.1 | loop fusion | flops 4096 | bytes 49156 | tf_op jit(solution)/shard_map/add | solution.py:363
  (10 shorter events, 0.1 us)
Async XLA Ops:
  0.6 7.0 %copy-start = (f32[3,4,128,128]{3,2,1,0:T(8,128)S(1)}, f32[3,4,128,128]{3,2,1,0:T(8,128)}, u32[]{:S(2)}) copy-start(f32[3,4,128,128]{3,2,1,0:T(8,128)} %refs_2_.3) | copy-start | bytes 2359300
  0.6 1.0 %copy-start.2 = (f32[4,128,128]{2,1,0:T(8,128)S(1)}, f32[4,128,128]{2,1,0:T(8,128)}, u32[]{:S(2)}) copy-start(f32[4,128,128]{2,1,0:T(8,128)} %refs_0_.1) | copy-start | bytes 786436
  1.7 0.9 %copy-start.3 = (f32[4,128,128]{2,1,0:T(8,128)S(1)}, f32[4,128,128]{2,1,0:T(8,128)}, u32[]{:S(2)}) copy-start(f32[4,128,128]{2,1,0:T(8,128)} %refs_1_.1) | copy-start | bytes 786436
  2.6 0.9 %copy-start.4 = (f32[4,128,128]{2,1,0:T(8,128)S(1)}, f32[4,128,128]{2,1,0:T(8,128)}, u32[]{:S(2)}) copy-start(f32[4,128,128]{2,1,0:T(8,128)} %refs_2_.2) | copy-start | bytes 786436
  3.7 9.9 %collective-permute-start = (f32[2,128,128]{2,1,0:T(8,128)S(1)}, f32[2,128,128]{2,1,0:T(8,128)S(1)}, u32[]{:S(2)}, u32[]{:S(2)}) collective-permute-start(f32[2,128,128]{2,1,0:T(8,128)S(1)} %get-tuple-element.30), channel_id=1, source_target_pairs={{0,4},{4,0},{8,12},{12,8},{16,20},{20,16},{24,28},{28,24},{1,5},{5... | collective-permute-start | bytes 393224 | tf_op jit(solution)/shard_map/ppermute | solution.py:54
  5.3 8.4 %collective-permute-start.1 = (f32[2,128,128]{2,1,0:T(8,128)S(1)}, f32[2,128,128]{2,1,0:T(8,128)S(1)}, u32[]{:S(2)}, u32[]{:S(2)}) collective-permute-start(f32[2,128,128]{2,1,0:T(8,128)S(1)} %get-tuple-element.31), channel_id=1, source_target_pairs={{4,8},{8,4},{12,16},{16,12},{20,24},{24,20},{5,9},{9,5},{13,17},{1... | collective-permute-start | bytes 393224 | tf_op jit(solution)/shard_map/ppermute | solution.py:54
  7.6 1.0 %copy-start.6 = (s32[4,128,128]{2,1,0:T(8,128)S(1)}, s32[4,128,128]{2,1,0:T(8,128)}, u32[]{:S(2)}) copy-start(s32[4,128,128]{2,1,0:T(8,128)} %refs_3_.1) | copy-start | bytes 786436
  8.6 3.7 %copy-start.1 = (f32[3,4,128,128]{3,2,1,0:T(8,128)S(1)}, f32[3,4,128,128]{3,2,1,0:T(8,128)}, u32[]{:S(2)}) copy-start(f32[3,4,128,128]{3,2,1,0:T(8,128)} %v_ref.1) | copy-start | bytes 2359300
  8.6 3.7 %copy-start.5 = (f32[4,128,128]{2,1,0:T(8,128)S(1)}, f32[4,128,128]{2,1,0:T(8,128)}, u32[]{:S(2)}) copy-start(f32[4,128,128]{2,1,0:T(8,128)} %d_ref.1) | copy-start | bytes 786436
  9.2 4.4 %collective-permute-start.2 = (f32[4,4,128]{2,1,0:T(4,128)S(1)}, f32[4,4,128]{2,1,0:T(4,128)S(1)}, u32[]{:S(2)}, u32[]{:S(2)}) collective-permute-start(f32[4,4,128]{2,1,0:T(4,128)S(1)} %get-tuple-element.32), channel_id=1, source_target_pairs={{0,2},{2,0},{1,3},{3,1},{4,6},{6,4},{5,7},{7,5},{8,10},{10,8},{9,1... | collective-permute-start | bytes 24584 | tf_op jit(solution)/shard_map/ppermute | solution.py:54
  9.3 3.0 %copy-start.9 = (s32[1,1,1,512]{3,2,1,0:T(1,128)S(1)}, s32[1,1,1,512]{3,2,1,0:T(1,128)}, u32[]{:S(2)}) copy-start(s32[1,1,1,512]{3,2,1,0:T(1,128)} %param.19) | copy-start | bytes 6148
  9.3 4.3 %collective-permute-start.3 = (f32[4,4,128]{2,1,0:T(4,128)S(1)}, f32[4,4,128]{2,1,0:T(4,128)S(1)}, u32[]{:S(2)}, u32[]{:S(2)}) collective-permute-start(f32[4,4,128]{2,1,0:T(4,128)S(1)} %get-tuple-element.33), channel_id=1, source_target_pairs={{0,1},{1,0},{2,3},{3,2},{4,5},{5,4},{6,7},{7,6},{8,9},{9,8},{10,11... | collective-permute-start | bytes 24584 | tf_op jit(solution)/shard_map/ppermute | solution.py:54
  12.2 0.7 %copy-start.8 = (f32[1,1,1,512]{3,2,1,0:T(1,128)S(1)}, f32[1,1,1,512]{3,2,1,0:T(1,128)}, u32[]{:S(2)}) copy-start(f32[1,1,1,512]{3,2,1,0:T(1,128)} %param.21) | copy-start | bytes 6148
  12.3 0.7 %copy-start.7 = (s32[1,1,1,512]{3,2,1,0:T(1,128)S(1)}, s32[1,1,1,512]{3,2,1,0:T(1,128)}, u32[]{:S(2)}) copy-start(s32[1,1,1,512]{3,2,1,0:T(1,128)} %param.20) | copy-start | bytes 6148
  14.4 4.3 %collective-permute-start.6 = (f32[3,4,128]{2,1,0:T(4,128)S(1)}, f32[3,4,128]{2,1,0:T(4,128)S(1)}, u32[]{:S(2)}, u32[]{:S(2)}) collective-permute-start(f32[3,4,128]{2,1,0:T(4,128)S(1)} %get-tuple-element.40), channel_id=1, source_target_pairs={{0,4},{4,0},{8,12},{12,8},{16,20},{20,16},{24,28},{28,24},{1,5},{5... | collective-permute-start | bytes 18440 | tf_op jit(solution)/shard_map/ppermute | solution.py:345
  18.8 3.7 %collective-permute-start.7 = (f32[6,4,128]{2,1,0:T(4,128)S(1)}, f32[6,4,128]{2,1,0:T(4,128)S(1)}, u32[]{:S(2)}, u32[]{:S(2)}) collective-permute-start(f32[6,4,128]{2,1,0:T(4,128)S(1)} %pad_maximum_fusion), channel_id=1, source_target_pairs={{0,8},{4,12},{8,0},{12,4},{16,24},{20,28},{24,16},{28,20},{1,9},{5... | collective-permute-start | bytes 36872 | tf_op jit(solution)/shard_map/ppermute | solution.py:345
  22.5 4.7 %collective-permute-start.8 = (f32[12,4,128]{2,1,0:T(4,128)S(1)}, f32[12,4,128]{2,1,0:T(4,128)S(1)}, u32[]{:S(2)}, u32[]{:S(2)}) collective-permute-start(f32[12,4,128]{2,1,0:T(4,128)S(1)} %constant_dynamic-update-slice_fusion.refs_0_), channel_id=1, source_target_pairs={{0,16},{4,20},{8,24},{12,28},{16,0},{20,4},{24,8},{28,12},{1,17},{... | collective-permute-start | bytes 73736 | tf_op jit(solution)/shard_map/ppermute | solution.py:345
  28.3 4.1 %collective-permute-start.9 = (f32[128,64]{1,0:T(8,128)S(1)}, f32[128,64]{1,0:T(8,128)S(1)}, u32[]{:S(2)}, u32[]{:S(2)}) collective-permute-start(f32[128,64]{1,0:T(8,128)S(1)} %constant_dynamic-slice_fusion.1), channel_id=1, source_target_pairs={{0,2},{2,0},{1,3},{3,1},{4,6},{6,4},{5,7},{7,5},{8,10},{10,8},{9,1... | collective-permute-start | bytes 98312 | tf_op jit(solution)/shard_map/ppermute | solution.py:363
  28.4 6.1 %collective-permute-start.4 = (f32[128,128]{1,0:T(8,128)S(1)}, f32[128,128]{1,0:T(8,128)S(1)}, u32[]{:S(2)}, u32[]{:S(2)}) collective-permute-start(f32[128,128]{1,0:T(8,128)S(1)} %get-tuple-element.37), channel_id=1, source_target_pairs={{0,4},{4,0},{8,12},{12,8},{16,20},{20,16},{24,28},{28,24},{1,5},{5... | collective-permute-start | bytes 196616 | tf_op jit(solution)/shard_map/ppermute | solution.py:54
  30.5 7.0 %collective-permute-start.5 = (f32[128,128]{1,0:T(8,128)S(1)}, f32[128,128]{1,0:T(8,128)S(1)}, u32[]{:S(2)}, u32[]{:S(2)}) collective-permute-start(f32[128,128]{1,0:T(8,128)S(1)} %get-tuple-element.38), channel_id=1, source_target_pairs={{4,8},{8,4},{12,16},{16,12},{20,24},{24,20},{5,9},{9,5},{13,17},{1... | collective-permute-start | bytes 196616 | tf_op jit(solution)/shard_map/ppermute | solution.py:54
  32.5 5.8 %collective-permute-start.10 = (f32[64,64]{1,0:T(8,128)S(1)}, f32[64,64]{1,0:T(8,128)S(1)}, u32[]{:S(2)}, u32[]{:S(2)}) collective-permute-start(f32[64,64]{1,0:T(8,128)S(1)} %constant_dynamic-slice_fusion), channel_id=1, source_target_pairs={{0,1},{1,0},{2,3},{3,2},{4,5},{5,4},{6,7},{7,6},{8,9},{9,8},{10,11... | collective-permute-start | bytes 49160 | tf_op jit(solution)/shard_map/ppermute | solution.py:363

commit v3 on v2

--- a/solution.py
+++ b/solution.py
@@ -1,3 +1,5 @@
+import functools
+
 import jax
 import jax.numpy as jnp
 from jax import lax
@@ -12,7 +14,7 @@
 BF16 = jnp.bfloat16
 VM = pl.BlockSpec(memory_space=pltpu.VMEM)
 HB = pl.BlockSpec(memory_space=pltpu.HBM)
-SM = pl.BlockSpec(memory_space=pltpu.SMEM)
+ANY = pl.BlockSpec(memory_space=pl.ANY)
 LIMIT = pltpu.CompilerParams(vmem_limit_bytes=24 << 20)
 
 
@@ -26,6 +28,10 @@
         compiler_params=LIMIT,
         cost_estimate=pl.CostEstimate(flops=1_000_000, bytes_accessed=1_000_000, transcendentals=0),
     )(*args)
+
+
+def stay(array):
+    return pltpu.with_memory_space_constraint(array, pltpu.HBM)
 
 
 def fetch(pairs, sems):
@@ -133,12 +139,17 @@
     return top, mid, (rest - mid.astype(F32)).astype(BF16)
 
 
-def inner_body(pv_ref, qv_ref, tv_ref, v_ref, d_ref, c_ref, r_ref, g_ref, ph_ref,
-               total_ref, moved_ref, pick_ref, slot_in_ref, vv_ref, dv_ref, sems):
+def inner_body(pv_ref, qv_ref, tv_ref, v_ref, d_ref, c_ref, r_ref, g_ref, n_ref, s_ref,
+               total_ref, moved_ref, pick_ref, cell_ref, row_ref, angle_ref, live_ref,
+               vv_ref, dv_ref, count_ref, step_ref, sems):
     depth, _, width = pv_ref.shape
     copies = fetch(
         (
-            (c_ref, slot_in_ref.at[0]),
+            (s_ref, step_ref),
+            (n_ref, count_ref),
+            (c_ref, cell_ref),
+            (r_ref, row_ref),
+            (g_ref, angle_ref),
             (v_ref, vv_ref),
             (d_ref, dv_ref),
         ),
@@ -151,14 +162,17 @@
         total_ref[0, x] = tv_ref[0, x] + (upper - lower) * 0.5
         total_ref[1, x] = tv_ref[1, x] + side(q, 0, 0.0, 0.0)
         total_ref[2, x] = tv_ref[2, x] + side(q, 1, 0.0, 0.0)
-    copies[0].wait()
-    cells = slot_in_ref[0]
-    line = lax.div(cells, width)
+    for copy in copies[:5]:
+        copy.wait()
+    line = lax.div(cell_ref[...], width)
     at = lax.broadcasted_iota(jnp.int32, pick_ref.shape, 0)
     pick_ref[...] = jnp.where(at == line, 1.0, 0.0).astype(BF16)
-    copies[1].wait()
-    copies[2].wait()
-    phase = ph_ref[0]
+    slot = lax.broadcasted_iota(jnp.int32, live_ref.shape, 1)
+    live_ref[...] = jnp.where(slot < count_ref[0], 1, 0)
+    turn = lax.rem(step_ref[0], 97).astype(F32) * 0.5
+    phase = jnp.cos(jnp.full((8, width), turn, F32))[:1]
+    copies[5].wait()
+    copies[6].wait()
     for x in range(depth):
         p = pv_ref[x]
         upper = pv_ref[x + 1] if x + 1 < depth else 0.0
@@ -179,7 +193,7 @@
 
 
 def main_body(counts, refs):
-    total_ref, moved_ref, free_ref, pick_ref, cell_ref, row_ref, angle_ref, n_ref = refs[:8]
+    total_ref, moved_ref, free_ref, pick_ref, cell_ref, row_ref, angle_ref, live_ref = refs[:8]
     rest = refs[8:]
     n_slab, n_row, n_col = counts
     slab_refs, rest = rest[:n_slab], rest[n_slab:]
@@ -233,8 +247,7 @@
     found = found[:width] + found[width : 2 * width] + found[2 * width :]
     lane = lax.broadcasted_iota(jnp.int32, (width, slots), 0)
     values = jnp.sum(jnp.where(lane == lax.rem(cells, width), found, 0.0), axis=0, keepdims=True)
-    live = lax.broadcasted_iota(jnp.int32, (1, slots), 1) < n_ref[0]
-    values = jnp.where(live, values, 0.0)
+    values = jnp.where(live_ref[...] == 1, values, 0.0)
     rows = row_ref[...].astype(F32)
     angles = angle_ref[...]
     for j in range(slots // 128):
@@ -292,10 +305,33 @@
         out_ref[x] = value
 
 
-def dense_body(block, n_slots, n_prior, refs):
+def pack(rows):
+    half = rows.shape[0] // 2
+    return jnp.concatenate([rows[:half], rows[half:]], axis=1)
+
+
+def high_side(axis, step):
+    return lax.rem(lax.div(lax.axis_index(axis), step), 2) == 1
+
+
+def split(low, high, mine_high, kept_ref, sent_ref):
+    kept_ref[...] = pack(jnp.where(mine_high, high, low))
+    sent_ref[...] = pack(jnp.where(mine_high, low, high))
+
+
+def add_body(parts, kept_ref, got_ref, *out_refs):
+    total = kept_ref[...] + got_ref[...]
+    low, high = total[:, :ANG], total[:, ANG:]
+    if parts is None:
+        out_refs[0][...] = jnp.concatenate([low, high], axis=0)
+    else:
+        split(low, high, high_side(*parts), *out_refs)
+
+
+def dense_body(block, parts, n_slots, n_prior, refs):
     slot_refs = refs[:n_slots]
     prior = refs[n_slots : n_slots + n_prior]
-    out_ref, pick_ref, piece_ref = refs[n_slots + n_prior :]
+    *out_refs, pick_ref, piece_ref = refs[n_slots + n_prior :]
     base = (lax.axis_index("slab") * block).astype(F32)
     here = lax.broadcasted_iota(jnp.int32, (block, 128), 0).astype(F32) + base
     knots = lax.broadcasted_iota(jnp.int32, (ANG, 128), 0).astype(F32)
@@ -319,50 +355,56 @@
         piece_ref[...], pick_ref[...], (((1,), (1,)), ((), ())), preferred_element_type=F32
     )
     total = (total[:ANG] + total[ANG : 2 * ANG] + total[2 * ANG :]).T
-    out_ref[...] = total + prior[0][...] if prior else total
-
-
-def dense(block, slots, prior=()):
+    if prior:
+        total = total + prior[0][...]
+    if len(out_refs) == 1:
+        out_refs[0][...] = total
+    else:
+        split(total[: block // 2], total[block // 2 :], high_side(*parts), *out_refs)
+
+
+def dense(block, parts, slots, prior=()):
     count = sum(s.shape[0] // 3 * s.shape[1] * 128 for s in slots)
-
-    def body(*refs):
-        dense_body(block, len(slots), len(prior), refs)
-
+    packed = shape((block // 4, 2 * ANG))
     return call(
-        body,
-        shape((block, ANG)),
+        lambda *refs: dense_body(block, parts, len(slots), len(prior), refs),
+        [packed] * 2 if parts else [shape((block, ANG))],
         (*slots, *prior),
         [VM] * (len(slots) + len(prior)),
         [pltpu.VMEM((block, count), BF16), pltpu.VMEM((3 * ANG, count), BF16)],
     )
 
 
-def share_and_add(slots, axis, block):
+def share_and_add(slots, axis, block, parts):
     count = lax.axis_size(axis)
     have = slots
-    total = None
     for k in range(count.bit_length() - 1):
         got = lax.ppermute(have, axis, [(i, i ^ (1 << k)) for i in range(count)])
         if 2 << k < count:
             have = jnp.concatenate([have, got], axis=0)
         else:
-            total = dense(block, (have,))
-            total = dense(block, (got,), (total,))
-    return dense(block, (have,)) if total is None else total
-
-
-def halve(total, axis):
+            total = dense(block, None, (have,))
+            return dense(block, parts, (got,), total)
+
+
+def halve(kept, sent, steps, rows):
+    for k, (axis, step) in enumerate(steps):
+        count = lax.axis_size(axis)
+        got = lax.ppermute(sent, axis, [(i, i ^ step) for i in range(count)])
+        following = steps[k + 1] if k + 1 < len(steps) else None
+        rows = rows // 2
+        outs = [shape((rows // 4, 2 * ANG))] * 2 if following else [shape((rows, ANG))]
+        kept, *rest = call(
+            functools.partial(add_body, following), outs, (kept, got), [VM] * 2
+        )
+        if following:
+            sent = rest[0]
+    return kept
+
+
+def halving_steps(axis):
     count = lax.axis_size(axis)
-    me = lax.axis_index(axis)
-    step = count // 2
-    while step > 0:
-        half = total.shape[0] // 2
-        bit = lax.rem(me // step, 2)
-        sent = lax.dynamic_slice_in_dim(total, (1 - bit) * half, half, axis=0)
-        kept = lax.dynamic_slice_in_dim(total, bit * half, half, axis=0)
-        total = kept + lax.ppermute(sent, axis, [(i, i ^ step) for i in range(count)])
-        step //= 2
-    return total
+    return [(axis, count >> (k + 1)) for k in range(count.bit_length() - 1)]
 
 
 def rounds_of(axis):
@@ -394,7 +436,6 @@
     slots = wall_cells.size
     flat = (1, slots)
     sems = pltpu.SemaphoreType.DMA
-    phase = jnp.cos(0.5 * (step % 97).astype(F32))
     slab_rounds, row_rounds, col_rounds = (rounds_of(a) for a in ("slab", "row", "col"))
     side_rounds = row_rounds + col_rounds
     counts = (len(slab_rounds), len(row_rounds), len(col_rounds))
@@ -402,7 +443,7 @@
     *faces, p_in, q_in, a_in = call(
         lambda *refs: faces_body(slab_rounds, refs),
         [shape((2, height, width))] * counts[0] + [shape(grid)] * 3,
-        (pressure, kappa, adj_pressure_in),
+        (stay(pressure), stay(kappa), stay(adj_pressure_in)),
         [HB] * 3,
         [pltpu.VMEM(grid, F32), sems((3,))],
     )
@@ -411,32 +452,42 @@
         lambda *refs: sides_body(side_rounds, refs),
         [shape((4, depth, width if axis == "row" else height)) for axis, _ in side_rounds]
         + [shape((3, *grid)), shape(grid)],
-        (p_in, q_in, adj_velocity_in, wall_mask),
+        (p_in, q_in, stay(adj_velocity_in), stay(wall_mask)),
         [VM] * 2 + [HB] * 2,
         [pltpu.VMEM(grid, jnp.int32), sems((2,))],
     )
     side_got = swap_all(side_rounds, messages)
-    total, moved, picks, cells = call(
+    total, moved, picks, *slot_data = call(
         inner_body,
         [
             shape((3, *grid)),
             shape((3, *grid)),
             shape((depth * height, slots), BF16),
-            shape((1, 1, slots), jnp.int32),
+            shape(flat, jnp.int32),
+            shape(flat, jnp.int32),
+            shape(flat),
+            shape(flat, jnp.int32),
         ],
         (
             p_in,
             q_in,
             t_in,
-            velocity,
-            drive,
-            wall_cells.reshape(flat),
-            wall_rows.reshape(flat),
-            slot_angle.reshape(flat),
-            phase,
+            stay(velocity),
+            stay(drive),
+            stay(wall_cells.reshape(flat)),
+            stay(wall_rows.reshape(flat)),
+            stay(slot_angle.reshape(flat)),
+            wall_count.reshape(1),
+            step,
         ),
-        [VM] * 3 + [HB] * 5 + [SM],
-        [pltpu.VMEM((3, *grid), F32), pltpu.VMEM(grid, F32), sems((3,))],
+        [VM] * 3 + [HB] * 5 + [ANY] * 2,
+        [
+            pltpu.VMEM((3, *grid), F32),
+            pltpu.VMEM(grid, F32),
+            pltpu.SMEM((1,), jnp.int32),
+            pltpu.SMEM((1,), jnp.int32),
+            sems((7,)),
+        ],
     )
     lam, mine, *lam_faces = call(
         lambda *refs: main_body(counts, refs),
@@ -446,14 +497,11 @@
             moved,
             free,
             picks,
-            cells.reshape(flat),
-            wall_rows.reshape(flat),
-            slot_angle.reshape(flat),
-            wall_count.reshape(1),
+            *slot_data,
             *slab_got,
             *side_got,
         ),
-        [VM] * 7 + [SM] + [VM] * sum(counts),
+        [VM] * (8 + sum(counts)),
         [pltpu.VMEM((depth * height, width), F32)],
     )
     lam_got = swap_all(slab_rounds, lam_faces)
@@ -471,8 +519,10 @@
         (part, *lam_got),
         [VM] * (1 + counts[0]),
     )
-    total = share_and_add(mine, "slab", NROWS // lax.axis_size("slab"))
-    total = halve(halve(total, "row"), "col")
+    block = NROWS // lax.axis_size("slab")
+    steps = halving_steps("row") + halving_steps("col")
+    kept, sent = share_and_add(mine, "slab", block, steps[0])
+    total = halve(kept, sent, steps, block)
     return (adj_pressure, adj_velocity, total)
 
 

time: 39.2 us -> 36 us (0.918)
  the two profiles are of different devices: /device:TPU:16 before, /device:TPU:0 now
where the time goes in v3:
time: 36 us; the launch traced here: 35.8 us
  starting transfers between devices  17.2 us (48%)
  Pallas kernels  10.3 us (29%)
  waiting for transfers between devices  6.17 us (17%)
  between operations  2.08 us (6%)
    pallas_call x10, Pallas kernels, call(): pl.pallas_call(body, out_shape=outs, in_specs=specs, out_specs=jax.tree.m...  10.3 us
    ppermute x3, starting transfers between devices, share_and_add(): got = lax.ppermute(have, axis, [(i, i ^ 1 << k) for i in range(count)])  8.5 us
    ppermute x6, starting transfers between devices, swap(): return lax.ppermute(message, axis, swap_pairs(lax.axis_size(axis), first))  8.02 us
    ppermute x3, waiting for transfers between devices, share_and_add(): got = lax.ppermute(have, axis, [(i, i ^ 1 << k) for i in range(count)])  3.73 us
    ppermute x2, waiting for transfers between devices, halve(): got = lax.ppermute(sent, axis, [(i, i ^ step) for i in range(count)])  2.43 us
    ppermute x2, starting transfers between devices, halve(): got = lax.ppermute(sent, axis, [(i, i ^ step) for i in range(count)])  0.72 us
  transfers between devices with their start and end apart: 11, of which 4 were waited for; matrix products, arithmetic and copies ran while one was open for 0% of the time, Pallas kernels for 22%

profile of v3, /device:TPU:0, one launch (start us, length us, event | category | flops | bytes accessed | tf_op | source)
XLA Modules:
  0.0 35.8 jit_solution(15918277239015631184)
XLA Ops:
  0.6 1.2 %shard_map.139 = (f32[2,128,128]{2,1,0:T(8,128)S(1)}, f32[2,128,128]{2,1,0:T(8,128)S(1)}, f32[4,128,128]{2,1,0:T(8,128)S(1)}, f32[4,128,128]{2,1,0:T(8,128)S(1)}, f32[4,128,128]{2,1,0:T(8,128)S(1)}) custom-call(f32[4,128,128]{2,1,0:T(8,128)} %refs_0_.1, f32[4,128,128]{2,1,0:T(8,128)} %refs_1_.1, f32[4,128,128]{2,1,0:T(8,128)} %refs_2_.2), custom_call_target="tpu_custom_call" | custom-call | flops 1000000 | bytes 1000000 | tf_op jit(solution)/shard_map/pallas_call | solution.py:22
  1.8 3.1 %collective-permute-start = (f32[2,128,128]{2,1,0:T(8,128)S(1)}, f32[2,128,128]{2,1,0:T(8,128)S(1)}, u32[]{:S(2)}, u32[]{:S(2)}) collective-permute-start(f32[2,128,128]{2,1,0:T(8,128)S(1)} %get-tuple-element.40), channel_id=1, source_target_pairs={{0,4},{4,0},{8,12},{12,8},{16,20},{20,16},{24,28},{28,24},{1,5},{5... | collective-permute-start | bytes 393224 | tf_op jit(solution)/shard_map/ppermute | solution.py:60
  4.9 0.7 %collective-permute-start.1 = (f32[2,128,128]{2,1,0:T(8,128)S(1)}, f32[2,128,128]{2,1,0:T(8,128)S(1)}, u32[]{:S(2)}, u32[]{:S(2)}) collective-permute-start(f32[2,128,128]{2,1,0:T(8,128)S(1)} %get-tuple-element.41), channel_id=1, source_target_pairs={{4,8},{8,4},{12,16},{16,12},{20,24},{24,20},{5,9},{9,5},{13,17},{1... | collective-permute-start | bytes 393224 | tf_op jit(solution)/shard_map/ppermute | solution.py:60
  5.5 1.8 %shard_map.140 = (f32[4,4,128]{2,1,0:T(4,128)S(1)}, f32[4,4,128]{2,1,0:T(4,128)S(1)}, f32[3,4,128,128]{3,2,1,0:T(8,128)S(1)}, f32[4,128,128]{2,1,0:T(8,128)S(1)}) custom-call(f32[4,128,128]{2,1,0:T(8,128)S(1)} %get-tuple-element.29.refs_0_.pv_ref, f32[4,128,128]{2,1,0:T(8,128)S(1)} %get-tuple-element.30.refs_1_.qv_ref, f32[3,4,128,128]{3,2,1,0:T(8,128)} %refs_2_.3, ...), custom_call_target="tpu_custom_call" | custom-call | flops 1000000 | bytes 1000000 | tf_op jit(solution)/shard_map/pallas_call | solution.py:22
  7.3 0.1 collective-permute-start.2
  7.4 1.6 %collective-permute-start.3 = (f32[4,4,128]{2,1,0:T(4,128)S(1)}, f32[4,4,128]{2,1,0:T(4,128)S(1)}, u32[]{:S(2)}, u32[]{:S(2)}) collective-permute-start(f32[4,4,128]{2,1,0:T(4,128)S(1)} %get-tuple-element.43), channel_id=1, source_target_pairs={{0,1},{1,0},{2,3},{3,2},{4,5},{5,4},{6,7},{7,6},{8,9},{9,8},{10,11... | collective-permute-start | bytes 24584 | tf_op jit(solution)/shard_map/ppermute | solution.py:60
  10.2 1.7 %shard_map.141 = (f32[3,4,128,128]{3,2,1,0:T(8,128)S(1)}, f32[3,4,128,128]{3,2,1,0:T(8,128)S(1)}, bf16[512,512]{1,0:T(8,128)(2,1)S(1)}, s32[1,512]{1,0:T(1,128)S...) custom-call(f32[4,128,128]{2,1,0:T(8,128)S(1)} %get-tuple-element.29.refs_0_.pv_ref, ...), custom_call_target="tpu_custom_call" | custom-call | flops 1000000 | bytes 1000000 | tf_op jit(solution)/shard_map/pallas_call | solution.py:22
  11.9 0.0 collective-permute-done.2.refs_10_.refs_3_
  11.9 0.0 collective-permute-done.3.refs_11_.refs_4_
  11.9 0.0 collective-permute-done.refs_8_
  11.9 0.0 collective-permute-done.1.refs_9_
  12.0 0.7 %shard_map.142 = (f32[3,4,128,128]{3,2,1,0:T(8,128)S(1)}, f32[3,4,128]{2,1,0:T(4,128)S(1)}, f32[128,128]{1,0:T(8,128)S(1)}, f32[128,128]{1,0:T(8,128)S(1)}) custom-call(f32[3,4,128,128]{3,2,1,0:T(8,128)S(1)} %get-tuple-element.32.refs_0_, f32[3,4,128,128]{3,2,1,0:T(8,128)S(1)} %get-tuple-element.33.refs_1_, f32[4,128,128]{2,1,0:T(8,128)S(1)} %get-tuple-element.34.refs_2_, ...), custom_call_target="tpu_custom_call" | custom-call | flops 1000000 | bytes 1000000 | tf_op jit(solution)/shard_map/pallas_call | solution.py:22
  12.7 4.3 %collective-permute-start.6 = (f32[3,4,128]{2,1,0:T(4,128)S(1)}, f32[3,4,128]{2,1,0:T(4,128)S(1)}, u32[]{:S(2)}, u32[]{:S(2)}) collective-permute-start(f32[3,4,128]{2,1,0:T(4,128)S(1)} %get-tuple-element.50), channel_id=1, source_target_pairs={{0,4},{4,0},{8,12},{12,8},{16,20},{20,16},{24,28},{28,24},{1,5},{5... | collective-permute-start | bytes 18440 | tf_op jit(solution)/shard_map/ppermute | solution.py:382
  17.1 1.6 %collective-permute-done.6 = f32[3,4,128]{2,1,0:T(4,128)S(1)} collective-permute-done((f32[3,4,128]{2,1,0:T(4,128)S(1)}, f32[3,4,128]{2,1,0:T(4,128)S(1)}, u32[]{:S(2)}, u32[]{:S(2)}) %collective-permute-start.6) | collective-permute-done | bytes 6176 | tf_op jit(solution)/shard_map/ppermute | solution.py:382
  18.7 1.6 %collective-permute-start.7 = (f32[6,4,128]{2,1,0:T(4,128)S(1)}, f32[6,4,128]{2,1,0:T(4,128)S(1)}, u32[]{:S(2)}, u32[]{:S(2)}) collective-permute-start(f32[6,4,128]{2,1,0:T(4,128)S(1)} %pad_maximum_fusion), channel_id=1, source_target_pairs={{0,8},{4,12},{8,0},{12,4},{16,24},{20,28},{24,16},{28,20},{1,9},{5... | collective-permute-start | bytes 36872 | tf_op jit(solution)/shard_map/ppermute | solution.py:382
  20.2 2.1 %collective-permute-done.7 = f32[6,4,128]{2,1,0:T(4,128)S(1)} collective-permute-done((f32[6,4,128]{2,1,0:T(4,128)S(1)}, f32[6,4,128]{2,1,0:T(4,128)S(1)}, u32[]{:S(2)}, u32[]{:S(2)}) %collective-permute-start.7) | collective-permute-done | bytes 12320 | tf_op jit(solution)/shard_map/ppermute | solution.py:382
  22.4 2.6 %collective-permute-start.8 = (f32[12,4,128]{2,1,0:T(4,128)S(1)}, f32[12,4,128]{2,1,0:T(4,128)S(1)}, u32[]{:S(2)}, u32[]{:S(2)}) collective-permute-start(f32[12,4,128]{2,1,0:T(4,128)S(1)} %constant_dynamic-update-slice_fusion.refs_0_), channel_id=1, source_target_pairs={{0,16},{4,20},{8,24},{12,28},{16,0},{20,4},{24,8},{28,12},{1,17},{... | collective-permute-start | bytes 73736 | tf_op jit(solution)/shard_map/ppermute | solution.py:382
  24.9 2.0 %collective-permute-start.4 = (f32[128,128]{1,0:T(8,128)S(1)}, f32[128,128]{1,0:T(8,128)S(1)}, u32[]{:S(2)}, u32[]{:S(2)}) collective-permute-start(f32[128,128]{1,0:T(8,128)S(1)} %get-tuple-element.47), channel_id=1, source_target_pairs={{0,4},{4,0},{8,12},{12,8},{16,20},{20,16},{24,28},{28,24},{1,5},{5... | collective-permute-start | bytes 196616 | tf_op jit(solution)/shard_map/ppermute | solution.py:60
  27.0 0.7 %collective-permute-start.5 = (f32[128,128]{1,0:T(8,128)S(1)}, f32[128,128]{1,0:T(8,128)S(1)}, u32[]{:S(2)}, u32[]{:S(2)}) collective-permute-start(f32[128,128]{1,0:T(8,128)S(1)} %get-tuple-element.48), channel_id=1, source_target_pairs={{4,8},{8,4},{12,16},{16,12},{20,24},{24,20},{5,9},{9,5},{13,17},{1... | collective-permute-start | bytes 196616 | tf_op jit(solution)/shard_map/ppermute | solution.py:60
  27.6 1.1 %shard_map.145.refs_1_ = f32[256,64]{1,0:T(8,128)S(1)} custom-call(f32[12,4,128]{2,1,0:T(4,128)S(1)} %constant_dynamic-update-slice_fusion.refs_0_), custom_call_target="tpu_custom_call" | custom-call | flops 1000000 | bytes 1000000 | tf_op jit(solution)/shard_map/pallas_call | solution.py:22
  28.7 0.0 collective-permute-done.8.refs_0_
  28.7 1.2 %shard_map.146 = (f32[64,128]{1,0:T(8,128)S(1)}, f32[64,128]{1,0:T(8,128)S(1)}) custom-call(f32[12,4,128]{2,1,0:T(4,128)S(1)} %collective-permute-done.8.refs_0_, f32[256,64]{1,0:T(8,128)S(1)} %shard_map.145.refs_1_), custom_call_target="tpu_custom_call" | custom-call | flops 1000000 | bytes 1000000 | tf_op jit(solution)/shard_map/pallas_call | solution.py:22
  29.9 0.1 collective-permute-start.9
  30.0 1.2 %collective-permute-done.9.got_ref = f32[64,128]{1,0:T(8,128)S(1)} collective-permute-done((f32[64,128]{1,0:T(8,128)S(1)}, f32[64,128]{1,0:T(8,128)S(1)}, u32[]{:S(2)}, u32[]{:S(2)}) %collective-permute-start.9) | collective-permute-done | bytes 32800 | tf_op jit(solution)/shard_map/ppermute | solution.py:393
  31.2 0.1 shard_map.147
  31.3 0.7 %collective-permute-start.10 = (f32[32,128]{1,0:T(8,128)S(1)}, f32[32,128]{1,0:T(8,128)S(1)}, u32[]{:S(2)}, u32[]{:S(2)}) collective-permute-start(f32[32,128]{1,0:T(8,128)S(1)} %get-tuple-element.54), channel_id=1, source_target_pairs={{0,1},{1,0},{2,3},{3,2},{4,5},{5,4},{6,7},{7,6},{8,9},{9,8},{10,11... | collective-permute-start | bytes 49160 | tf_op jit(solution)/shard_map/ppermute | solution.py:393
  32.0 1.1 %shard_map.143 = (f32[4,128,128]{2,1,0:T(8,128)S(1)}, f32[3,4,128,128]{3,2,1,0:T(8,128)}) custom-call(f32[3,4,128,128]{3,2,1,0:T(8,128)S(1)} %get-tuple-element.44.refs_0_, f32[4,128,128]{2,1,0:T(8,128)S(1)} %get-tuple-element.30.refs_1_.qv_ref, f32[4,128,128]{2,1,0:T(8,128)S(1)} %get-tuple-element.45.refs_2_, ...), custom_call_target="tpu_custom_call" | custom-call | flops 1000000 | bytes 1000000 | tf_op jit(solution)/shard_map/pallas_call | solution.py:22
  33.1 0.0 collective-permute-done.4.refs_1_
  33.1 0.0 collective-permute-done.5.refs_2_
  33.1 0.7 %shard_map.144 = f32[4,128,128]{2,1,0:T(8,128)} custom-call(f32[4,128,128]{2,1,0:T(8,128)S(1)} %get-tuple-element.46.refs_0_, f32[128,128]{1,0:T(8,128)S(1)} %collective-permute-done.4.refs_1_, f32[128,128]{1,0:T(8,128)S(1)} %collective-permute-done.5.refs_2_), custom_call_target="tpu_custom_call" | custom-call | flops 1000000 | bytes 1000000 | tf_op jit(solution)/shard_map/pallas_call | solution.py:22
  33.9 1.2 %collective-permute-done.10.got_ref = f32[32,128]{1,0:T(8,128)S(1)} collective-permute-done((f32[32,128]{1,0:T(8,128)S(1)}, f32[32,128]{1,0:T(8,128)S(1)}, u32[]{:S(2)}, u32[]{:S(2)}) %collective-permute-start.10) | collective-permute-done | bytes 16416 | tf_op jit(solution)/shard_map/ppermute | solution.py:393
  35.1 0.7 %shard_map.148 = f32[64,64]{1,0:T(8,128)} custom-call(f32[32,128]{1,0:T(8,128)S(1)} %get-tuple-element.53.kept_ref, f32[32,128]{1,0:T(8,128)S(1)} %collective-permute-done.10.got_ref), custom_call_target="tpu_custom_call" | custom-call | flops 1000000 | bytes 1000000 | tf_op jit(solution)/shard_map/pallas_call | solution.py:22
  (4 shorter events, 0.0 us)
Async XLA Ops:
  1.8 10.1 %collective-permute-start = (f32[2,128,128]{2,1,0:T(8,128)S(1)}, f32[2,128,128]{2,1,0:T(8,128)S(1)}, u32[]{:S(2)}, u32[]{:S(2)}) collective-permute-start(f32[2,128,128]{2,1,0:T(8,128)S(1)} %get-tuple-element.40), channel_id=1, source_target_pairs={{0,4},{4,0},{8,12},{12,8},{16,20},{20,16},{24,28},{28,24},{1,5},{5... | collective-permute-start | bytes 393224 | tf_op jit(solution)/shard_map/ppermute | solution.py:60
  4.9 7.1 %collective-permute-start.1 = (f32[2,128,128]{2,1,0:T(8,128)S(1)}, f32[2,128,128]{2,1,0:T(8,128)S(1)}, u32[]{:S(2)}, u32[]{:S(2)}) collective-permute-start(f32[2,128,128]{2,1,0:T(8,128)S(1)} %get-tuple-element.41), channel_id=1, source_target_pairs={{4,8},{8,4},{12,16},{16,12},{20,24},{24,20},{5,9},{9,5},{13,17},{1... | collective-permute-start | bytes 393224 | tf_op jit(solution)/shard_map/ppermute | solution.py:60
  7.3 4.6 %collective-permute-start.2 = (f32[4,4,128]{2,1,0:T(4,128)S(1)}, f32[4,4,128]{2,1,0:T(4,128)S(1)}, u32[]{:S(2)}, u32[]{:S(2)}) collective-permute-start(f32[4,4,128]{2,1,0:T(4,128)S(1)} %get-tuple-element.42), channel_id=1, source_target_pairs={{0,2},{2,0},{1,3},{3,1},{4,6},{6,4},{5,7},{7,5},{8,10},{10,8},{9,1... | collective-permute-start | bytes 24584 | tf_op jit(solution)/shard_map/ppermute | solution.py:60
  7.4 4.6 %collective-permute-start.3 = (f32[4,4,128]{2,1,0:T(4,128)S(1)}, f32[4,4,128]{2,1,0:T(4,128)S(1)}, u32[]{:S(2)}, u32[]{:S(2)}) collective-permute-start(f32[4,4,128]{2,1,0:T(4,128)S(1)} %get-tuple-element.43), channel_id=1, source_target_pairs={{0,1},{1,0},{2,3},{3,2},{4,5},{5,4},{6,7},{7,6},{8,9},{9,8},{10,11... | collective-permute-start | bytes 24584 | tf_op jit(solution)/shard_map/ppermute | solution.py:60
  12.7 6.0 %collective-permute-start.6 = (f32[3,4,128]{2,1,0:T(4,128)S(1)}, f32[3,4,128]{2,1,0:T(4,128)S(1)}, u32[]{:S(2)}, u32[]{:S(2)}) collective-permute-start(f32[3,4,128]{2,1,0:T(4,128)S(1)} %get-tuple-element.50), channel_id=1, source_target_pairs={{0,4},{4,0},{8,12},{12,8},{16,20},{20,16},{24,28},{28,24},{1,5},{5... | collective-permute-start | bytes 18440 | tf_op jit(solution)/shard_map/ppermute | solution.py:382
  18.7 3.7 %collective-permute-start.7 = (f32[6,4,128]{2,1,0:T(4,128)S(1)}, f32[6,4,128]{2,1,0:T(4,128)S(1)}, u32[]{:S(2)}, u32[]{:S(2)}) collective-permute-start(f32[6,4,128]{2,1,0:T(4,128)S(1)} %pad_maximum_fusion), channel_id=1, source_target_pairs={{0,8},{4,12},{8,0},{12,4},{16,24},{20,28},{24,16},{28,20},{1,9},{5... | collective-permute-start | bytes 36872 | tf_op jit(solution)/shard_map/ppermute | solution.py:382
  22.4 6.4 %collective-permute-start.8 = (f32[12,4,128]{2,1,0:T(4,128)S(1)}, f32[12,4,128]{2,1,0:T(4,128)S(1)}, u32[]{:S(2)}, u32[]{:S(2)}) collective-permute-start(f32[12,4,128]{2,1,0:T(4,128)S(1)} %constant_dynamic-update-slice_fusion.refs_0_), channel_id=1, source_target_pairs={{0,16},{4,20},{8,24},{12,28},{16,0},{20,4},{24,8},{28,12},{1,17},{... | collective-permute-start | bytes 73736 | tf_op jit(solution)/shard_map/ppermute | solution.py:382
  24.9 8.2 %collective-permute-start.4 = (f32[128,128]{1,0:T(8,128)S(1)}, f32[128,128]{1,0:T(8,128)S(1)}, u32[]{:S(2)}, u32[]{:S(2)}) collective-permute-start(f32[128,128]{1,0:T(8,128)S(1)} %get-tuple-element.47), channel_id=1, source_target_pairs={{0,4},{4,0},{8,12},{12,8},{16,20},{20,16},{24,28},{28,24},{1,5},{5... | collective-permute-start | bytes 196616 | tf_op jit(solution)/shard_map/ppermute | solution.py:60
  27.0 6.1 %collective-permute-start.5 = (f32[128,128]{1,0:T(8,128)S(1)}, f32[128,128]{1,0:T(8,128)S(1)}, u32[]{:S(2)}, u32[]{:S(2)}) collective-permute-start(f32[128,128]{1,0:T(8,128)S(1)} %get-tuple-element.48), channel_id=1, source_target_pairs={{4,8},{8,4},{12,16},{16,12},{20,24},{24,20},{5,9},{9,5},{13,17},{1... | collective-permute-start | bytes 196616 | tf_op jit(solution)/shard_map/ppermute | solution.py:60
  29.9 1.3 %collective-permute-start.9 = (f32[64,128]{1,0:T(8,128)S(1)}, f32[64,128]{1,0:T(8,128)S(1)}, u32[]{:S(2)}, u32[]{:S(2)}) collective-permute-start(f32[64,128]{1,0:T(8,128)S(1)} %get-tuple-element.52), channel_id=1, source_target_pairs={{0,2},{2,0},{1,3},{3,1},{4,6},{6,4},{5,7},{7,5},{8,10},{10,8},{9,1... | collective-permute-start | bytes 98312 | tf_op jit(solution)/shard_map/ppermute | solution.py:393
  31.3 3.8 %collective-permute-start.10 = (f32[32,128]{1,0:T(8,128)S(1)}, f32[32,128]{1,0:T(8,128)S(1)}, u32[]{:S(2)}, u32[]{:S(2)}) collective-permute-start(f32[32,128]{1,0:T(8,128)S(1)} %get-tuple-element.54), channel_id=1, source_target_pairs={{0,1},{1,0},{2,3},{3,2},{4,5},{5,4},{6,7},{7,6},{8,9},{9,8},{10,11... | collective-permute-start | bytes 49160 | tf_op jit(solution)/shard_map/ppermute | solution.py:393

commit v4 on v3

--- a/solution.py
+++ b/solution.py
@@ -1,5 +1,3 @@
-import functools
-
 import jax
 import jax.numpy as jnp
 from jax import lax
@@ -13,8 +11,8 @@
 F32 = jnp.float32
 BF16 = jnp.bfloat16
 VM = pl.BlockSpec(memory_space=pltpu.VMEM)
+SM = pl.BlockSpec(memory_space=pltpu.SMEM)
 HB = pl.BlockSpec(memory_space=pltpu.HBM)
-ANY = pl.BlockSpec(memory_space=pl.ANY)
 LIMIT = pltpu.CompilerParams(vmem_limit_bytes=24 << 20)
 
 
@@ -61,10 +59,23 @@
 
 
 def faces_body(rounds, refs):
-    p_ref, k_ref, a_ref = refs[:3]
-    outs, (pv_ref, qv_ref, av_ref, kv_ref, sems) = refs[3 : 3 + len(rounds)], refs[3 + len(rounds) :]
+    p_ref, k_ref, a_ref, m_ref, c_ref, r_ref, g_ref = refs[:7]
+    outs, rest = refs[7 : 7 + len(rounds)], refs[7 + len(rounds) :]
+    pv_ref, qv_ref, av_ref, free_ref, cell_ref, row_ref, angle_ref = rest[:7]
+    kv_ref, mv_ref, sems = rest[7:]
     depth = pv_ref.shape[0]
-    copies = fetch(((k_ref, kv_ref), (a_ref, av_ref), (p_ref, pv_ref)), sems)
+    copies = fetch(
+        (
+            (k_ref, kv_ref),
+            (a_ref, av_ref),
+            (p_ref, pv_ref),
+            (m_ref, mv_ref),
+            (c_ref, cell_ref),
+            (r_ref, row_ref),
+            (g_ref, angle_ref),
+        ),
+        sems,
+    )
     copies[0].wait()
     copies[1].wait()
     for x in range(depth):
@@ -75,17 +86,16 @@
         at = jnp.where(odd != (first == 1), 0, depth - 1)
         out_ref[0] = pv_ref[at]
         out_ref[1] = qv_ref[at]
-
-
-def sides_body(rounds, refs):
-    pv_ref, qv_ref, t_ref, m_ref = refs[:4]
-    outs, (tv_ref, free_ref, mv_ref, sems) = refs[4 : 4 + len(rounds)], refs[4 + len(rounds) :]
-    depth, height, width = pv_ref.shape
-    copies = fetch(((m_ref, mv_ref), (t_ref, tv_ref)), sems)
-    copies[0].wait()
+    copies[3].wait()
     for x in range(depth):
         free_ref[x] = 1.0 - mv_ref[x].astype(F32)
-    copies[1].wait()
+    for copy in copies[4:]:
+        copy.wait()
+
+
+def sides_body(rounds, refs):
+    pv_ref, qv_ref, tv_ref, free_ref, *outs = refs
+    depth, height, width = pv_ref.shape
     lanes = lax.broadcasted_iota(jnp.int32, (height, width), 1)
     for (axis, first), out_ref in zip(rounds, outs):
         high = is_odd(axis) == (first == 1)
@@ -139,31 +149,8 @@
     return top, mid, (rest - mid.astype(F32)).astype(BF16)
 
 
-def inner_body(pv_ref, qv_ref, tv_ref, v_ref, d_ref, c_ref, r_ref, g_ref, n_ref, s_ref,
-               total_ref, moved_ref, pick_ref, cell_ref, row_ref, angle_ref, live_ref,
-               vv_ref, dv_ref, count_ref, step_ref, sems):
+def inner_body(pv_ref, qv_ref, tv_ref, v_ref, d_ref, cell_ref, step_ref, count_ref, total_ref, moved_ref, pick_ref, live_ref):
     depth, _, width = pv_ref.shape
-    copies = fetch(
-        (
-            (s_ref, step_ref),
-            (n_ref, count_ref),
-            (c_ref, cell_ref),
-            (r_ref, row_ref),
-            (g_ref, angle_ref),
-            (v_ref, vv_ref),
-            (d_ref, dv_ref),
-        ),
-        sems,
-    )
-    for x in range(depth):
-        q = qv_ref[x]
-        upper = qv_ref[x + 1] if x + 1 < depth else 0.0
-        lower = qv_ref[x - 1] if x > 0 else 0.0
-        total_ref[0, x] = tv_ref[0, x] + (upper - lower) * 0.5
-        total_ref[1, x] = tv_ref[1, x] + side(q, 0, 0.0, 0.0)
-        total_ref[2, x] = tv_ref[2, x] + side(q, 1, 0.0, 0.0)
-    for copy in copies[:5]:
-        copy.wait()
     line = lax.div(cell_ref[...], width)
     at = lax.broadcasted_iota(jnp.int32, pick_ref.shape, 0)
     pick_ref[...] = jnp.where(at == line, 1.0, 0.0).astype(BF16)
@@ -171,15 +158,18 @@
     live_ref[...] = jnp.where(slot < count_ref[0], 1, 0)
     turn = lax.rem(step_ref[0], 97).astype(F32) * 0.5
     phase = jnp.cos(jnp.full((8, width), turn, F32))[:1]
-    copies[5].wait()
-    copies[6].wait()
     for x in range(depth):
-        p = pv_ref[x]
-        upper = pv_ref[x + 1] if x + 1 < depth else 0.0
-        lower = pv_ref[x - 1] if x > 0 else 0.0
-        moved_ref[0, x] = vv_ref[0, x] - 0.3 * ((upper - lower) * 0.5) + dv_ref[x] * phase
-        moved_ref[1, x] = vv_ref[1, x] - 0.3 * side(p, 0, 0.0, 0.0)
-        moved_ref[2, x] = vv_ref[2, x] - 0.3 * side(p, 1, 0.0, 0.0)
+        p, q = pv_ref[x], qv_ref[x]
+
+        def along(field, ref):
+            upper = ref[x + 1] if x + 1 < depth else 0.0
+            lower = ref[x - 1] if x > 0 else 0.0
+            return (upper - lower) * 0.5, side(field, 0, 0.0, 0.0), side(field, 1, 0.0, 0.0)
+
+        for comp, (slope, gain) in enumerate(zip(along(p, pv_ref), along(q, qv_ref))):
+            total_ref[comp, x] = tv_ref[comp, x] + gain
+            moved = v_ref[comp, x] - 0.3 * slope
+            moved_ref[comp, x] = moved + d_ref[x] * phase if comp == 0 else moved
 
 
 def edge_table(low, high, height, width):
@@ -310,28 +300,18 @@
     return jnp.concatenate([rows[:half], rows[half:]], axis=1)
 
 
-def high_side(axis, step):
-    return lax.rem(lax.div(lax.axis_index(axis), step), 2) == 1
-
-
-def split(low, high, mine_high, kept_ref, sent_ref):
-    kept_ref[...] = pack(jnp.where(mine_high, high, low))
-    sent_ref[...] = pack(jnp.where(mine_high, low, high))
-
-
-def add_body(parts, kept_ref, got_ref, *out_refs):
-    total = kept_ref[...] + got_ref[...]
-    low, high = total[:, :ANG], total[:, ANG:]
-    if parts is None:
-        out_refs[0][...] = jnp.concatenate([low, high], axis=0)
-    else:
-        split(low, high, high_side(*parts), *out_refs)
-
-
-def dense_body(block, parts, n_slots, n_prior, refs):
+def add_body(*refs):
+    *parts, out_ref = refs
+    total = parts[0][...]
+    for part in parts[1:]:
+        total = total + part[...]
+    out_ref[...] = jnp.concatenate([total[:, :ANG], total[:, ANG:]], axis=0)
+
+
+def dense_body(block, group, n_slots, n_prior, refs):
     slot_refs = refs[:n_slots]
     prior = refs[n_slots : n_slots + n_prior]
-    *out_refs, pick_ref, piece_ref = refs[n_slots + n_prior :]
+    *out_refs, pick_ref, piece_ref = refs[n_slots + n_prior : len(refs) - bool(group)]
     base = (lax.axis_index("slab") * block).astype(F32)
     here = lax.broadcasted_iota(jnp.int32, (block, 128), 0).astype(F32) + base
     knots = lax.broadcasted_iota(jnp.int32, (ANG, 128), 0).astype(F32)
@@ -357,25 +337,33 @@
     total = (total[:ANG] + total[ANG : 2 * ANG] + total[2 * ANG :]).T
     if prior:
         total = total + prior[0][...]
-    if len(out_refs) == 1:
+    if group is None:
         out_refs[0][...] = total
     else:
-        split(total[: block // 2], total[block // 2 :], high_side(*parts), *out_refs)
-
-
-def dense(block, parts, slots, prior=()):
+        total_ref = refs[-1]
+        rows = block // len(out_refs)
+        for i in range(len(out_refs)):
+            total_ref[i] = pack(total[i * rows : (i + 1) * rows])
+        me = lax.axis_index(group)
+        for i, out_ref in enumerate(out_refs):
+            out_ref[...] = total_ref[lax.bitwise_xor(me, i)]
+
+
+def dense(block, group, slots, prior=()):
     count = sum(s.shape[0] // 3 * s.shape[1] * 128 for s in slots)
-    packed = shape((block // 4, 2 * ANG))
+    members = lax.axis_size(group) if group else 1
+    packed = (block // members // 2, 2 * ANG)
     return call(
-        lambda *refs: dense_body(block, parts, len(slots), len(prior), refs),
-        [packed] * 2 if parts else [shape((block, ANG))],
+        lambda *refs: dense_body(block, group, len(slots), len(prior), refs),
+        [shape(packed)] * members if group else [shape((block, ANG))],
         (*slots, *prior),
         [VM] * (len(slots) + len(prior)),
-        [pltpu.VMEM((block, count), BF16), pltpu.VMEM((3 * ANG, count), BF16)],
-    )
-
-
-def share_and_add(slots, axis, block, parts):
+        [pltpu.VMEM((block, count), BF16), pltpu.VMEM((3 * ANG, count), BF16)]
+        + ([pltpu.VMEM((members, *packed), F32)] if group else []),
+    )
+
+
+def share_and_add(slots, axis, block, group):
     count = lax.axis_size(axis)
     have = slots
     for k in range(count.bit_length() - 1):
@@ -384,27 +372,15 @@
             have = jnp.concatenate([have, got], axis=0)
         else:
             total = dense(block, None, (have,))
-            return dense(block, parts, (got,), total)
-
-
-def halve(kept, sent, steps, rows):
-    for k, (axis, step) in enumerate(steps):
-        count = lax.axis_size(axis)
-        got = lax.ppermute(sent, axis, [(i, i ^ step) for i in range(count)])
-        following = steps[k + 1] if k + 1 < len(steps) else None
-        rows = rows // 2
-        outs = [shape((rows // 4, 2 * ANG))] * 2 if following else [shape((rows, ANG))]
-        kept, *rest = call(
-            functools.partial(add_body, following), outs, (kept, got), [VM] * 2
-        )
-        if following:
-            sent = rest[0]
-    return kept
-
-
-def halving_steps(axis):
-    count = lax.axis_size(axis)
-    return [(axis, count >> (k + 1)) for k in range(count.bit_length() - 1)]
+            return dense(block, group, (got,), total)
+
+
+def collect(sums, group):
+    count = lax.axis_size(group)
+    parts = [sums[0]]
+    for i in range(1, count):
+        parts.append(lax.ppermute(sums[i], group, [(j, j ^ i) for j in range(count)]))
+    return call(add_body, shape((2 * sums[0].shape[0], ANG)), parts, [VM] * count)
 
 
 def rounds_of(axis):
@@ -440,54 +416,37 @@
     side_rounds = row_rounds + col_rounds
     counts = (len(slab_rounds), len(row_rounds), len(col_rounds))
 
-    *faces, p_in, q_in, a_in = call(
+    outs = call(
         lambda *refs: faces_body(slab_rounds, refs),
-        [shape((2, height, width))] * counts[0] + [shape(grid)] * 3,
-        (stay(pressure), stay(kappa), stay(adj_pressure_in)),
-        [HB] * 3,
-        [pltpu.VMEM(grid, F32), sems((3,))],
-    )
+        [shape((2, height, width))] * counts[0]
+        + [shape(grid)] * 4
+        + [shape(flat, jnp.int32), shape(flat, jnp.int32), shape(flat)],
+        (
+            *(stay(x) for x in (pressure, kappa, adj_pressure_in, wall_mask)),
+            *(stay(x.reshape(flat)) for x in (wall_cells, wall_rows, slot_angle)),
+        ),
+        [HB] * 7,
+        [pltpu.VMEM(grid, F32), pltpu.VMEM(grid, jnp.int32), sems((7,))],
+    )
+    faces, (p_in, q_in, a_in, free, *slot_data) = outs[: counts[0]], outs[counts[0] :]
     slab_got = swap_all(slab_rounds, faces)
-    *messages, t_in, free = call(
+    messages = call(
         lambda *refs: sides_body(side_rounds, refs),
-        [shape((4, depth, width if axis == "row" else height)) for axis, _ in side_rounds]
-        + [shape((3, *grid)), shape(grid)],
-        (p_in, q_in, stay(adj_velocity_in), stay(wall_mask)),
-        [VM] * 2 + [HB] * 2,
-        [pltpu.VMEM(grid, jnp.int32), sems((2,))],
+        [shape((4, depth, width if axis == "row" else height)) for axis, _ in side_rounds],
+        (p_in, q_in, adj_velocity_in, free),
+        [VM] * 4,
     )
     side_got = swap_all(side_rounds, messages)
-    total, moved, picks, *slot_data = call(
+    total, moved, picks, live = call(
         inner_body,
         [
             shape((3, *grid)),
             shape((3, *grid)),
             shape((depth * height, slots), BF16),
             shape(flat, jnp.int32),
-            shape(flat, jnp.int32),
-            shape(flat),
-            shape(flat, jnp.int32),
         ],
-        (
-            p_in,
-            q_in,
-            t_in,
-            stay(velocity),
-            stay(drive),
-            stay(wall_cells.reshape(flat)),
-            stay(wall_rows.reshape(flat)),
-            stay(slot_angle.reshape(flat)),
-            wall_count.reshape(1),
-            step,
-        ),
-        [VM] * 3 + [HB] * 5 + [ANY] * 2,
-        [
-            pltpu.VMEM((3, *grid), F32),
-            pltpu.VMEM(grid, F32),
-            pltpu.SMEM((1,), jnp.int32),
-            pltpu.SMEM((1,), jnp.int32),
-            sems((7,)),
-        ],
+        (p_in, q_in, adj_velocity_in, velocity, drive, slot_data[0], step, wall_count.reshape(1)),
+        [VM] * 6 + [SM] * 2,
     )
     lam, mine, *lam_faces = call(
         lambda *refs: main_body(counts, refs),
@@ -498,6 +457,7 @@
             free,
             picks,
             *slot_data,
+            live,
             *slab_got,
             *side_got,
         ),
@@ -520,9 +480,8 @@
         [VM] * (1 + counts[0]),
     )
     block = NROWS // lax.axis_size("slab")
-    steps = halving_steps("row") + halving_steps("col")
-    kept, sent = share_and_add(mine, "slab", block, steps[0])
-    total = halve(kept, sent, steps, block)
+    group = ("row", "col")
+    total = collect(share_and_add(mine, "slab", block, group), group)
     return (adj_pressure, adj_velocity, total)
 
 

time: 36 us -> 35.2 us (0.978)
  the two profiles are of different devices: /device:TPU:0 before, /device:TPU:1 now
where the time goes in v4:
time: 35.2 us; the launch traced here: 35 us
  starting transfers between devices  20.8 us (59%)
  Pallas kernels  8.07 us (23%)
  waiting for transfers between devices  3.99 us (11%)
  between operations  2.09 us (6%)
    ppermute x3, starting transfers between devices, share_and_add(): got = lax.ppermute(have, axis, [(i, i ^ 1 << k) for i in range(count)])  9.99 us
    pallas_call x9, Pallas kernels, call(): pl.pallas_call(body, out_shape=outs, in_specs=specs, out_specs=jax.tree.m...  8.07 us
    ppermute x6, starting transfers between devices, swap(): return lax.ppermute(message, axis, swap_pairs(lax.axis_size(axis), first))  5.72 us
    ppermute x3, starting transfers between devices, collect(): lax.ppermute(sums[i], group, [(j, j ^ i) for j in range(count)])  5.09 us
    ppermute x3, waiting for transfers between devices, share_and_add(): got = lax.ppermute(have, axis, [(i, i ^ 1 << k) for i in range(count)])  2.1 us
    ppermute x3, waiting for transfers between devices, collect(): lax.ppermute(sums[i], group, [(j, j ^ i) for j in range(count)])  1.87 us
  transfers between devices with their start and end apart: 12, of which 4 were waited for; matrix products, arithmetic and copies ran while one was open for 0% of the time, Pallas kernels for 15%

profile of v4, /device:TPU:1, one launch (start us, length us, event | category | flops | bytes accessed | tf_op | source)
XLA Modules:
  0.0 35.0 jit_solution(51116128389649291)
XLA Ops:
  0.6 0.0 copy-start
  0.6 1.3 %shard_map.139 = (f32[2,128,128]{2,1,0:T(8,128)S(1)}, f32[2,128,128]{2,1,0:T(8,128)S(1)}, f32[4,128,128]{2,1,0:T(8,128)S(1)}, f32[4,128,128]{2,1,0:T(8,128)S(1)}...) custom-call(f32[4,128,128]{2,1,0:T(8,128)} %refs_0_.1, ...), custom_call_target="tpu_custom_call" | custom-call | flops 1000000 | bytes 1000000 | tf_op jit(solution)/shard_map/pallas_call | solution.py:20
  2.0 2.1 %collective-permute-start = (f32[2,128,128]{2,1,0:T(8,128)S(1)}, f32[2,128,128]{2,1,0:T(8,128)S(1)}, u32[]{:S(2)}, u32[]{:S(2)}) collective-permute-start(f32[2,128,128]{2,1,0:T(8,128)S(1)} %get-tuple-element.38), channel_id=1, source_target_pairs={{0,4},{4,0},{8,12},{12,8},{16,20},{20,16},{24,28},{28,24},{1,5},{5... | collective-permute-start | bytes 393224 | tf_op jit(solution)/shard_map/ppermute | solution.py:58
  4.1 0.7 %collective-permute-start.1 = (f32[2,128,128]{2,1,0:T(8,128)S(1)}, f32[2,128,128]{2,1,0:T(8,128)S(1)}, u32[]{:S(2)}, u32[]{:S(2)}) collective-permute-start(f32[2,128,128]{2,1,0:T(8,128)S(1)} %get-tuple-element.39), channel_id=1, source_target_pairs={{4,8},{8,4},{12,16},{16,12},{20,24},{24,20},{5,9},{9,5},{13,17},{1... | collective-permute-start | bytes 393224 | tf_op jit(solution)/shard_map/ppermute | solution.py:58
  4.8 0.0 copy-done
  4.8 0.0 copy-start.1
  4.8 0.0 copy-start.2
  4.8 0.5 %shard_map.141 = (f32[4,4,128]{2,1,0:T(4,128)S(1)}, f32[4,4,128]{2,1,0:T(4,128)S(1)}) custom-call(f32[4,128,128]{2,1,0:T(8,128)S(1)} %get-tuple-element.28.pv_ref.refs_0_, f32[4,128,128]{2,1,0:T(8,128)S(1)} %get-tuple-element.29.qv_ref.refs_1_, f32[3,4,128,128]{3,2,1,0:T(8,128)S(1)} %copy-done, f32[4,128,128]{2,1,0:T(8,128)S(1)} %get-tuple-element.33.refs_3_.refs_2_), custom_call_target="tpu_custom_call" | custom-call | flops 1000000 | bytes 1000000 | tf_op jit(solution)/shard_map/pallas_call | solution.py:20
  5.4 1.0 %collective-permute-start.2 = (f32[4,4,128]{2,1,0:T(4,128)S(1)}, f32[4,4,128]{2,1,0:T(4,128)S(1)}, u32[]{:S(2)}, u32[]{:S(2)}) collective-permute-start(f32[4,4,128]{2,1,0:T(4,128)S(1)} %get-tuple-element.40), channel_id=1, source_target_pairs={{0,2},{2,0},{1,3},{3,1},{4,6},{6,4},{5,7},{7,5},{8,10},{10,8},{9,1... | collective-permute-start | bytes 24584 | tf_op jit(solution)/shard_map/ppermute | solution.py:58
  6.3 1.2 %collective-permute-start.3 = (f32[4,4,128]{2,1,0:T(4,128)S(1)}, f32[4,4,128]{2,1,0:T(4,128)S(1)}, u32[]{:S(2)}, u32[]{:S(2)}) collective-permute-start(f32[4,4,128]{2,1,0:T(4,128)S(1)} %get-tuple-element.41), channel_id=1, source_target_pairs={{0,1},{1,0},{2,3},{3,2},{4,5},{5,4},{6,7},{7,6},{8,9},{9,8},{10,11... | collective-permute-start | bytes 24584 | tf_op jit(solution)/shard_map/ppermute | solution.py:58
  8.9 0.0 copy-done.1
  8.9 0.0 copy-done.2
  8.9 0.6 %shard_map.140 = (f32[3,4,128,128]{3,2,1,0:T(8,128)S(1)}, f32[3,4,128,128]{3,2,1,0:T(8,128)S(1)}, bf16[512,512]{1,0:T(8,128)(2,1)S(1)}, s32[1,512]{1,0:T(1,128)S(1)}) custom-call(f32[4,128,128]{2,1,0:T(8,128)S(1)} %get-tuple-element.28.pv_ref.refs_0_, f32[4,128,128]{2,1,0:T(8,128)S(1)} %get-tuple-element.29.qv_ref.refs_1_, f32[3,4,128,128]{3,2,1,0:T(8,128)S(1)} %copy-done, ...), custom_call_target="tpu_custom_call" | custom-call | flops 1000000 | bytes 1000000 | tf_op jit(solution)/shard_map/pallas_call | solution.py:20
  9.5 0.0 collective-permute-done.2.refs_10_.refs_3_
  9.5 0.0 collective-permute-done.3.refs_11_.refs_4_
  9.5 0.0 collective-permute-done.refs_8_
  9.5 0.0 collective-permute-done.1.refs_9_
  9.5 0.8 %shard_map.142 = (f32[3,4,128,128]{3,2,1,0:T(8,128)S(1)}, f32[3,4,128]{2,1,0:T(4,128)S(1)}, f32[128,128]{1,0:T(8,128)S(1)}, f32[128,128]{1,0:T(8,128)S(1)}) custom-call(f32[3,4,128,128]{3,2,1,0:T(8,128)S(1)} %get-tuple-element.31.refs_0_, f32[3,4,128,128]{3,2,1,0:T(8,128)S(1)} %get-tuple-element.32.refs_1_, ...), custom_call_target="tpu_custom_call" | custom-call | flops 1000000 | bytes 1000000 | tf_op jit(solution)/shard_map/pallas_call | solution.py:20
  10.3 4.1 %collective-permute-start.6 = (f32[3,4,128]{2,1,0:T(4,128)S(1)}, f32[3,4,128]{2,1,0:T(4,128)S(1)}, u32[]{:S(2)}, u32[]{:S(2)}) collective-permute-start(f32[3,4,128]{2,1,0:T(4,128)S(1)} %get-tuple-element.48), channel_id=1, source_target_pairs={{0,4},{4,0},{8,12},{12,8},{16,20},{20,16},{24,28},{28,24},{1,5},{5... | collective-permute-start | bytes 18440 | tf_op jit(solution)/shard_map/ppermute | solution.py:370
  14.4 0.1 collective-permute-start.4
  14.5 0.7 %collective-permute-start.5 = (f32[128,128]{1,0:T(8,128)S(1)}, f32[128,128]{1,0:T(8,128)S(1)}, u32[]{:S(2)}, u32[]{:S(2)}) collective-permute-start(f32[128,128]{1,0:T(8,128)S(1)} %get-tuple-element.46), channel_id=1, source_target_pairs={{4,8},{8,4},{12,16},{16,12},{20,24},{24,20},{5,9},{9,5},{13,17},{1... | collective-permute-start | bytes 196616 | tf_op jit(solution)/shard_map/ppermute | solution.py:58
  15.1 0.3 collective-permute-done.6
  15.4 3.6 %collective-permute-start.7 = (f32[6,4,128]{2,1,0:T(4,128)S(1)}, f32[6,4,128]{2,1,0:T(4,128)S(1)}, u32[]{:S(2)}, u32[]{:S(2)}) collective-permute-start(f32[6,4,128]{2,1,0:T(4,128)S(1)} %pad_maximum_fusion), channel_id=1, source_target_pairs={{0,8},{4,12},{8,0},{12,4},{16,24},{20,28},{24,16},{28,20},{1,9},{5... | collective-permute-start | bytes 36872 | tf_op jit(solution)/shard_map/ppermute | solution.py:370
  19.0 1.7 %collective-permute-done.7 = f32[6,4,128]{2,1,0:T(4,128)S(1)} collective-permute-done((f32[6,4,128]{2,1,0:T(4,128)S(1)}, f32[6,4,128]{2,1,0:T(4,128)S(1)}, u32[]{:S(2)}, u32[]{:S(2)}) %collective-permute-start.7) | collective-permute-done | bytes 12320 | tf_op jit(solution)/shard_map/ppermute | solution.py:370
  20.7 2.3 %collective-permute-start.8 = (f32[12,4,128]{2,1,0:T(4,128)S(1)}, f32[12,4,128]{2,1,0:T(4,128)S(1)}, u32[]{:S(2)}, u32[]{:S(2)}) collective-permute-start(f32[12,4,128]{2,1,0:T(4,128)S(1)} %constant_dynamic-update-slice_fusion.refs_0_), channel_id=1, source_target_pairs={{0,16},{4,20},{8,24},{12,28},{16,0},{20,4},{24,8},{28,12},{1,17},{... | collective-permute-start | bytes 73736 | tf_op jit(solution)/shard_map/ppermute | solution.py:370
  23.0 1.1 %shard_map.145.refs_1_ = f32[256,64]{1,0:T(8,128)S(1)} custom-call(f32[12,4,128]{2,1,0:T(4,128)S(1)} %constant_dynamic-update-slice_fusion.refs_0_), custom_call_target="tpu_custom_call" | custom-call | flops 1000000 | bytes 1000000 | tf_op jit(solution)/shard_map/pallas_call | solution.py:20
  24.1 0.2 collective-permute-done.8.refs_0_
  24.3 1.2 %shard_map.146 = (f32[32,128]{1,0:T(8,128)S(1)}, f32[32,128]{1,0:T(8,128)S(1)}, f32[32,128]{1,0:T(8,128)S(1)}, f32[32,128]{1,0:T(8,128)S(1)}) custom-call(f32[12,4,128]{2,1,0:T(4,128)S(1)} %collective-permute-done.8.refs_0_, f32[256,64]{1,0:T(8,128)S(1)} %shard_map.145.refs_1_), custom_call_target="tpu_custom_call" | custom-call | flops 1000000 | bytes 1000000 | tf_op jit(solution)/shard_map/pallas_call | solution.py:20
  25.5 0.6 %collective-permute-start.9 = (f32[32,128]{1,0:T(8,128)S(1)}, f32[32,128]{1,0:T(8,128)S(1)}, u32[]{:S(2)}, u32[]{:S(2)}) collective-permute-start(f32[32,128]{1,0:T(8,128)S(1)} %get-tuple-element.50), channel_id=1, source_target_pairs={{0,1},{1,0},{2,3},{3,2},{4,5},{5,4},{6,7},{7,6},{8,9},{9,8},{10,11... | collective-permute-start | bytes 49160 | tf_op jit(solution)/shard_map/ppermute | solution.py:382
  26.0 4.4 %collective-permute-start.10 = (f32[32,128]{1,0:T(8,128)S(1)}, f32[32,128]{1,0:T(8,128)S(1)}, u32[]{:S(2)}, u32[]{:S(2)}) collective-permute-start(f32[32,128]{1,0:T(8,128)S(1)} %get-tuple-element.51), channel_id=1, source_target_pairs={{0,2},{1,3},{2,0},{3,1},{4,6},{5,7},{6,4},{7,5},{8,10},{9,11},{10,... | collective-permute-start | bytes 49160 | tf_op jit(solution)/shard_map/ppermute | solution.py:382
  30.4 0.1 collective-permute-start.11
  30.5 1.1 %shard_map.143 = (f32[4,128,128]{2,1,0:T(8,128)S(1)}, f32[3,4,128,128]{3,2,1,0:T(8,128)}) custom-call(f32[3,4,128,128]{3,2,1,0:T(8,128)S(1)} %get-tuple-element.42.refs_0_, f32[4,128,128]{2,1,0:T(8,128)S(1)} %get-tuple-element.29.qv_ref.refs_1_, f32[4,128,128]{2,1,0:T(8,128)S(1)} %get-tuple-element.43.refs_2_, ...), custom_call_target="tpu_custom_call" | custom-call | flops 1000000 | bytes 1000000 | tf_op jit(solution)/shard_map/pallas_call | solution.py:20
  31.7 0.0 collective-permute-done.9.refs_1_
  31.7 0.0 collective-permute-done.10.refs_2_
  31.7 1.9 %collective-permute-done.11.refs_3_ = f32[32,128]{1,0:T(8,128)S(1)} collective-permute-done((f32[32,128]{1,0:T(8,128)S(1)}, f32[32,128]{1,0:T(8,128)S(1)}, u32[]{:S(2)}, u32[]{:S(2)}) %collective-permute-start.11) | collective-permute-done | bytes 16416 | tf_op jit(solution)/shard_map/ppermute | solution.py:382
  33.6 0.7 %shard_map.147 = f32[64,64]{1,0:T(8,128)} custom-call(f32[32,128]{1,0:T(8,128)S(1)} %get-tuple-element.49.refs_0_, f32[32,128]{1,0:T(8,128)S(1)} %collective-permute-done.9.refs_1_, f32[32,128]{1,0:T(8,128)S(1)} %collective-permute-done.10.refs_2_, f32[32,128]{1,0:T(8,128)S(1)} %collective-permute-done.11.refs_3_), custom_call_target="tpu_custom_call" | custom-call | flops 1000000 | bytes 1000000 | tf_op jit(solution)/shard_map/pallas_call | solution.py:20
  34.3 0.0 collective-permute-done.4.refs_1_
  34.3 0.0 collective-permute-done.5.refs_2_
  34.3 0.7 %shard_map.144 = f32[4,128,128]{2,1,0:T(8,128)} custom-call(f32[4,128,128]{2,1,0:T(8,128)S(1)} %get-tuple-element.44.refs_0_, f32[128,128]{1,0:T(8,128)S(1)} %collective-permute-done.4.refs_1_, f32[128,128]{1,0:T(8,128)S(1)} %collective-permute-done.5.refs_2_), custom_call_target="tpu_custom_call" | custom-call | flops 1000000 | bytes 1000000 | tf_op jit(solution)/shard_map/pallas_call | solution.py:20
  (4 shorter events, 0.0 us)
Async XLA Ops:
  0.6 4.2 %copy-start = (f32[3,4,128,128]{3,2,1,0:T(8,128)S(1)}, f32[3,4,128,128]{3,2,1,0:T(8,128)}, u32[]{:S(2)}) copy-start(f32[3,4,128,128]{3,2,1,0:T(8,128)} %refs_2_.3) | copy-start | bytes 2359300
  2.0 7.5 %collective-permute-start = (f32[2,128,128]{2,1,0:T(8,128)S(1)}, f32[2,128,128]{2,1,0:T(8,128)S(1)}, u32[]{:S(2)}, u32[]{:S(2)}) collective-permute-start(f32[2,128,128]{2,1,0:T(8,128)S(1)} %get-tuple-element.38), channel_id=1, source_target_pairs={{0,4},{4,0},{8,12},{12,8},{16,20},{20,16},{24,28},{28,24},{1,5},{5... | collective-permute-start | bytes 393224 | tf_op jit(solution)/shard_map/ppermute | solution.py:58
  4.1 5.4 %collective-permute-start.1 = (f32[2,128,128]{2,1,0:T(8,128)S(1)}, f32[2,128,128]{2,1,0:T(8,128)S(1)}, u32[]{:S(2)}, u32[]{:S(2)}) collective-permute-start(f32[2,128,128]{2,1,0:T(8,128)S(1)} %get-tuple-element.39), channel_id=1, source_target_pairs={{4,8},{8,4},{12,16},{16,12},{20,24},{24,20},{5,9},{9,5},{13,17},{1... | collective-permute-start | bytes 393224 | tf_op jit(solution)/shard_map/ppermute | solution.py:58
  4.8 4.1 %copy-start.1 = (f32[3,4,128,128]{3,2,1,0:T(8,128)S(1)}, f32[3,4,128,128]{3,2,1,0:T(8,128)}, u32[]{:S(2)}) copy-start(f32[3,4,128,128]{3,2,1,0:T(8,128)} %v_ref.1) | copy-start | bytes 2359300
  4.8 4.1 %copy-start.2 = (f32[4,128,128]{2,1,0:T(8,128)S(1)}, f32[4,128,128]{2,1,0:T(8,128)}, u32[]{:S(2)}) copy-start(f32[4,128,128]{2,1,0:T(8,128)} %d_ref.1) | copy-start | bytes 786436
  5.4 4.1 %collective-permute-start.2 = (f32[4,4,128]{2,1,0:T(4,128)S(1)}, f32[4,4,128]{2,1,0:T(4,128)S(1)}, u32[]{:S(2)}, u32[]{:S(2)}) collective-permute-start(f32[4,4,128]{2,1,0:T(4,128)S(1)} %get-tuple-element.40), channel_id=1, source_target_pairs={{0,2},{2,0},{1,3},{3,1},{4,6},{6,4},{5,7},{7,5},{8,10},{10,8},{9,1... | collective-permute-start | bytes 24584 | tf_op jit(solution)/shard_map/ppermute | solution.py:58
  6.3 3.2 %collective-permute-start.3 = (f32[4,4,128]{2,1,0:T(4,128)S(1)}, f32[4,4,128]{2,1,0:T(4,128)S(1)}, u32[]{:S(2)}, u32[]{:S(2)}) collective-permute-start(f32[4,4,128]{2,1,0:T(4,128)S(1)} %get-tuple-element.41), channel_id=1, source_target_pairs={{0,1},{1,0},{2,3},{3,2},{4,5},{5,4},{6,7},{7,6},{8,9},{9,8},{10,11... | collective-permute-start | bytes 24584 | tf_op jit(solution)/shard_map/ppermute | solution.py:58
  10.3 5.1 %collective-permute-start.6 = (f32[3,4,128]{2,1,0:T(4,128)S(1)}, f32[3,4,128]{2,1,0:T(4,128)S(1)}, u32[]{:S(2)}, u32[]{:S(2)}) collective-permute-start(f32[3,4,128]{2,1,0:T(4,128)S(1)} %get-tuple-element.48), channel_id=1, source_target_pairs={{0,4},{4,0},{8,12},{12,8},{16,20},{20,16},{24,28},{28,24},{1,5},{5... | collective-permute-start | bytes 18440 | tf_op jit(solution)/shard_map/ppermute | solution.py:370
  14.4 19.9 %collective-permute-start.4 = (f32[128,128]{1,0:T(8,128)S(1)}, f32[128,128]{1,0:T(8,128)S(1)}, u32[]{:S(2)}, u32[]{:S(2)}) collective-permute-start(f32[128,128]{1,0:T(8,128)S(1)} %get-tuple-element.45), channel_id=1, source_target_pairs={{0,4},{4,0},{8,12},{12,8},{16,20},{20,16},{24,28},{28,24},{1,5},{5... | collective-permute-start | bytes 196616 | tf_op jit(solution)/shard_map/ppermute | solution.py:58
  14.5 19.8 %collective-permute-start.5 = (f32[128,128]{1,0:T(8,128)S(1)}, f32[128,128]{1,0:T(8,128)S(1)}, u32[]{:S(2)}, u32[]{:S(2)}) collective-permute-start(f32[128,128]{1,0:T(8,128)S(1)} %get-tuple-element.46), channel_id=1, source_target_pairs={{4,8},{8,4},{12,16},{16,12},{20,24},{24,20},{5,9},{9,5},{13,17},{1... | collective-permute-start | bytes 196616 | tf_op jit(solution)/shard_map/ppermute | solution.py:58
  15.4 5.3 %collective-permute-start.7 = (f32[6,4,128]{2,1,0:T(4,128)S(1)}, f32[6,4,128]{2,1,0:T(4,128)S(1)}, u32[]{:S(2)}, u32[]{:S(2)}) collective-permute-start(f32[6,4,128]{2,1,0:T(4,128)S(1)} %pad_maximum_fusion), channel_id=1, source_target_pairs={{0,8},{4,12},{8,0},{12,4},{16,24},{20,28},{24,16},{28,20},{1,9},{5... | collective-permute-start | bytes 36872 | tf_op jit(solution)/shard_map/ppermute | solution.py:370
  20.7 3.6 %collective-permute-start.8 = (f32[12,4,128]{2,1,0:T(4,128)S(1)}, f32[12,4,128]{2,1,0:T(4,128)S(1)}, u32[]{:S(2)}, u32[]{:S(2)}) collective-permute-start(f32[12,4,128]{2,1,0:T(4,128)S(1)} %constant_dynamic-update-slice_fusion.refs_0_), channel_id=1, source_target_pairs={{0,16},{4,20},{8,24},{12,28},{16,0},{20,4},{24,8},{28,12},{1,17},{... | collective-permute-start | bytes 73736 | tf_op jit(solution)/shard_map/ppermute | solution.py:370
  25.5 6.2 %collective-permute-start.9 = (f32[32,128]{1,0:T(8,128)S(1)}, f32[32,128]{1,0:T(8,128)S(1)}, u32[]{:S(2)}, u32[]{:S(2)}) collective-permute-start(f32[32,128]{1,0:T(8,128)S(1)} %get-tuple-element.50), channel_id=1, source_target_pairs={{0,1},{1,0},{2,3},{3,2},{4,5},{5,4},{6,7},{7,6},{8,9},{9,8},{10,11... | collective-permute-start | bytes 49160 | tf_op jit(solution)/shard_map/ppermute | solution.py:382
  26.0 5.7 %collective-permute-start.10 = (f32[32,128]{1,0:T(8,128)S(1)}, f32[32,128]{1,0:T(8,128)S(1)}, u32[]{:S(2)}, u32[]{:S(2)}) collective-permute-start(f32[32,128]{1,0:T(8,128)S(1)} %get-tuple-element.51), channel_id=1, source_target_pairs={{0,2},{1,3},{2,0},{3,1},{4,6},{5,7},{6,4},{7,5},{8,10},{9,11},{10,... | collective-permute-start | bytes 49160 | tf_op jit(solution)/shard_map/ppermute | solution.py:382
  30.4 3.2 %collective-permute-start.11 = (f32[32,128]{1,0:T(8,128)S(1)}, f32[32,128]{1,0:T(8,128)S(1)}, u32[]{:S(2)}, u32[]{:S(2)}) collective-permute-start(f32[32,128]{1,0:T(8,128)S(1)} %get-tuple-element.52), channel_id=1, source_target_pairs={{0,3},{1,2},{2,1},{3,0},{4,7},{5,6},{6,5},{7,4},{8,11},{9,10},{10,... | collective-permute-start | bytes 49160 | tf_op jit(solution)/shard_map/ppermute | solution.py:382

commit v5 on v4

--- a/solution.py
+++ b/solution.py
@@ -55,27 +55,22 @@
 
 
 def swap(axis, first, message):
-    return lax.ppermute(message, axis, swap_pairs(lax.axis_size(axis), first))
+    count, lines = lax.axis_size(axis), lax.axis_size("row")
+    pairs = swap_pairs(count, first)
+    if axis != "slab" or lines % 2:
+        return lax.ppermute(message, axis, pairs)
+    left = set(range(count)) - {i for i, _ in pairs}
+    both = [(i * lines + r, j * lines + r) for i, j in pairs for r in range(lines)]
+    both += [(i * lines + r, i * lines + (r ^ 1)) for i in sorted(left) for r in range(lines)]
+    return lax.ppermute(message, (axis, "row"), both)
 
 
 def faces_body(rounds, refs):
-    p_ref, k_ref, a_ref, m_ref, c_ref, r_ref, g_ref = refs[:7]
-    outs, rest = refs[7 : 7 + len(rounds)], refs[7 + len(rounds) :]
-    pv_ref, qv_ref, av_ref, free_ref, cell_ref, row_ref, angle_ref = rest[:7]
-    kv_ref, mv_ref, sems = rest[7:]
+    p_ref, k_ref, a_ref, m_ref = refs[:4]
+    outs, rest = refs[4 : 4 + len(rounds)], refs[4 + len(rounds) :]
+    pv_ref, qv_ref, av_ref, free_ref, kv_ref, mv_ref, sems = rest
     depth = pv_ref.shape[0]
-    copies = fetch(
-        (
-            (k_ref, kv_ref),
-            (a_ref, av_ref),
-            (p_ref, pv_ref),
-            (m_ref, mv_ref),
-            (c_ref, cell_ref),
-            (r_ref, row_ref),
-            (g_ref, angle_ref),
-        ),
-        sems,
-    )
+    copies = fetch(((k_ref, kv_ref), (a_ref, av_ref), (p_ref, pv_ref), (m_ref, mv_ref)), sems)
     copies[0].wait()
     copies[1].wait()
     for x in range(depth):
@@ -89,8 +84,6 @@
     copies[3].wait()
     for x in range(depth):
         free_ref[x] = 1.0 - mv_ref[x].astype(F32)
-    for copy in copies[4:]:
-        copy.wait()
 
 
 def sides_body(rounds, refs):
@@ -131,7 +124,9 @@
     odd = is_odd(axis)
     first = refs[0][...]
     second = refs[1][...] if len(refs) > 1 else jnp.zeros_like(first)
-    return jnp.where(odd, first, second), jnp.where(odd, second, first)
+    me = lax.axis_index(axis)
+    low, high = jnp.where(odd, first, second), jnp.where(odd, second, first)
+    return jnp.where(me == 0, 0.0, low), jnp.where(me == lax.axis_size(axis) - 1, 0.0, high)
 
 
 def side(field, axis, low, high):
@@ -149,11 +144,10 @@
     return top, mid, (rest - mid.astype(F32)).astype(BF16)
 
 
-def inner_body(pv_ref, qv_ref, tv_ref, v_ref, d_ref, cell_ref, step_ref, count_ref, total_ref, moved_ref, pick_ref, live_ref):
+def inner_body(pv_ref, qv_ref, tv_ref, v_ref, d_ref, c_ref, r_ref, g_ref, step_ref, count_ref,
+               total_ref, moved_ref, pick_ref, cell_ref, row_ref, angle_ref, live_ref, sems):
     depth, _, width = pv_ref.shape
-    line = lax.div(cell_ref[...], width)
-    at = lax.broadcasted_iota(jnp.int32, pick_ref.shape, 0)
-    pick_ref[...] = jnp.where(at == line, 1.0, 0.0).astype(BF16)
+    copies = fetch(((c_ref, cell_ref), (r_ref, row_ref), (g_ref, angle_ref)), sems)
     slot = lax.broadcasted_iota(jnp.int32, live_ref.shape, 1)
     live_ref[...] = jnp.where(slot < count_ref[0], 1, 0)
     turn = lax.rem(step_ref[0], 97).astype(F32) * 0.5
@@ -170,6 +164,11 @@
             total_ref[comp, x] = tv_ref[comp, x] + gain
             moved = v_ref[comp, x] - 0.3 * slope
             moved_ref[comp, x] = moved + d_ref[x] * phase if comp == 0 else moved
+    for copy in copies:
+        copy.wait()
+    line = lax.div(cell_ref[...], width)
+    at = lax.broadcasted_iota(jnp.int32, pick_ref.shape, 0)
+    pick_ref[...] = jnp.where(at == line, 1.0, 0.0).astype(BF16)
 
 
 def edge_table(low, high, height, width):
@@ -308,31 +307,58 @@
     out_ref[...] = jnp.concatenate([total[:, :ANG], total[:, ANG:]], axis=0)
 
 
+def four_weights(angle):
+    below = jnp.floor(angle)
+    f = angle - below
+    g = 1.0 - f
+    f3, g3 = f * f * f, g * g * g
+    f1, g1 = 1.0 + f, 1.0 + g
+    weights = (g3, g1 * g1 * g1 - 4.0 * g3, f1 * f1 * f1 - 4.0 * f3, f3)
+    knots = [below + shift for shift in (-1.0, 0.0, 1.0, 2.0)]
+    knots = [jnp.where(k < 0.0, k + ANG, jnp.where(k >= ANG, k - ANG, k)) for k in knots]
+    return knots, weights
+
+
 def dense_body(block, group, n_slots, n_prior, refs):
     slot_refs = refs[:n_slots]
     prior = refs[n_slots : n_slots + n_prior]
-    *out_refs, pick_ref, piece_ref = refs[n_slots + n_prior : len(refs) - bool(group)]
+    out_refs = refs[n_slots + n_prior : len(refs) - bool(group)]
+    picks, pieces = [], []
     base = (lax.axis_index("slab") * block).astype(F32)
-    here = lax.broadcasted_iota(jnp.int32, (block, 128), 0).astype(F32) + base
-    knots = lax.broadcasted_iota(jnp.int32, (ANG, 128), 0).astype(F32)
-    at = 0
+    tall = 16
+    exact = BF16 if block <= 256 else F32
+    count = lax.broadcasted_iota(jnp.int32, (tall, 128), 0)
+    one, zero = jnp.ones((tall, 128), BF16), jnp.zeros((tall, 128), BF16)
+
+    def spread(rows, j, kind=BF16):
+        return jnp.broadcast_to(rows[j : j + 1], (tall, 128)).astype(kind)
+
     for slot_ref in slot_refs:
         for d in range(slot_ref.shape[0] // 3):
+            value = slot_ref[3 * d] * (1.0 / 6.0)
+            row = slot_ref[3 * d + 1] - base
+            row = jnp.where((row < 0.0) | (row >= block), -1.0, row)
+            places, weights = four_weights(slot_ref[3 * d + 2])
+            parts = [[p.astype(F32) for p in halves(value * w)] for w in weights]
             for j in range(slot_ref.shape[1]):
-                value = slot_ref[3 * d, pl.ds(j, 1), :] * (1.0 / 6.0)
-                row = slot_ref[3 * d + 1, pl.ds(j, 1), :]
-                angle = slot_ref[3 * d + 2, pl.ds(j, 1), :]
-                lanes = pl.ds(at, 128)
-                pick_ref[:, lanes] = jnp.where(here == row, 1.0, 0.0).astype(BF16)
-                dist = jnp.abs(angle - knots)
-                dist = jnp.minimum(dist, ANG - dist)
-                outer = jnp.maximum(2.0 - dist, 0.0)
-                inner = jnp.maximum(1.0 - dist, 0.0)
-                weight = outer * outer * outer - 4.0 * (inner * inner * inner)
-                piece_ref[:, lanes] = jnp.concatenate(halves(value * weight), axis=0)
-                at += 128
+                mine = spread(row, j, exact)
+                lines = [(count + y).astype(F32).astype(exact) for y in range(0, block, tall)]
+                picks.append(jnp.concatenate([jnp.where(l == mine, one, zero) for l in lines], axis=0))
+                marks = [spread(p, j) for p in places]
+                shares = [[spread(p, j) for p in part] for part in parts]
+                columns_of = [[], [], []]
+                for y in range(0, ANG, tall):
+                    here = (count + y).astype(F32).astype(BF16)
+                    hits = [here == mark for mark in marks]
+                    for p in range(3):
+                        total = zero
+                        for hit, share in zip(hits, shares):
+                            total = jnp.where(hit, share[p], total)
+                        columns_of[p].append(total)
+                pieces.append(jnp.concatenate(columns_of[0] + columns_of[1] + columns_of[2], axis=0))
+    picks, pieces = jnp.concatenate(picks, axis=1), jnp.concatenate(pieces, axis=1)
     total = lax.dot_general(
-        piece_ref[...], pick_ref[...], (((1,), (1,)), ((), ())), preferred_element_type=F32
+        pieces, picks, (((1,), (1,)), ((), ())), preferred_element_type=F32
     )
     total = (total[:ANG] + total[ANG : 2 * ANG] + total[2 * ANG :]).T
     if prior:
@@ -350,7 +376,6 @@
 
 
 def dense(block, group, slots, prior=()):
-    count = sum(s.shape[0] // 3 * s.shape[1] * 128 for s in slots)
     members = lax.axis_size(group) if group else 1
     packed = (block // members // 2, 2 * ANG)
     return call(
@@ -358,8 +383,7 @@
         [shape(packed)] * members if group else [shape((block, ANG))],
         (*slots, *prior),
         [VM] * (len(slots) + len(prior)),
-        [pltpu.VMEM((block, count), BF16), pltpu.VMEM((3 * ANG, count), BF16)]
-        + ([pltpu.VMEM((members, *packed), F32)] if group else []),
+        [pltpu.VMEM((members, *packed), F32)] if group else [],
     )
 
 
@@ -419,16 +443,12 @@
     outs = call(
         lambda *refs: faces_body(slab_rounds, refs),
         [shape((2, height, width))] * counts[0]
-        + [shape(grid)] * 4
-        + [shape(flat, jnp.int32), shape(flat, jnp.int32), shape(flat)],
-        (
-            *(stay(x) for x in (pressure, kappa, adj_pressure_in, wall_mask)),
-            *(stay(x.reshape(flat)) for x in (wall_cells, wall_rows, slot_angle)),
-        ),
-        [HB] * 7,
-        [pltpu.VMEM(grid, F32), pltpu.VMEM(grid, jnp.int32), sems((7,))],
-    )
-    faces, (p_in, q_in, a_in, free, *slot_data) = outs[: counts[0]], outs[counts[0] :]
+        + [shape(grid)] * 4,
+        [stay(x) for x in (pressure, kappa, adj_pressure_in, wall_mask)],
+        [HB] * 4,
+        [pltpu.VMEM(grid, F32), pltpu.VMEM(grid, jnp.int32), sems((4,))],
+    )
+    faces, (p_in, q_in, a_in, free) = outs[: counts[0]], outs[counts[0] :]
     slab_got = swap_all(slab_rounds, faces)
     messages = call(
         lambda *refs: sides_body(side_rounds, refs),
@@ -437,16 +457,29 @@
         [VM] * 4,
     )
     side_got = swap_all(side_rounds, messages)
-    total, moved, picks, live = call(
+    total, moved, picks, *slot_data = call(
         inner_body,
         [
             shape((3, *grid)),
             shape((3, *grid)),
             shape((depth * height, slots), BF16),
             shape(flat, jnp.int32),
+            shape(flat, jnp.int32),
+            shape(flat),
+            shape(flat, jnp.int32),
         ],
-        (p_in, q_in, adj_velocity_in, velocity, drive, slot_data[0], step, wall_count.reshape(1)),
-        [VM] * 6 + [SM] * 2,
+        (
+            p_in,
+            q_in,
+            adj_velocity_in,
+            velocity,
+            drive,
+            *(stay(x.reshape(flat)) for x in (wall_cells, wall_rows, slot_angle)),
+            step,
+            wall_count.reshape(1),
+        ),
+        [VM] * 5 + [HB] * 3 + [SM] * 2,
+        [sems((3,))],
     )
     lam, mine, *lam_faces = call(
         lambda *refs: main_body(counts, refs),
@@ -457,7 +490,6 @@
             free,
             picks,
             *slot_data,
-            live,
             *slab_got,
             *side_got,
         ),

time: 35.2 us -> 31.6 us (0.90)
  starting transfers between devices: 20.8 us -> 17.4 us
  Pallas kernels: 8.07 us -> 7.4 us
  waiting for transfers between devices: 3.99 us -> 4.47 us
    ppermute x3, starting transfers between devices: 9.99 us -> 6.4 us  [share_and_add(): got = lax.ppermute(have, axis, [(i, i ^ 1 << k) for i in range(count)])]
    pallas_call x9, Pallas kernels: 8.07 us -> 7.4 us  [call(): pl.pallas_call(body, out_shape=outs, in_specs=specs, out_specs=jax.tree.m...]
    ppermute x3, waiting for transfers between devices: 2.1 us -> 2.58 us  [share_and_add(): got = lax.ppermute(have, axis, [(i, i ^ 1 << k) for i in range(count)])]
  transfers between devices with their start and end apart: 12 -> 12, of which waited for: 4 -> 3; matrix products, arithmetic and copies ran while one was open for 0% -> 0% of each run, Pallas kernels for 15% -> 15%
where the time goes in v5:
time: 31.6 us; the launch traced here: 31.4 us
  starting transfers between devices  17.4 us (55%)
  Pallas kernels  7.4 us (23%)
  waiting for transfers between devices  4.47 us (14%)
  between operations  2.06 us (7%)
    pallas_call x9, Pallas kernels, call(): pl.pallas_call(body, out_shape=outs, in_specs=specs, out_specs=jax.tree.m...  7.4 us
    ppermute x3, starting transfers between devices, share_and_add(): got = lax.ppermute(have, axis, [(i, i ^ 1 << k) for i in range(count)])  6.4 us
    ppermute x3, starting transfers between devices, collect(): lax.ppermute(sums[i], group, [(j, j ^ i) for j in range(count)])  5.27 us
    ppermute x4, starting transfers between devices, swap(): return lax.ppermute(message, (axis, 'row'), both)  4.45 us
    ppermute x3, waiting for transfers between devices, share_and_add(): got = lax.ppermute(have, axis, [(i, i ^ 1 << k) for i in range(count)])  2.58 us
    ppermute x3, waiting for transfers between devices, collect(): lax.ppermute(sums[i], group, [(j, j ^ i) for j in range(count)])  1.88 us
    ppermute x2, starting transfers between devices, swap(): return lax.ppermute(message, axis, pairs)  1.32 us
  transfers between devices with their start and end apart: 12, of which 3 were waited for; matrix products, arithmetic and copies ran while one was open for 0% of the time, Pallas kernels for 15%

profile of v5, /device:TPU:1, one launch (start us, length us, event | category | flops | bytes accessed | tf_op | source)
XLA Modules:
  0.0 31.4 jit_solution(2442826043375034044)
XLA Ops:
  0.6 0.0 copy-start
  0.6 1.3 %shard_map.139 = (f32[2,128,128]{2,1,0:T(8,128)S(1)}, f32[2,128,128]{2,1,0:T(8,128)S(1)}, f32[4,128,128]{2,1,0:T(8,128)S(1)}, f32[4,128,128]{2,1,0:T(8,128)S(1)}...) custom-call(f32[4,128,128]{2,1,0:T(8,128)} %refs_0_.1, f32[4,128,128]{2,1,0:T(8,128)} %refs_1_.1, ...), custom_call_target="tpu_custom_call" | custom-call | flops 1000000 | bytes 1000000 | tf_op jit(solution)/shard_map/pallas_call | solution.py:20
  2.0 2.1 %collective-permute-start = (f32[2,128,128]{2,1,0:T(8,128)S(1)}, f32[2,128,128]{2,1,0:T(8,128)S(1)}, u32[]{:S(2)}, u32[]{:S(2)}) collective-permute-start(f32[2,128,128]{2,1,0:T(8,128)S(1)} %get-tuple-element.38), channel_id=1, source_target_pairs={{0,4},{2,6},{4,0},{6,2},{8,12},{10,14},{12,8},{14,10},{16,20},{18,... | collective-permute-start | bytes 393224 | tf_op jit(solution)/shard_map/ppermute | solution.py:65
  4.1 1.0 %collective-permute-start.1 = (f32[2,128,128]{2,1,0:T(8,128)S(1)}, f32[2,128,128]{2,1,0:T(8,128)S(1)}, u32[]{:S(2)}, u32[]{:S(2)}) collective-permute-start(f32[2,128,128]{2,1,0:T(8,128)S(1)} %get-tuple-element.39), channel_id=1, source_target_pairs={{4,8},{6,10},{8,4},{10,6},{12,16},{14,18},{16,12},{18,14},{20,24},... | collective-permute-start | bytes 393224 | tf_op jit(solution)/shard_map/ppermute | solution.py:65
  5.0 0.0 copy-done
  5.0 0.0 copy-start.1
  5.0 0.0 copy-start.2
  5.0 0.5 %shard_map.141 = (f32[4,4,128]{2,1,0:T(4,128)S(1)}, f32[4,4,128]{2,1,0:T(4,128)S(1)}) custom-call(f32[4,128,128]{2,1,0:T(8,128)S(1)} %get-tuple-element.28.pv_ref.refs_0_, f32[4,128,128]{2,1,0:T(8,128)S(1)} %get-tuple-element.29.qv_ref.refs_1_, f32[3,4,128,128]{3,2,1,0:T(8,128)S(1)} %copy-done, f32[4,128,128]{2,1,0:T(8,128)S(1)} %get-tuple-element.32.refs_3_.refs_2_), custom_call_target="tpu_custom_call" | custom-call | flops 1000000 | bytes 1000000 | tf_op jit(solution)/shard_map/pallas_call | solution.py:20
  5.6 0.0 collective-permute-start.2
  5.6 1.3 %collective-permute-start.3 = (f32[4,4,128]{2,1,0:T(4,128)S(1)}, f32[4,4,128]{2,1,0:T(4,128)S(1)}, u32[]{:S(2)}, u32[]{:S(2)}) collective-permute-start(f32[4,4,128]{2,1,0:T(4,128)S(1)} %get-tuple-element.41), channel_id=1, source_target_pairs={{0,1},{1,0},{2,3},{3,2},{4,5},{5,4},{6,7},{7,6},{8,9},{9,8},{10,11... | collective-permute-start | bytes 24584 | tf_op jit(solution)/shard_map/ppermute | solution.py:61
  8.2 0.0 copy-done.1
  8.2 0.0 copy-done.2
  8.2 0.8 %shard_map.140 = (f32[3,4,128,128]{3,2,1,0:T(8,128)S(1)}, f32[3,4,128,128]{3,2,1,0:T(8,128)S(1)}, bf16[512,512]{1,0:T(8,128)(2,1)S(1)}, s32[1,512]{1,0:T(1,128)S...) custom-call(f32[4,128,128]{2,1,0:T(8,128)S(1)} %get-tuple-element.28.pv_ref.refs_0_, ...), custom_call_target="tpu_custom_call" | custom-call | flops 1000000 | bytes 1000000 | tf_op jit(solution)/shard_map/pallas_call | solution.py:20
  9.1 0.0 collective-permute-done.2.refs_10_.refs_3_
  9.1 0.0 collective-permute-done.3.refs_11_.refs_4_
  9.1 0.0 collective-permute-done.refs_8_
  9.1 0.0 collective-permute-done.1.refs_9_
  9.1 0.7 %shard_map.142 = (f32[3,4,128,128]{3,2,1,0:T(8,128)S(1)}, f32[3,4,128]{2,1,0:T(4,128)S(1)}, f32[128,128]{1,0:T(8,128)S(1)}, f32[128,128]{1,0:T(8,128)S(1)}) custom-call(f32[3,4,128,128]{3,2,1,0:T(8,128)S(1)} %get-tuple-element.30.refs_0_, f32[3,4,128,128]{3,2,1,0:T(8,128)S(1)} %get-tuple-element.31.refs_1_, ...), custom_call_target="tpu_custom_call" | custom-call | flops 1000000 | bytes 1000000 | tf_op jit(solution)/shard_map/pallas_call | solution.py:20
  9.8 2.7 %collective-permute-start.6 = (f32[3,4,128]{2,1,0:T(4,128)S(1)}, f32[3,4,128]{2,1,0:T(4,128)S(1)}, u32[]{:S(2)}, u32[]{:S(2)}) collective-permute-start(f32[3,4,128]{2,1,0:T(4,128)S(1)} %get-tuple-element.48), channel_id=1, source_target_pairs={{0,4},{4,0},{8,12},{12,8},{16,20},{20,16},{24,28},{28,24},{1,5},{5... | collective-permute-start | bytes 18440 | tf_op jit(solution)/shard_map/ppermute | solution.py:394
  12.6 0.1 collective-permute-start.4
  12.7 1.3 %collective-permute-start.5 = (f32[128,128]{1,0:T(8,128)S(1)}, f32[128,128]{1,0:T(8,128)S(1)}, u32[]{:S(2)}, u32[]{:S(2)}) collective-permute-start(f32[128,128]{1,0:T(8,128)S(1)} %get-tuple-element.46), channel_id=1, source_target_pairs={{4,8},{6,10},{8,4},{10,6},{12,16},{14,18},{16,12},{18,14},{20,24},... | collective-permute-start | bytes 196616 | tf_op jit(solution)/shard_map/ppermute | solution.py:65
  14.0 0.0 collective-permute-done.6
  14.0 1.3 %collective-permute-start.7 = (f32[6,4,128]{2,1,0:T(4,128)S(1)}, f32[6,4,128]{2,1,0:T(4,128)S(1)}, u32[]{:S(2)}, u32[]{:S(2)}) collective-permute-start(f32[6,4,128]{2,1,0:T(4,128)S(1)} %pad_maximum_fusion), channel_id=1, source_target_pairs={{0,8},{4,12},{8,0},{12,4},{16,24},{20,28},{24,16},{28,20},{1,9},{5... | collective-permute-start | bytes 36872 | tf_op jit(solution)/shard_map/ppermute | solution.py:394
  15.3 2.0 %collective-permute-done.7 = f32[6,4,128]{2,1,0:T(4,128)S(1)} collective-permute-done((f32[6,4,128]{2,1,0:T(4,128)S(1)}, f32[6,4,128]{2,1,0:T(4,128)S(1)}, u32[]{:S(2)}, u32[]{:S(2)}) %collective-permute-start.7) | collective-permute-done | bytes 12320 | tf_op jit(solution)/shard_map/ppermute | solution.py:394
  17.3 2.3 %collective-permute-start.8 = (f32[12,4,128]{2,1,0:T(4,128)S(1)}, f32[12,4,128]{2,1,0:T(4,128)S(1)}, u32[]{:S(2)}, u32[]{:S(2)}) collective-permute-start(f32[12,4,128]{2,1,0:T(4,128)S(1)} %constant_dynamic-update-slice_fusion.refs_0_), channel_id=1, source_target_pairs={{0,16},{4,20},{8,24},{12,28},{16,0},{20,4},{24,8},{28,12},{1,17},{... | collective-permute-start | bytes 73736 | tf_op jit(solution)/shard_map/ppermute | solution.py:394
  19.6 0.7 %shard_map.145.refs_1_ = f32[256,64]{1,0:T(8,128)S(1)} custom-call(f32[12,4,128]{2,1,0:T(4,128)S(1)} %constant_dynamic-update-slice_fusion.refs_0_), custom_call_target="tpu_custom_call" | custom-call | flops 1000000 | bytes 1000000 | tf_op jit(solution)/shard_map/pallas_call | solution.py:20
  20.3 0.6 %collective-permute-done.8.refs_0_ = f32[12,4,128]{2,1,0:T(4,128)S(1)} collective-permute-done((f32[12,4,128]{2,1,0:T(4,128)S(1)}, f32[12,4,128]{2,1,0:T(4,128)S(1)}, u32[]{:S(2)}, u32[]{:S(2)}) %collective-permute-start.8) | collective-permute-done | bytes 24608 | tf_op jit(solution)/shard_map/ppermute | solution.py:394
  20.9 0.8 %shard_map.146 = (f32[32,128]{1,0:T(8,128)S(1)}, f32[32,128]{1,0:T(8,128)S(1)}, f32[32,128]{1,0:T(8,128)S(1)}, f32[32,128]{1,0:T(8,128)S(1)}) custom-call(f32[12,4,128]{2,1,0:T(4,128)S(1)} %collective-permute-done.8.refs_0_, f32[256,64]{1,0:T(8,128)S(1)} %shard_map.145.refs_1_), custom_call_target="tpu_custom_call" | custom-call | flops 1000000 | bytes 1000000 | tf_op jit(solution)/shard_map/pallas_call | solution.py:20
  21.7 0.6 %collective-permute-start.9 = (f32[32,128]{1,0:T(8,128)S(1)}, f32[32,128]{1,0:T(8,128)S(1)}, u32[]{:S(2)}, u32[]{:S(2)}) collective-permute-start(f32[32,128]{1,0:T(8,128)S(1)} %get-tuple-element.50), channel_id=1, source_target_pairs={{0,1},{1,0},{2,3},{3,2},{4,5},{5,4},{6,7},{7,6},{8,9},{9,8},{10,11... | collective-permute-start | bytes 49160 | tf_op jit(solution)/shard_map/ppermute | solution.py:406
  22.2 4.6 %collective-permute-start.10 = (f32[32,128]{1,0:T(8,128)S(1)}, f32[32,128]{1,0:T(8,128)S(1)}, u32[]{:S(2)}, u32[]{:S(2)}) collective-permute-start(f32[32,128]{1,0:T(8,128)S(1)} %get-tuple-element.51), channel_id=1, source_target_pairs={{0,2},{1,3},{2,0},{3,1},{4,6},{5,7},{6,4},{7,5},{8,10},{9,11},{10,... | collective-permute-start | bytes 49160 | tf_op jit(solution)/shard_map/ppermute | solution.py:406
  26.8 0.1 collective-permute-start.11
  26.9 1.1 %shard_map.143 = (f32[4,128,128]{2,1,0:T(8,128)S(1)}, f32[3,4,128,128]{3,2,1,0:T(8,128)}) custom-call(f32[3,4,128,128]{3,2,1,0:T(8,128)S(1)} %get-tuple-element.42.refs_0_, f32[4,128,128]{2,1,0:T(8,128)S(1)} %get-tuple-element.29.qv_ref.refs_1_, f32[4,128,128]{2,1,0:T(8,128)S(1)} %get-tuple-element.43.refs_2_, ...), custom_call_target="tpu_custom_call" | custom-call | flops 1000000 | bytes 1000000 | tf_op jit(solution)/shard_map/pallas_call | solution.py:20
  28.1 0.0 collective-permute-done.9.refs_1_
  28.1 0.0 collective-permute-done.10.refs_2_
  28.1 1.9 %collective-permute-done.11.refs_3_ = f32[32,128]{1,0:T(8,128)S(1)} collective-permute-done((f32[32,128]{1,0:T(8,128)S(1)}, f32[32,128]{1,0:T(8,128)S(1)}, u32[]{:S(2)}, u32[]{:S(2)}) %collective-permute-start.11) | collective-permute-done | bytes 16416 | tf_op jit(solution)/shard_map/ppermute | solution.py:406
  30.0 0.7 %shard_map.147 = f32[64,64]{1,0:T(8,128)} custom-call(f32[32,128]{1,0:T(8,128)S(1)} %get-tuple-element.49.refs_0_, f32[32,128]{1,0:T(8,128)S(1)} %collective-permute-done.9.refs_1_, f32[32,128]{1,0:T(8,128)S(1)} %collective-permute-done.10.refs_2_, f32[32,128]{1,0:T(8,128)S(1)} %collective-permute-done.11.refs_3_), custom_call_target="tpu_custom_call" | custom-call | flops 1000000 | bytes 1000000 | tf_op jit(solution)/shard_map/pallas_call | solution.py:20
  30.7 0.0 collective-permute-done.4.refs_1_
  30.7 0.0 collective-permute-done.5.refs_2_
  30.7 0.7 %shard_map.144 = f32[4,128,128]{2,1,0:T(8,128)} custom-call(f32[4,128,128]{2,1,0:T(8,128)S(1)} %get-tuple-element.44.refs_0_, f32[128,128]{1,0:T(8,128)S(1)} %collective-permute-done.4.refs_1_, f32[128,128]{1,0:T(8,128)S(1)} %collective-permute-done.5.refs_2_), custom_call_target="tpu_custom_call" | custom-call | flops 1000000 | bytes 1000000 | tf_op jit(solution)/shard_map/pallas_call | solution.py:20
  (4 shorter events, 0.0 us)
Async XLA Ops:
  0.6 4.4 %copy-start = (f32[3,4,128,128]{3,2,1,0:T(8,128)S(1)}, f32[3,4,128,128]{3,2,1,0:T(8,128)}, u32[]{:S(2)}) copy-start(f32[3,4,128,128]{3,2,1,0:T(8,128)} %refs_2_.3) | copy-start | bytes 2359300
  2.0 7.1 %collective-permute-start = (f32[2,128,128]{2,1,0:T(8,128)S(1)}, f32[2,128,128]{2,1,0:T(8,128)S(1)}, u32[]{:S(2)}, u32[]{:S(2)}) collective-permute-start(f32[2,128,128]{2,1,0:T(8,128)S(1)} %get-tuple-element.38), channel_id=1, source_target_pairs={{0,4},{2,6},{4,0},{6,2},{8,12},{10,14},{12,8},{14,10},{16,20},{18,... | collective-permute-start | bytes 393224 | tf_op jit(solution)/shard_map/ppermute | solution.py:65
  4.1 5.0 %collective-permute-start.1 = (f32[2,128,128]{2,1,0:T(8,128)S(1)}, f32[2,128,128]{2,1,0:T(8,128)S(1)}, u32[]{:S(2)}, u32[]{:S(2)}) collective-permute-start(f32[2,128,128]{2,1,0:T(8,128)S(1)} %get-tuple-element.39), channel_id=1, source_target_pairs={{4,8},{6,10},{8,4},{10,6},{12,16},{14,18},{16,12},{18,14},{20,24},... | collective-permute-start | bytes 393224 | tf_op jit(solution)/shard_map/ppermute | solution.py:65
  5.0 3.2 %copy-start.1 = (f32[3,4,128,128]{3,2,1,0:T(8,128)S(1)}, f32[3,4,128,128]{3,2,1,0:T(8,128)}, u32[]{:S(2)}) copy-start(f32[3,4,128,128]{3,2,1,0:T(8,128)} %v_ref.1) | copy-start | bytes 2359300
  5.0 3.2 %copy-start.2 = (f32[4,128,128]{2,1,0:T(8,128)S(1)}, f32[4,128,128]{2,1,0:T(8,128)}, u32[]{:S(2)}) copy-start(f32[4,128,128]{2,1,0:T(8,128)} %d_ref.1) | copy-start | bytes 786436
  5.6 3.5 %collective-permute-start.2 = (f32[4,4,128]{2,1,0:T(4,128)S(1)}, f32[4,4,128]{2,1,0:T(4,128)S(1)}, u32[]{:S(2)}, u32[]{:S(2)}) collective-permute-start(f32[4,4,128]{2,1,0:T(4,128)S(1)} %get-tuple-element.40), channel_id=1, source_target_pairs={{0,2},{2,0},{1,3},{3,1},{4,6},{6,4},{5,7},{7,5},{8,10},{10,8},{9,1... | collective-permute-start | bytes 24584 | tf_op jit(solution)/shard_map/ppermute | solution.py:61
  5.6 3.5 %collective-permute-start.3 = (f32[4,4,128]{2,1,0:T(4,128)S(1)}, f32[4,4,128]{2,1,0:T(4,128)S(1)}, u32[]{:S(2)}, u32[]{:S(2)}) collective-permute-start(f32[4,4,128]{2,1,0:T(4,128)S(1)} %get-tuple-element.41), channel_id=1, source_target_pairs={{0,1},{1,0},{2,3},{3,2},{4,5},{5,4},{6,7},{7,6},{8,9},{9,8},{10,11... | collective-permute-start | bytes 24584 | tf_op jit(solution)/shard_map/ppermute | solution.py:61
  9.8 4.1 %collective-permute-start.6 = (f32[3,4,128]{2,1,0:T(4,128)S(1)}, f32[3,4,128]{2,1,0:T(4,128)S(1)}, u32[]{:S(2)}, u32[]{:S(2)}) collective-permute-start(f32[3,4,128]{2,1,0:T(4,128)S(1)} %get-tuple-element.48), channel_id=1, source_target_pairs={{0,4},{4,0},{8,12},{12,8},{16,20},{20,16},{24,28},{28,24},{1,5},{5... | collective-permute-start | bytes 18440 | tf_op jit(solution)/shard_map/ppermute | solution.py:394
  12.6 18.1 %collective-permute-start.4 = (f32[128,128]{1,0:T(8,128)S(1)}, f32[128,128]{1,0:T(8,128)S(1)}, u32[]{:S(2)}, u32[]{:S(2)}) collective-permute-start(f32[128,128]{1,0:T(8,128)S(1)} %get-tuple-element.45), channel_id=1, source_target_pairs={{0,4},{2,6},{4,0},{6,2},{8,12},{10,14},{12,8},{14,10},{16,20},{18,... | collective-permute-start | bytes 196616 | tf_op jit(solution)/shard_map/ppermute | solution.py:65
  12.7 18.0 %collective-permute-start.5 = (f32[128,128]{1,0:T(8,128)S(1)}, f32[128,128]{1,0:T(8,128)S(1)}, u32[]{:S(2)}, u32[]{:S(2)}) collective-permute-start(f32[128,128]{1,0:T(8,128)S(1)} %get-tuple-element.46), channel_id=1, source_target_pairs={{4,8},{6,10},{8,4},{10,6},{12,16},{14,18},{16,12},{18,14},{20,24},... | collective-permute-start | bytes 196616 | tf_op jit(solution)/shard_map/ppermute | solution.py:65
  14.0 3.3 %collective-permute-start.7 = (f32[6,4,128]{2,1,0:T(4,128)S(1)}, f32[6,4,128]{2,1,0:T(4,128)S(1)}, u32[]{:S(2)}, u32[]{:S(2)}) collective-permute-start(f32[6,4,128]{2,1,0:T(4,128)S(1)} %pad_maximum_fusion), channel_id=1, source_target_pairs={{0,8},{4,12},{8,0},{12,4},{16,24},{20,28},{24,16},{28,20},{1,9},{5... | collective-permute-start | bytes 36872 | tf_op jit(solution)/shard_map/ppermute | solution.py:394
  17.3 3.6 %collective-permute-start.8 = (f32[12,4,128]{2,1,0:T(4,128)S(1)}, f32[12,4,128]{2,1,0:T(4,128)S(1)}, u32[]{:S(2)}, u32[]{:S(2)}) collective-permute-start(f32[12,4,128]{2,1,0:T(4,128)S(1)} %constant_dynamic-update-slice_fusion.refs_0_), channel_id=1, source_target_pairs={{0,16},{4,20},{8,24},{12,28},{16,0},{20,4},{24,8},{28,12},{1,17},{... | collective-permute-start | bytes 73736 | tf_op jit(solution)/shard_map/ppermute | solution.py:394
  21.7 6.4 %collective-permute-start.9 = (f32[32,128]{1,0:T(8,128)S(1)}, f32[32,128]{1,0:T(8,128)S(1)}, u32[]{:S(2)}, u32[]{:S(2)}) collective-permute-start(f32[32,128]{1,0:T(8,128)S(1)} %get-tuple-element.50), channel_id=1, source_target_pairs={{0,1},{1,0},{2,3},{3,2},{4,5},{5,4},{6,7},{7,6},{8,9},{9,8},{10,11... | collective-permute-start | bytes 49160 | tf_op jit(solution)/shard_map/ppermute | solution.py:406
  22.2 5.8 %collective-permute-start.10 = (f32[32,128]{1,0:T(8,128)S(1)}, f32[32,128]{1,0:T(8,128)S(1)}, u32[]{:S(2)}, u32[]{:S(2)}) collective-permute-start(f32[32,128]{1,0:T(8,128)S(1)} %get-tuple-element.51), channel_id=1, source_target_pairs={{0,2},{1,3},{2,0},{3,1},{4,6},{5,7},{6,4},{7,5},{8,10},{9,11},{10,... | collective-permute-start | bytes 49160 | tf_op jit(solution)/shard_map/ppermute | solution.py:406
  26.8 3.2 %collective-permute-start.11 = (f32[32,128]{1,0:T(8,128)S(1)}, f32[32,128]{1,0:T(8,128)S(1)}, u32[]{:S(2)}, u32[]{:S(2)}) collective-permute-start(f32[32,128]{1,0:T(8,128)S(1)} %get-tuple-element.52), channel_id=1, source_target_pairs={{0,3},{1,2},{2,1},{3,0},{4,7},{5,6},{6,5},{7,4},{8,11},{9,10},{10,... | collective-permute-start | bytes 49160 | tf_op jit(solution)/shard_map/ppermute | solution.py:406

commit v6 on v5

--- a/solution.py
+++ b/solution.py
@@ -387,16 +387,21 @@
     )
 
 
+def rounds_of_partners(count):
+    bits = count.bit_length() - 1
+    return [[d << low for d in range(1, 1 << min(2, bits - low))] for low in range(0, bits, 2)]
+
+
 def share_and_add(slots, axis, block, group):
     count = lax.axis_size(axis)
-    have = slots
-    for k in range(count.bit_length() - 1):
-        got = lax.ppermute(have, axis, [(i, i ^ (1 << k)) for i in range(count)])
-        if 2 << k < count:
-            have = jnp.concatenate([have, got], axis=0)
-        else:
-            total = dense(block, None, (have,))
-            return dense(block, group, (got,), total)
+    have, got = [slots], []
+    for partners in rounds_of_partners(count):
+        joined = jnp.concatenate(have + got, axis=0)
+        have, got = [joined], []
+        for d in partners:
+            got.append(lax.ppermute(joined, axis, [(i, i ^ d) for i in range(count)]))
+    total = dense(block, None, have)
+    return dense(block, group, got, total)
 
 
 def collect(sums, group):

time: 31.6 us -> 31.1 us (0.984)
  waiting for transfers between devices: 4.47 us -> 3.75 us
    ppermute x4, starting transfers between devices: 4.45 us -> 6.47 us  [swap(): return lax.ppermute(message, (axis, 'row'), both)]
    ppermute x3, starting transfers between devices: 5.27 us -> 4.19 us  [collect(): lax.ppermute(sums[i], group, [(j, j ^ i) for j in range(count)])]
    ppermute x3 -> x4, waiting for transfers between devices: 2.58 us -> 1.72 us  [share_and_add(): got.append(lax.ppermute(joined, axis, [(i, i ^ d) for i in range(count)]))]
    ppermute x3 -> x4, starting transfers between devices: 6.4 us -> 5.67 us  [share_and_add(): got.append(lax.ppermute(joined, axis, [(i, i ^ d) for i in range(count)]))]
  transfers between devices with their start and end apart: 12 -> 13, of which waited for: 3 -> 2; matrix products, arithmetic and copies ran while one was open for 0% -> 0% of each run, Pallas kernels for 15% -> 15%
where the time goes in v6:
time: 31.1 us; the launch traced here: 30.9 us
  starting transfers between devices  17.7 us (57%)
  Pallas kernels  7.4 us (24%)
  waiting for transfers between devices  3.75 us (12%)
  between operations  2.07 us (7%)
    pallas_call x9, Pallas kernels, call(): pl.pallas_call(body, out_shape=outs, in_specs=specs, out_specs=jax.tree.m...  7.4 us
    ppermute x4, starting transfers between devices, swap(): return lax.ppermute(message, (axis, 'row'), both)  6.47 us
    ppermute x4, starting transfers between devices, share_and_add(): got.append(lax.ppermute(joined, axis, [(i, i ^ d) for i in range(count)]))  5.67 us
    ppermute x3, starting transfers between devices, collect(): lax.ppermute(sums[i], group, [(j, j ^ i) for j in range(count)])  4.19 us
    ppermute x3, waiting for transfers between devices, collect(): lax.ppermute(sums[i], group, [(j, j ^ i) for j in range(count)])  2.02 us
    ppermute x4, waiting for transfers between devices, share_and_add(): got.append(lax.ppermute(joined, axis, [(i, i ^ d) for i in range(count)]))  1.72 us
    ppermute x2, starting transfers between devices, swap(): return lax.ppermute(message, axis, pairs)  1.32 us
  transfers between devices with their start and end apart: 13, of which 2 were waited for; matrix products, arithmetic and copies ran while one was open for 0% of the time, Pallas kernels for 15%

profile of v6, /device:TPU:1, one launch (start us, length us, event | category | flops | bytes accessed | tf_op | source)
XLA Modules:
  0.0 30.9 jit_solution(9854747305903239596)
XLA Ops:
  0.6 0.0 copy-start
  0.6 1.3 %shard_map.139 = (f32[2,128,128]{2,1,0:T(8,128)S(1)}, f32[2,128,128]{2,1,0:T(8,128)S(1)}, f32[4,128,128]{2,1,0:T(8,128)S(1)}, f32[4,128,128]{2,1,0:T(8,128)S(1)}...) custom-call(f32[4,128,128]{2,1,0:T(8,128)} %refs_0_.1, f32[4,128,128]{2,1,0:T(8,128)} %refs_1_.1, ...), custom_call_target="tpu_custom_call" | custom-call | flops 1000000 | bytes 1000000 | tf_op jit(solution)/shard_map/pallas_call | solution.py:20
  2.0 2.1 %collective-permute-start = (f32[2,128,128]{2,1,0:T(8,128)S(1)}, f32[2,128,128]{2,1,0:T(8,128)S(1)}, u32[]{:S(2)}, u32[]{:S(2)}) collective-permute-start(f32[2,128,128]{2,1,0:T(8,128)S(1)} %get-tuple-element.38), channel_id=1, source_target_pairs={{0,4},{2,6},{4,0},{6,2},{8,12},{10,14},{12,8},{14,10},{16,20},{18,... | collective-permute-start | bytes 393224 | tf_op jit(solution)/shard_map/ppermute | solution.py:65
  4.1 1.0 %collective-permute-start.1 = (f32[2,128,128]{2,1,0:T(8,128)S(1)}, f32[2,128,128]{2,1,0:T(8,128)S(1)}, u32[]{:S(2)}, u32[]{:S(2)}) collective-permute-start(f32[2,128,128]{2,1,0:T(8,128)S(1)} %get-tuple-element.39), channel_id=1, source_target_pairs={{4,8},{6,10},{8,4},{10,6},{12,16},{14,18},{16,12},{18,14},{20,24},... | collective-permute-start | bytes 393224 | tf_op jit(solution)/shard_map/ppermute | solution.py:65
  5.0 0.0 copy-done
  5.0 0.0 copy-start.1
  5.0 0.0 copy-start.2
  5.0 0.5 %shard_map.141 = (f32[4,4,128]{2,1,0:T(4,128)S(1)}, f32[4,4,128]{2,1,0:T(4,128)S(1)}) custom-call(f32[4,128,128]{2,1,0:T(8,128)S(1)} %get-tuple-element.28.pv_ref.refs_0_, f32[4,128,128]{2,1,0:T(8,128)S(1)} %get-tuple-element.29.qv_ref.refs_1_, f32[3,4,128,128]{3,2,1,0:T(8,128)S(1)} %copy-done, f32[4,128,128]{2,1,0:T(8,128)S(1)} %get-tuple-element.32.refs_3_.refs_2_), custom_call_target="tpu_custom_call" | custom-call | flops 1000000 | bytes 1000000 | tf_op jit(solution)/shard_map/pallas_call | solution.py:20
  5.6 0.0 collective-permute-start.2
  5.6 1.3 %collective-permute-start.3 = (f32[4,4,128]{2,1,0:T(4,128)S(1)}, f32[4,4,128]{2,1,0:T(4,128)S(1)}, u32[]{:S(2)}, u32[]{:S(2)}) collective-permute-start(f32[4,4,128]{2,1,0:T(4,128)S(1)} %get-tuple-element.41), channel_id=1, source_target_pairs={{0,1},{1,0},{2,3},{3,2},{4,5},{5,4},{6,7},{7,6},{8,9},{9,8},{10,11... | collective-permute-start | bytes 24584 | tf_op jit(solution)/shard_map/ppermute | solution.py:61
  8.2 0.0 copy-done.1
  8.2 0.0 copy-done.2
  8.2 0.8 %shard_map.140 = (f32[3,4,128,128]{3,2,1,0:T(8,128)S(1)}, f32[3,4,128,128]{3,2,1,0:T(8,128)S(1)}, bf16[512,512]{1,0:T(8,128)(2,1)S(1)}, s32[1,512]{1,0:T(1,128)S...) custom-call(f32[4,128,128]{2,1,0:T(8,128)S(1)} %get-tuple-element.28.pv_ref.refs_0_, ...), custom_call_target="tpu_custom_call" | custom-call | flops 1000000 | bytes 1000000 | tf_op jit(solution)/shard_map/pallas_call | solution.py:20
  9.1 0.0 collective-permute-done.2.refs_10_.refs_3_
  9.1 0.0 collective-permute-done.3.refs_11_.refs_4_
  9.1 0.0 collective-permute-done.refs_8_
  9.1 0.0 collective-permute-done.1.refs_9_
  9.1 0.7 %shard_map.142 = (f32[3,4,128,128]{3,2,1,0:T(8,128)S(1)}, f32[3,4,128]{2,1,0:T(4,128)S(1)}, f32[128,128]{1,0:T(8,128)S(1)}, f32[128,128]{1,0:T(8,128)S(1)}) custom-call(f32[3,4,128,128]{3,2,1,0:T(8,128)S(1)} %get-tuple-element.30.refs_0_, f32[3,4,128,128]{3,2,1,0:T(8,128)S(1)} %get-tuple-element.31.refs_1_, ...), custom_call_target="tpu_custom_call" | custom-call | flops 1000000 | bytes 1000000 | tf_op jit(solution)/shard_map/pallas_call | solution.py:20
  9.8 3.8 %collective-permute-start.8 = (f32[3,4,128]{2,1,0:T(4,128)S(1)}, f32[3,4,128]{2,1,0:T(4,128)S(1)}, u32[]{:S(2)}, u32[]{:S(2)}) collective-permute-start(f32[3,4,128]{2,1,0:T(4,128)S(1)} %get-tuple-element.48), channel_id=1, source_target_pairs={{0,12},{4,8},{8,4},{12,0},{16,28},{20,24},{24,20},{28,16},{1,13},{... | collective-permute-start | bytes 18440 | tf_op jit(solution)/shard_map/ppermute | solution.py:402
  13.6 0.2 collective-permute-start.7
  13.8 0.2 collective-permute-start.6
  14.0 1.3 %collective-permute-start.4 = (f32[128,128]{1,0:T(8,128)S(1)}, f32[128,128]{1,0:T(8,128)S(1)}, u32[]{:S(2)}, u32[]{:S(2)}) collective-permute-start(f32[128,128]{1,0:T(8,128)S(1)} %get-tuple-element.45), channel_id=1, source_target_pairs={{0,4},{2,6},{4,0},{6,2},{8,12},{10,14},{12,8},{14,10},{16,20},{18,... | collective-permute-start | bytes 196616 | tf_op jit(solution)/shard_map/ppermute | solution.py:65
  15.2 2.1 %collective-permute-start.5 = (f32[128,128]{1,0:T(8,128)S(1)}, f32[128,128]{1,0:T(8,128)S(1)}, u32[]{:S(2)}, u32[]{:S(2)}) collective-permute-start(f32[128,128]{1,0:T(8,128)S(1)} %get-tuple-element.46), channel_id=1, source_target_pairs={{4,8},{6,10},{8,4},{10,6},{12,16},{14,18},{16,12},{18,14},{20,24},... | collective-permute-start | bytes 196616 | tf_op jit(solution)/shard_map/ppermute | solution.py:65
  17.4 0.0 collective-permute-done.6
  17.4 0.0 collective-permute-done.7
  17.4 0.0 collective-permute-done.8
  17.4 1.6 %collective-permute-start.9 = (f32[12,4,128]{2,1,0:T(4,128)S(1)}, f32[12,4,128]{2,1,0:T(4,128)S(1)}, u32[]{:S(2)}, u32[]{:S(2)}) collective-permute-start(f32[12,4,128]{2,1,0:T(4,128)S(1)} %constant_dynamic-update-slice_fusion.refs_0_), channel_id=1, source_target_pairs={{0,16},{4,20},{8,24},{12,28},{16,0},{20,4},{24,8},{28,12},{1,17},{... | collective-permute-start | bytes 73736 | tf_op jit(solution)/shard_map/ppermute | solution.py:402
  19.0 0.7 %shard_map.145.refs_1_ = f32[256,64]{1,0:T(8,128)S(1)} custom-call(f32[12,4,128]{2,1,0:T(4,128)S(1)} %constant_dynamic-update-slice_fusion.refs_0_), custom_call_target="tpu_custom_call" | custom-call | flops 1000000 | bytes 1000000 | tf_op jit(solution)/shard_map/pallas_call | solution.py:20
  19.7 1.7 %collective-permute-done.9.refs_0_ = f32[12,4,128]{2,1,0:T(4,128)S(1)} collective-permute-done((f32[12,4,128]{2,1,0:T(4,128)S(1)}, f32[12,4,128]{2,1,0:T(4,128)S(1)}, u32[]{:S(2)}, u32[]{:S(2)}) %collective-permute-start.9) | collective-permute-done | bytes 24608 | tf_op jit(solution)/shard_map/ppermute | solution.py:402
  21.4 0.8 %shard_map.146 = (f32[32,128]{1,0:T(8,128)S(1)}, f32[32,128]{1,0:T(8,128)S(1)}, f32[32,128]{1,0:T(8,128)S(1)}, f32[32,128]{1,0:T(8,128)S(1)}) custom-call(f32[12,4,128]{2,1,0:T(4,128)S(1)} %collective-permute-done.9.refs_0_, f32[256,64]{1,0:T(8,128)S(1)} %shard_map.145.refs_1_), custom_call_target="tpu_custom_call" | custom-call | flops 1000000 | bytes 1000000 | tf_op jit(solution)/shard_map/pallas_call | solution.py:20
  22.1 1.0 %collective-permute-start.10 = (f32[32,128]{1,0:T(8,128)S(1)}, f32[32,128]{1,0:T(8,128)S(1)}, u32[]{:S(2)}, u32[]{:S(2)}) collective-permute-start(f32[32,128]{1,0:T(8,128)S(1)} %get-tuple-element.50), channel_id=1, source_target_pairs={{0,1},{1,0},{2,3},{3,2},{4,5},{5,4},{6,7},{7,6},{8,9},{9,8},{10,11... | collective-permute-start | bytes 49160 | tf_op jit(solution)/shard_map/ppermute | solution.py:411
  23.1 3.2 %collective-permute-start.11 = (f32[32,128]{1,0:T(8,128)S(1)}, f32[32,128]{1,0:T(8,128)S(1)}, u32[]{:S(2)}, u32[]{:S(2)}) collective-permute-start(f32[32,128]{1,0:T(8,128)S(1)} %get-tuple-element.51), channel_id=1, source_target_pairs={{0,2},{1,3},{2,0},{3,1},{4,6},{5,7},{6,4},{7,5},{8,10},{9,11},{10,... | collective-permute-start | bytes 49160 | tf_op jit(solution)/shard_map/ppermute | solution.py:411
  26.3 0.0 collective-permute-start.12
  26.3 1.1 %shard_map.143 = (f32[4,128,128]{2,1,0:T(8,128)S(1)}, f32[3,4,128,128]{3,2,1,0:T(8,128)}) custom-call(f32[3,4,128,128]{3,2,1,0:T(8,128)S(1)} %get-tuple-element.42.refs_0_, f32[4,128,128]{2,1,0:T(8,128)S(1)} %get-tuple-element.29.qv_ref.refs_1_, f32[4,128,128]{2,1,0:T(8,128)S(1)} %get-tuple-element.43.refs_2_, ...), custom_call_target="tpu_custom_call" | custom-call | flops 1000000 | bytes 1000000 | tf_op jit(solution)/shard_map/pallas_call | solution.py:20
  27.4 0.0 collective-permute-done.10.refs_1_
  27.5 0.0 collective-permute-done.11.refs_2_
  27.5 2.0 %collective-permute-done.12.refs_3_ = f32[32,128]{1,0:T(8,128)S(1)} collective-permute-done((f32[32,128]{1,0:T(8,128)S(1)}, f32[32,128]{1,0:T(8,128)S(1)}, u32[]{:S(2)}, u32[]{:S(2)}) %collective-permute-start.12) | collective-permute-done | bytes 16416 | tf_op jit(solution)/shard_map/ppermute | solution.py:411
  29.5 0.7 %shard_map.147 = f32[64,64]{1,0:T(8,128)} custom-call(f32[32,128]{1,0:T(8,128)S(1)} %get-tuple-element.49.refs_0_, f32[32,128]{1,0:T(8,128)S(1)} %collective-permute-done.10.refs_1_, f32[32,128]{1,0:T(8,128)S(1)} %collective-permute-done.11.refs_2_, f32[32,128]{1,0:T(8,128)S(1)} %collective-permute-done.12.refs_3_), custom_call_target="tpu_custom_call" | custom-call | flops 1000000 | bytes 1000000 | tf_op jit(solution)/shard_map/pallas_call | solution.py:20
  30.2 0.0 collective-permute-done.4.refs_1_
  30.2 0.0 collective-permute-done.5.refs_2_
  30.2 0.7 %shard_map.144 = f32[4,128,128]{2,1,0:T(8,128)} custom-call(f32[4,128,128]{2,1,0:T(8,128)S(1)} %get-tuple-element.44.refs_0_, f32[128,128]{1,0:T(8,128)S(1)} %collective-permute-done.4.refs_1_, f32[128,128]{1,0:T(8,128)S(1)} %collective-permute-done.5.refs_2_), custom_call_target="tpu_custom_call" | custom-call | flops 1000000 | bytes 1000000 | tf_op jit(solution)/shard_map/pallas_call | solution.py:20
  (4 shorter events, 0.0 us)
Async XLA Ops:
  0.6 4.4 %copy-start = (f32[3,4,128,128]{3,2,1,0:T(8,128)S(1)}, f32[3,4,128,128]{3,2,1,0:T(8,128)}, u32[]{:S(2)}) copy-start(f32[3,4,128,128]{3,2,1,0:T(8,128)} %refs_2_.3) | copy-start | bytes 2359300
  2.0 7.1 %collective-permute-start = (f32[2,128,128]{2,1,0:T(8,128)S(1)}, f32[2,128,128]{2,1,0:T(8,128)S(1)}, u32[]{:S(2)}, u32[]{:S(2)}) collective-permute-start(f32[2,128,128]{2,1,0:T(8,128)S(1)} %get-tuple-element.38), channel_id=1, source_target_pairs={{0,4},{2,6},{4,0},{6,2},{8,12},{10,14},{12,8},{14,10},{16,20},{18,... | collective-permute-start | bytes 393224 | tf_op jit(solution)/shard_map/ppermute | solution.py:65
  4.1 5.0 %collective-permute-start.1 = (f32[2,128,128]{2,1,0:T(8,128)S(1)}, f32[2,128,128]{2,1,0:T(8,128)S(1)}, u32[]{:S(2)}, u32[]{:S(2)}) collective-permute-start(f32[2,128,128]{2,1,0:T(8,128)S(1)} %get-tuple-element.39), channel_id=1, source_target_pairs={{4,8},{6,10},{8,4},{10,6},{12,16},{14,18},{16,12},{18,14},{20,24},... | collective-permute-start | bytes 393224 | tf_op jit(solution)/shard_map/ppermute | solution.py:65
  5.0 3.2 %copy-start.1 = (f32[3,4,128,128]{3,2,1,0:T(8,128)S(1)}, f32[3,4,128,128]{3,2,1,0:T(8,128)}, u32[]{:S(2)}) copy-start(f32[3,4,128,128]{3,2,1,0:T(8,128)} %v_ref.1) | copy-start | bytes 2359300
  5.0 3.2 %copy-start.2 = (f32[4,128,128]{2,1,0:T(8,128)S(1)}, f32[4,128,128]{2,1,0:T(8,128)}, u32[]{:S(2)}) copy-start(f32[4,128,128]{2,1,0:T(8,128)} %d_ref.1) | copy-start | bytes 786436
  5.6 3.5 %collective-permute-start.2 = (f32[4,4,128]{2,1,0:T(4,128)S(1)}, f32[4,4,128]{2,1,0:T(4,128)S(1)}, u32[]{:S(2)}, u32[]{:S(2)}) collective-permute-start(f32[4,4,128]{2,1,0:T(4,128)S(1)} %get-tuple-element.40), channel_id=1, source_target_pairs={{0,2},{2,0},{1,3},{3,1},{4,6},{6,4},{5,7},{7,5},{8,10},{10,8},{9,1... | collective-permute-start | bytes 24584 | tf_op jit(solution)/shard_map/ppermute | solution.py:61
  5.6 3.5 %collective-permute-start.3 = (f32[4,4,128]{2,1,0:T(4,128)S(1)}, f32[4,4,128]{2,1,0:T(4,128)S(1)}, u32[]{:S(2)}, u32[]{:S(2)}) collective-permute-start(f32[4,4,128]{2,1,0:T(4,128)S(1)} %get-tuple-element.41), channel_id=1, source_target_pairs={{0,1},{1,0},{2,3},{3,2},{4,5},{5,4},{6,7},{7,6},{8,9},{9,8},{10,11... | collective-permute-start | bytes 24584 | tf_op jit(solution)/shard_map/ppermute | solution.py:61
  9.8 7.5 %collective-permute-start.8 = (f32[3,4,128]{2,1,0:T(4,128)S(1)}, f32[3,4,128]{2,1,0:T(4,128)S(1)}, u32[]{:S(2)}, u32[]{:S(2)}) collective-permute-start(f32[3,4,128]{2,1,0:T(4,128)S(1)} %get-tuple-element.48), channel_id=1, source_target_pairs={{0,12},{4,8},{8,4},{12,0},{16,28},{20,24},{24,20},{28,16},{1,13},{... | collective-permute-start | bytes 18440 | tf_op jit(solution)/shard_map/ppermute | solution.py:402
  13.6 3.8 %collective-permute-start.7 = (f32[3,4,128]{2,1,0:T(4,128)S(1)}, f32[3,4,128]{2,1,0:T(4,128)S(1)}, u32[]{:S(2)}, u32[]{:S(2)}) collective-permute-start(f32[3,4,128]{2,1,0:T(4,128)S(1)} %get-tuple-element.48), channel_id=1, source_target_pairs={{0,8},{4,12},{8,0},{12,4},{16,24},{20,28},{24,16},{28,20},{1,9},{5... | collective-permute-start | bytes 18440 | tf_op jit(solution)/shard_map/ppermute | solution.py:402
  13.8 3.6 %collective-permute-start.6 = (f32[3,4,128]{2,1,0:T(4,128)S(1)}, f32[3,4,128]{2,1,0:T(4,128)S(1)}, u32[]{:S(2)}, u32[]{:S(2)}) collective-permute-start(f32[3,4,128]{2,1,0:T(4,128)S(1)} %get-tuple-element.48), channel_id=1, source_target_pairs={{0,4},{4,0},{8,12},{12,8},{16,20},{20,16},{24,28},{28,24},{1,5},{5... | collective-permute-start | bytes 18440 | tf_op jit(solution)/shard_map/ppermute | solution.py:402
  14.0 16.2 %collective-permute-start.4 = (f32[128,128]{1,0:T(8,128)S(1)}, f32[128,128]{1,0:T(8,128)S(1)}, u32[]{:S(2)}, u32[]{:S(2)}) collective-permute-start(f32[128,128]{1,0:T(8,128)S(1)} %get-tuple-element.45), channel_id=1, source_target_pairs={{0,4},{2,6},{4,0},{6,2},{8,12},{10,14},{12,8},{14,10},{16,20},{18,... | collective-permute-start | bytes 196616 | tf_op jit(solution)/shard_map/ppermute | solution.py:65
  15.2 14.9 %collective-permute-start.5 = (f32[128,128]{1,0:T(8,128)S(1)}, f32[128,128]{1,0:T(8,128)S(1)}, u32[]{:S(2)}, u32[]{:S(2)}) collective-permute-start(f32[128,128]{1,0:T(8,128)S(1)} %get-tuple-element.46), channel_id=1, source_target_pairs={{4,8},{6,10},{8,4},{10,6},{12,16},{14,18},{16,12},{18,14},{20,24},... | collective-permute-start | bytes 196616 | tf_op jit(solution)/shard_map/ppermute | solution.py:65
  17.4 3.9 %collective-permute-start.9 = (f32[12,4,128]{2,1,0:T(4,128)S(1)}, f32[12,4,128]{2,1,0:T(4,128)S(1)}, u32[]{:S(2)}, u32[]{:S(2)}) collective-permute-start(f32[12,4,128]{2,1,0:T(4,128)S(1)} %constant_dynamic-update-slice_fusion.refs_0_), channel_id=1, source_target_pairs={{0,16},{4,20},{8,24},{12,28},{16,0},{20,4},{24,8},{28,12},{1,17},{... | collective-permute-start | bytes 73736 | tf_op jit(solution)/shard_map/ppermute | solution.py:402
  22.1 5.3 %collective-permute-start.10 = (f32[32,128]{1,0:T(8,128)S(1)}, f32[32,128]{1,0:T(8,128)S(1)}, u32[]{:S(2)}, u32[]{:S(2)}) collective-permute-start(f32[32,128]{1,0:T(8,128)S(1)} %get-tuple-element.50), channel_id=1, source_target_pairs={{0,1},{1,0},{2,3},{3,2},{4,5},{5,4},{6,7},{7,6},{8,9},{9,8},{10,11... | collective-permute-start | bytes 49160 | tf_op jit(solution)/shard_map/ppermute | solution.py:411
  23.1 4.4 %collective-permute-start.11 = (f32[32,128]{1,0:T(8,128)S(1)}, f32[32,128]{1,0:T(8,128)S(1)}, u32[]{:S(2)}, u32[]{:S(2)}) collective-permute-start(f32[32,128]{1,0:T(8,128)S(1)} %get-tuple-element.51), channel_id=1, source_target_pairs={{0,2},{1,3},{2,0},{3,1},{4,6},{5,7},{6,4},{7,5},{8,10},{9,11},{10,... | collective-permute-start | bytes 49160 | tf_op jit(solution)/shard_map/ppermute | solution.py:411
  26.3 3.2 %collective-permute-start.12 = (f32[32,128]{1,0:T(8,128)S(1)}, f32[32,128]{1,0:T(8,128)S(1)}, u32[]{:S(2)}, u32[]{:S(2)}) collective-permute-start(f32[32,128]{1,0:T(8,128)S(1)} %get-tuple-element.52), channel_id=1, source_target_pairs={{0,3},{1,2},{2,1},{3,0},{4,7},{5,6},{6,5},{7,4},{8,11},{9,10},{10,... | collective-permute-start | bytes 49160 | tf_op jit(solution)/shard_map/ppermute | solution.py:411
